TPU v7x, 32 devices: a whole 2x2x4 slice. The times are simulated.
32 devices in a mesh: gx: 4 (over z), gz: 4 (over y, core), sa: 2 (over x).
Axes of the slice: x: 2, y: 2, z: 4, core: 2. Of those that a mesh axis runs over, the one named last changes fastest.
Arguments:
- forcing: float32 [3, 8, 128, 32, 256], P(None, 'sa', 'gx', 'gz'), may hold values from -60 to 60
- velocity: float32 [256], replicated, may hold values from 0.3 to 1.2
- wall_solve: float32 [256, 256], replicated, may hold values from -1 to 1.7
Outputs:
- basis: float32 [3, 8, 128, 32, 256], P(None, 'sa', 'gx', 'gz')
- factor: float32 [8, 8], replicated
All inputs are finite; a program needn't handle non-finite values.
Results may differ from a plain program's by a relative error of at most 0.00015.
Values sent between devices are 32-bit elements; how exact they have to be, the bound alone decides.
No kernel may reach another device: no remote copies, remote signals or barrier semaphores. Data moves between devices by JAX's collectives and lax.ppermute only.
A program may use at most 64 MiB of HBM per device.

v0:
```python
import jax
import jax.numpy as jnp
from jax import lax
from jax.sharding import PartitionSpec as P

step_length = 0.4
viscosity = 0.2


def extended(cells, sides, width):
    for axis, dim in sides:
        count = lax.axis_size(axis)
        head = lax.slice_in_dim(cells, 0, width, axis=dim)
        tail = lax.slice_in_dim(cells, cells.shape[dim] - width, cells.shape[dim], axis=dim)
        cells = jnp.concatenate(
            [
                lax.ppermute(tail, axis, [(i, (i + 1) % count) for i in range(count)]),
                cells,
                lax.ppermute(head, axis, [((i + 1) % count, i) for i in range(count)]),
            ],
            axis=dim,
        )
    return cells


def shear_of(velocity):
    inner = (velocity[2:] - velocity[:-2]) * 0.5
    return jnp.concatenate([velocity[1:2] - velocity[0:1], inner, velocity[-1:] - velocity[-2:-1]])


def upper_factor(gram):
    order_size = gram.shape[0]
    column_ids = jnp.arange(order_size)
    row_list = []
    for pivot_index in range(order_size):
        current_row = gram[pivot_index]
        for other_index in range(pivot_index):
            current_row = current_row - row_list[other_index][pivot_index] * row_list[other_index]
        current_row = jnp.where(
            column_ids >= pivot_index, current_row, jnp.zeros_like(current_row)
        ) / jnp.sqrt(current_row[pivot_index])
        row_list.append(current_row)
    return jnp.stack(row_list)


def upper_inverse(factor):
    order_size = factor.shape[0]
    identity_rows = jnp.eye(order_size, dtype=factor.dtype)
    row_list = [None] * order_size
    for pivot_index in range(order_size - 1, -1, -1):
        current_row = identity_rows[pivot_index]
        for other_index in range(pivot_index + 1, order_size):
            current_row = current_row - factor[pivot_index, other_index] * row_list[other_index]
        row_list[pivot_index] = current_row / factor[pivot_index, pivot_index]
    return jnp.stack(row_list)


def stencil(padded, velocity, shear_rate, adjoint):
    center = padded[:, :, 1:-1, 1:-1]
    east_side = padded[:, :, 2:, 1:-1]
    west_side = padded[:, :, :-2, 1:-1]
    north_side = padded[:, :, 1:-1, 2:]
    south_side = padded[:, :, 1:-1, :-2]
    direction = 1.0 if adjoint else -1.0
    change = direction * velocity * (east_side - west_side) * 0.5 + viscosity * (
        east_side + west_side + north_side + south_side - 4.0 * center
    )
    if adjoint:
        change = change.at[1].add(-shear_rate * center[0])
    else:
        change = change.at[0].add(-shear_rate * center[1])
    return (center, change)


def wall_apply(field, wall_solve):
    return jnp.matmul(field, wall_solve, precision=lax.Precision.HIGHEST)


def wall_adjoint(field, wall_solve):
    return jnp.matmul(field, wall_solve.T, precision=lax.Precision.HIGHEST)


def near_faces(field):
    return extended(field, (("gx", 2), ("gz", 3)), 1)


def shards(forcing, velocity, wall_solve):
    shear_rate = shear_of(velocity)
    columns = forcing.shape[1]
    entries = (
        3
        * forcing.shape[2]
        * lax.axis_size("gx")
        * forcing.shape[3]
        * lax.axis_size("gz")
        * forcing.shape[4]
    )
    current = forcing
    for repeat in range(2):
        center, change = stencil(near_faces(current), velocity, shear_rate, False)
        current = wall_apply(center + step_length * (change + forcing), wall_solve)
    partial_value = jnp.sum(current * current, axis=(0, 2, 3, 4))
    response = current
    current = response
    for repeat in range(2):
        solved = wall_adjoint(current, wall_solve)
        center, change = stencil(near_faces(solved), velocity, shear_rate, True)
        current = center + step_length * change + step_length * response
    gathered = lax.all_gather(current, "sa", axis=1, tiled=True)
    half_rows = gathered.shape[4] // lax.axis_size("sa")
    row_block = lax.dynamic_slice_in_dim(gathered, lax.axis_index("sa") * half_rows, half_rows, 4)
    gram_local = jnp.einsum(
        "cixzy,cjxzy->ij", row_block, row_block, precision=lax.Precision.HIGHEST
    )
    slot_norms = jnp.zeros((columns * lax.axis_size("sa"),), jnp.float32)
    slot_norms = lax.dynamic_update_slice_in_dim(
        slot_norms, partial_value, lax.axis_index("sa") * columns, 0
    )
    raw_gram, totals = lax.psum((gram_local, slot_norms), ("gx", "gz", "sa"))
    scale_all = jnp.sqrt(totals / entries + 1e-06)
    gram = raw_gram / entries / (scale_all[:, None] * scale_all[None, :])
    factor = upper_factor(gram)
    inverse = upper_inverse(factor)
    coefficient = inverse / scale_all[:, None]
    own_coef = lax.dynamic_slice_in_dim(coefficient, lax.axis_index("sa") * columns, columns, 1)
    basis_own = jnp.einsum("cixzy,ij->cjxzy", gathered, own_coef, precision=lax.Precision.HIGHEST)
    return (basis_own, factor)


def solution(mesh):
    return jax.shard_map(
        shards,
        mesh=mesh,
        in_specs=(P(None, "sa", "gx", "gz", None), P(), P()),
        out_specs=(P(None, "sa", "gx", "gz", None), P()),
        check_vma=False,
    )
```

profile of v0, /device:TPU:0, one launch (start us, length us, event | category | flops | bytes accessed | tf_op | source)
XLA Modules:
  0.0 341.3 jit_solution(7292808118564609644)
XLA Ops:
  7.2 1.0 fusion.100
  8.2 3.1 collective-permute-start.1
  11.3 2.1 collective-permute-start
  13.4 0.8 subtract_multiply_fusion
  14.2 2.5 collective-permute-done.1
  16.8 2.3 constant_dynamic-update-slice_fusion.1
  20.8 1.4 maximum_negate_fusion
  22.2 6.5 %collective-permute-done.2 = f32[3,4,34,1,256]{4,3,2,1,0:T(1,128)S(1)} collective-permute-done((f32[3,4,34,1,256]{4,3,2,1,0:T(1,128)S(1)}, f32[3,4,34,1,256]{4,3,2,1,0:T(1,128)S(1)}, u32[]{:S(2)}, u32[]{:S(2)}) %collective-permute-start.2) | collective-permute-done | bytes 417824 | tf_op jit(solution)/shard_map/ppermute | solution.py:19
  28.7 3.0 collective-permute-done.3
  31.6 2.2 fusion.20
  34.2 2.8 fusion.32
  37.0 3.4 collective-permute-start.4
  40.4 3.2 collective-permute-done.4
  43.6 3.2 collective-permute-done.5
  47.9 9.3 %collective-permute-done.6 = f32[3,4,34,1,256]{4,3,2,1,0:T(1,128)S(1)} collective-permute-done((f32[3,4,34,1,256]{4,3,2,1,0:T(1,128)S(1)}, f32[3,4,34,1,256]{4,3,2,1,0:T(1,128)S(1)}, u32[]{:S(2)}, u32[]{:S(2)}) %collective-permute-start.6) | collective-permute-done | bytes 417824 | tf_op jit(solution)/shard_map/ppermute | solution.py:19
  57.3 1.2 collective-permute-done.7
  58.4 2.4 fusion.15
  61.1 2.9 fusion.28
  64.0 2.8 fusion.54
  66.9 0.6 collective-permute-start.8
  67.5 1.4 collective-permute-start.9
  69.0 3.6 %collective-permute-done.8 = f32[3,4,1,8,256]{4,3,2,1,0:T(8,128)S(1)} collective-permute-done((f32[3,4,1,8,256]{4,3,2,1,0:T(8,128)S(1)}, f32[3,4,1,8,256]{4,3,2,1,0:T(8,128)S(1)}, u32[]{:S(2)}, u32[]{:S(2)}) %collective-permute-start.8) | collective-permute-done | bytes 98336 | tf_op jit(solution)/shard_map/ppermute | solution.py:19
  72.6 1.4 collective-permute-done.9
  75.1 8.5 %collective-permute-done.10 = f32[3,4,34,1,256]{4,3,2,1,0:T(1,128)S(1)} collective-permute-done((f32[3,4,34,1,256]{4,3,2,1,0:T(1,128)S(1)}, f32[3,4,34,1,256]{4,3,2,1,0:T(1,128)S(1)}, u32[]{:S(2)}, u32[]{:S(2)}) %collective-permute-start.10) | collective-permute-done | bytes 417824 | tf_op jit(solution)/shard_map/ppermute | solution.py:19
  83.5 3.0 collective-permute-done.11
  86.5 2.4 fusion.10
  89.2 3.0 fusion.24
  92.2 0.9 collective-permute-start.12
  93.1 1.2 collective-permute-start.13
  94.2 2.8 collective-permute-done.12
  97.0 2.6 collective-permute-done.13
  100.8 9.1 %collective-permute-done.14 = f32[3,4,34,1,256]{4,3,2,1,0:T(1,128)S(1)} collective-permute-done((f32[3,4,34,1,256]{4,3,2,1,0:T(1,128)S(1)}, f32[3,4,34,1,256]{4,3,2,1,0:T(1,128)S(1)}, u32[]{:S(2)}, u32[]{:S(2)}) %collective-permute-start.14) | collective-permute-done | bytes 417824 | tf_op jit(solution)/shard_map/ppermute | solution.py:19
  109.9 2.4 collective-permute-done.15
  112.3 2.4 fusion.5
  115.0 2.5 multiply_reduce_fusion
  117.9 78.3 %all-gather.2.cloned.1.call-done = f32[3,8,32,8,256]{4,3,2,1,0:T(8,128)} async-done(((f32[3,4,32,8,256]{4,3,2,1,0:T(8,128)}), f32[3,8,32,8,256]{4,3,2,1,0:T(8,128)}) %all-gather.2.cloned.1.call-update) | async-done | bytes 6291472 | tf_op jit(solution)/shard_map/all_gather | solution.py:109
  196.1 2.1 constant_dynamic-slice_fusion
  198.2 7.5 %fusion.43 = f32[8,8]{1,0:T(8,128)S(1)} fusion(f32[3,8,32,8,128]{4,3,2,1,0:T(8,128)S(1)} %constant_dynamic-slice_fusion), kind=kOutput, calls=%fused_computation.71 | convolution fusion | flops 75497472 | bytes 3145984 | tf_op jit(solution)/shard_map/cixzy,cjxzy->ij/dot_general | solution.py:112
  205.7 39.6 %all-reduce = (f32[8,8]{1,0:T(8,128)S(1)}, f32[8]{0:T(128)S(1)}) all-reduce(f32[8,8]{1,0:T(8,128)S(1)} %fusion.43, f32[8]{0:T(128)S(1)} %dynamic_update_slice.3), channel_id=1, replica_groups=mesh['gx'=4,'gz'=4,'sa'=2] {'gx','gz','sa'}, use_global_device_ids=true, to_apply=%region_0.0 | all-reduce | flops 72 | bytes 576 | tf_op jit(solution)/shard_map/psum | solution.py:119
  246.6 0.7 fusion.112
  247.3 0.7 multiply_subtract_fusion.8
  248.0 0.6 slice.582
  249.3 0.7 fusion.107
  250.0 1.3 bitcast_subtract_fusion.5
  251.4 0.7 slice.588
  252.7 0.7 fusion.108
  253.4 1.7 fusion.86
  256.3 0.7 fusion.109
  257.0 2.5 fusion.85
  260.8 0.7 fusion.110
  261.5 3.1 fusion.83
  264.5 0.6 slice.612
  265.9 0.7 fusion.111
  266.5 3.8 %multiply_subtract_fusion.2 = f32[8]{0:T(128)S(1)} fusion(f32[]{:T(128)} %bitcast.40, f32[]{:T(128)} %bitcast.39, f32[]{:T(128)} %bitcast.38, f32[]{:T(128)} %bitcast.37, f32[]{:T(128)} %bitcast.36, f32[]{:T(128)} %bitcast.35, f32[8,8]{1,0:T(8,128)S(1)} %multiply_divide_fusion, f32[]{:T(128)} %bitcast.33, f32[8]{0:T(128)S(1)} %fusion.83, f32[]{:T(128)} %bitcast.25, ...), kind=kLoop, calls=%fused_computation.164 | loop fusion | flops 224 | bytes 304 | tf_op jit(solution)/shard_map/sub | solution.py:38
  270.3 0.7 slice.622
  271.7 0.6 slice.632
  272.3 4.6 %multiply_subtract_fusion = f32[8]{0:T(128)S(1)} fusion(f32[]{:T(128)} %bitcast.50, f32[]{:T(128)} %bitcast.49, f32[]{:T(128)} %bitcast.48, f32[]{:T(128)} %bitcast.47, f32[]{:T(128)} %bitcast.46, f32[]{:T(128)} %bitcast.45, f32[]{:T(128)} %bitcast.44, f32[8,8]{1,0:T(8,128)S(1)} %multiply_divide_fusion, f32[]{:T(128)} %bitcast.42, ...), kind=kLoop, calls=%fused_computation.161 | loop fusion | flops 264 | bytes 344 | tf_op jit(solution)/shard_map/sub | solution.py:38
  278.1 16.9 %fusion.73 = (f32[1,8]{1,0:T(1,128)S(1)}, f32[1,8]{1,0:T(1,128)S(1)}, f32[1,8]{1,0:T(1,128)S(1)}, f32[1,8]{1,0:T(1,128)S(1)}, f32[1,8]{1,0:T(1,128)S(1)}, /*index=5*/f32[1,8]{1,0:T(1,128)S(1)}, f32[1,8]{1,0:T(1,128)S(1)}) fusion(f32[]{:T(128)} %bitcast.52, f32[]{:T(128)} %bitcast.50, f32[]{:T(128)} %bitcast.49, f32[]{:T(128)} %bitcast.48, f32[]{:T(128)} %bitcast.47, ...), kind=kLoop, calls=%fused_computation.134 | loop fusion | flops 608 | bytes 620 | tf_op jit(solution)/shard_map/div | solution.py:39
  295.1 0.7 fusion.101
  295.7 0.7 fusion.103
  296.4 0.7 fusion.105
  298.3 22.7 %subtract_divide_fusion = (f32[1,8]{1,0:T(1,128)S(1)}, f32[1,8]{1,0:T(1,128)S(1)}, f32[1,8]{1,0:T(1,128)S(1)}, f32[1,8]{1,0:T(1,128)S(1)}, f32[1,8]{1,0:T(1,128)...) fusion(f32[8,8]{1,0:T(8,128)S(1)} %fusion.60, f32[]{:T(128)} %bitcast.75, f32[]{:T(128)} %bitcast.44, ...), kind=kLoop, calls=%fused_computation.154 | loop fusion | flops 512 | bytes 656 | tf_op jit(solution)/shard_map/div | solution.py:54
  321.1 11.2 %fusion.37 = f32[3,4,32,8,256]{4,1,3,2,0:T(4,128)S(1)} fusion(f32[3,8,32,8,256]{4,3,2,1,0:T(8,128)} %all-gather.2.cloned.1.call-done, f32[8,8]{1,0:T(8,128)S(1)} %broadcast_divide_fusion, s32[]{:T(128)S(6)} %select_n.71), kind=kOutput, calls=%fused_computation.67 | convolution fusion | flops 75497472 | bytes 9437444 | tf_op jit(solution)/shard_map/cixzy,ij->cjxzy/dot_general | solution.py:126
  332.3 2.2 copy.9
  (53 shorter events, 10.2 us)
Async XLA Ops:
  7.2 27.0 %copy-start = (f32[256,256]{1,0:T(8,128)S(1)}, f32[256,256]{1,0:T(8,128)}, u32[]{:S(2)}) copy-start(f32[256,256]{1,0:T(8,128)} %param.13) | copy-start | bytes 786436
  7.2 188.9 %all-gather.2.cloned.1.call-start = ((), (), s32[]{:S(2)}) async-start(), calls=%async_computation | async-start | bytes 9437184 | tf_op jit(solution)/shard_map/all_gather | solution.py:109
  8.2 8.6 %collective-permute-start.1 = (f32[3,4,1,8,256]{4,3,2,1,0:T(8,128)S(1)}, f32[3,4,1,8,256]{4,3,2,1,0:T(8,128)S(1)}, u32[]{:S(2)}, u32[]{:S(2)}) collective-permute-start(f32[3,4,1,8,256]{4,3,2,1,0:T(8,128)S(1)} %get-tuple-element.86), channel_id=1, source_target_pairs={{0,8},{8,16},{16,24},{24,0},{1,9},{9,17},{17,25},{25,1},{2,10},{10... | collective-permute-start | bytes 294920 | tf_op jit(solution)/shard_map/ppermute | solution.py:17
  11.3 7.8 %collective-permute-start = (f32[3,4,1,8,256]{4,3,2,1,0:T(8,128)S(1)}, f32[3,4,1,8,256]{4,3,2,1,0:T(8,128)S(1)}, u32[]{:S(2)}, u32[]{:S(2)}) collective-permute-start(f32[3,4,1,8,256]{4,3,2,1,0:T(8,128)S(1)} %get-tuple-element.85), channel_id=1, source_target_pairs={{8,0},{16,8},{24,16},{0,24},{9,1},{17,9},{25,17},{1,25},{10,2},{18... | collective-permute-start | bytes 294920 | tf_op jit(solution)/shard_map/ppermute | solution.py:19
  16.8 3.4 copy-start.2
  16.8 14.8 %copy-start.1 = (f32[3,4,32,8,256]{4,3,2,1,0:T(8,128)S(1)}, f32[3,4,32,8,256]{4,3,2,1,0:T(8,128)}, u32[]{:S(2)}) copy-start(f32[3,4,32,8,256]{4,3,2,1,0:T(8,128)} %param.11) | copy-start | bytes 9437188
  19.6 9.0 %collective-permute-start.2 = (f32[3,4,34,1,256]{4,3,2,1,0:T(1,128)S(1)}, f32[3,4,34,1,256]{4,3,2,1,0:T(1,128)S(1)}, u32[]{:S(2)}, u32[]{:S(2)}) collective-permute-start(f32[3,4,34,1,256]{4,3,2,1,0:T(1,128)S(1)} %get-tuple-element.75), channel_id=1, source_target_pairs={{2,0},{4,2},{6,4},{0,6},{3,1},{5,3},{7,5},{1,7},{10,8},{12,10},{14... | collective-permute-start | bytes 1253384 | tf_op jit(solution)/shard_map/ppermute | solution.py:19
  19.7 11.9 %collective-permute-start.3 = (f32[3,4,34,1,256]{4,3,2,1,0:T(1,128)S(1)}, f32[3,4,34,1,256]{4,3,2,1,0:T(1,128)S(1)}, u32[]{:S(2)}, u32[]{:S(2)}) collective-permute-start(f32[3,4,34,1,256]{4,3,2,1,0:T(1,128)S(1)} %get-tuple-element.76), channel_id=1, source_target_pairs={{0,2},{2,4},{4,6},{6,0},{1,3},{3,5},{5,7},{7,1},{8,10},{10,12},{12... | collective-permute-start | bytes 1253384 | tf_op jit(solution)/shard_map/ppermute | solution.py:17
  37.0 6.6 %collective-permute-start.4 = (f32[3,4,1,8,256]{4,3,2,1,0:T(8,128)S(1)}, f32[3,4,1,8,256]{4,3,2,1,0:T(8,128)S(1)}, u32[]{:S(2)}, u32[]{:S(2)}) collective-permute-start(f32[3,4,1,8,256]{4,3,2,1,0:T(8,128)S(1)} %get-tuple-element.84), channel_id=1, source_target_pairs={{8,0},{16,8},{24,16},{0,24},{9,1},{17,9},{25,17},{1,25},{10,2},{18... | collective-permute-start | bytes 294920 | tf_op jit(solution)/shard_map/ppermute | solution.py:19
  40.4 6.4 %collective-permute-start.5 = (f32[3,4,1,8,256]{4,3,2,1,0:T(8,128)S(1)}, f32[3,4,1,8,256]{4,3,2,1,0:T(8,128)S(1)}, u32[]{:S(2)}, u32[]{:S(2)}) collective-permute-start(f32[3,4,1,8,256]{4,3,2,1,0:T(8,128)S(1)} %get-tuple-element.83), channel_id=1, source_target_pairs={{0,8},{8,16},{16,24},{24,0},{1,9},{9,17},{17,25},{25,1},{2,10},{10... | collective-permute-start | bytes 294920 | tf_op jit(solution)/shard_map/ppermute | solution.py:17
  47.3 9.9 %collective-permute-start.6 = (f32[3,4,34,1,256]{4,3,2,1,0:T(1,128)S(1)}, f32[3,4,34,1,256]{4,3,2,1,0:T(1,128)S(1)}, u32[]{:S(2)}, u32[]{:S(2)}) collective-permute-start(f32[3,4,34,1,256]{4,3,2,1,0:T(1,128)S(1)} %get-tuple-element.73), channel_id=1, source_target_pairs={{2,0},{4,2},{6,4},{0,6},{3,1},{5,3},{7,5},{1,7},{10,8},{12,10},{14... | collective-permute-start | bytes 1253384 | tf_op jit(solution)/shard_map/ppermute | solution.py:19
  47.4 11.0 %collective-permute-start.7 = (f32[3,4,34,1,256]{4,3,2,1,0:T(1,128)S(1)}, f32[3,4,34,1,256]{4,3,2,1,0:T(1,128)S(1)}, u32[]{:S(2)}, u32[]{:S(2)}) collective-permute-start(f32[3,4,34,1,256]{4,3,2,1,0:T(1,128)S(1)} %get-tuple-element.74), channel_id=1, source_target_pairs={{0,2},{2,4},{4,6},{6,0},{1,3},{3,5},{5,7},{7,1},{8,10},{10,12},{12... | collective-permute-start | bytes 1253384 | tf_op jit(solution)/shard_map/ppermute | solution.py:17
  66.9 5.7 %collective-permute-start.8 = (f32[3,4,1,8,256]{4,3,2,1,0:T(8,128)S(1)}, f32[3,4,1,8,256]{4,3,2,1,0:T(8,128)S(1)}, u32[]{:S(2)}, u32[]{:S(2)}) collective-permute-start(f32[3,4,1,8,256]{4,3,2,1,0:T(8,128)S(1)} %get-tuple-element.82), channel_id=1, source_target_pairs={{8,0},{16,8},{24,16},{0,24},{9,1},{17,9},{25,17},{1,25},{10,2},{18... | collective-permute-start | bytes 294920 | tf_op jit(solution)/shard_map/ppermute | solution.py:19
  67.5 6.5 %collective-permute-start.9 = (f32[3,4,1,8,256]{4,3,2,1,0:T(8,128)S(1)}, f32[3,4,1,8,256]{4,3,2,1,0:T(8,128)S(1)}, u32[]{:S(2)}, u32[]{:S(2)}) collective-permute-start(f32[3,4,1,8,256]{4,3,2,1,0:T(8,128)S(1)} %get-tuple-element.81), channel_id=1, source_target_pairs={{0,8},{8,16},{16,24},{24,0},{1,9},{9,17},{17,25},{25,1},{2,10},{10... | collective-permute-start | bytes 294920 | tf_op jit(solution)/shard_map/ppermute | solution.py:17
  74.5 9.0 %collective-permute-start.10 = (f32[3,4,34,1,256]{4,3,2,1,0:T(1,128)S(1)}, f32[3,4,34,1,256]{4,3,2,1,0:T(1,128)S(1)}, u32[]{:S(2)}, u32[]{:S(2)}) collective-permute-start(f32[3,4,34,1,256]{4,3,2,1,0:T(1,128)S(1)} %get-tuple-element.71), channel_id=1, source_target_pairs={{2,0},{4,2},{6,4},{0,6},{3,1},{5,3},{7,5},{1,7},{10,8},{12,10},{14... | collective-permute-start | bytes 1253384 | tf_op jit(solution)/shard_map/ppermute | solution.py:19
  74.6 11.9 %collective-permute-start.11 = (f32[3,4,34,1,256]{4,3,2,1,0:T(1,128)S(1)}, f32[3,4,34,1,256]{4,3,2,1,0:T(1,128)S(1)}, u32[]{:S(2)}, u32[]{:S(2)}) collective-permute-start(f32[3,4,34,1,256]{4,3,2,1,0:T(1,128)S(1)} %get-tuple-element.72), channel_id=1, source_target_pairs={{0,2},{2,4},{4,6},{6,0},{1,3},{3,5},{5,7},{7,1},{8,10},{10,12},{12... | collective-permute-start | bytes 1253384 | tf_op jit(solution)/shard_map/ppermute | solution.py:17
  92.2 4.9 %collective-permute-start.12 = (f32[3,4,1,8,256]{4,3,2,1,0:T(8,128)S(1)}, f32[3,4,1,8,256]{4,3,2,1,0:T(8,128)S(1)}, u32[]{:S(2)}, u32[]{:S(2)}) collective-permute-start(f32[3,4,1,8,256]{4,3,2,1,0:T(8,128)S(1)} %get-tuple-element.80), channel_id=1, source_target_pairs={{8,0},{16,8},{24,16},{0,24},{9,1},{17,9},{25,17},{1,25},{10,2},{18... | collective-permute-start | bytes 294920 | tf_op jit(solution)/shard_map/ppermute | solution.py:19
  93.1 6.6 %collective-permute-start.13 = (f32[3,4,1,8,256]{4,3,2,1,0:T(8,128)S(1)}, f32[3,4,1,8,256]{4,3,2,1,0:T(8,128)S(1)}, u32[]{:S(2)}, u32[]{:S(2)}) collective-permute-start(f32[3,4,1,8,256]{4,3,2,1,0:T(8,128)S(1)} %get-tuple-element.79), channel_id=1, source_target_pairs={{0,8},{8,16},{16,24},{24,0},{1,9},{9,17},{17,25},{25,1},{2,10},{10... | collective-permute-start | bytes 294920 | tf_op jit(solution)/shard_map/ppermute | solution.py:17
  100.2 9.7 %collective-permute-start.14 = (f32[3,4,34,1,256]{4,3,2,1,0:T(1,128)S(1)}, f32[3,4,34,1,256]{4,3,2,1,0:T(1,128)S(1)}, u32[]{:S(2)}, u32[]{:S(2)}) collective-permute-start(f32[3,4,34,1,256]{4,3,2,1,0:T(1,128)S(1)} %get-tuple-element.69), channel_id=1, source_target_pairs={{2,0},{4,2},{6,4},{0,6},{3,1},{5,3},{7,5},{1,7},{10,8},{12,10},{14... | collective-permute-start | bytes 1253384 | tf_op jit(solution)/shard_map/ppermute | solution.py:19
  100.6 11.7 %collective-permute-start.15 = (f32[3,4,34,1,256]{4,3,2,1,0:T(1,128)S(1)}, f32[3,4,34,1,256]{4,3,2,1,0:T(1,128)S(1)}, u32[]{:S(2)}, u32[]{:S(2)}) collective-permute-start(f32[3,4,34,1,256]{4,3,2,1,0:T(1,128)S(1)} %get-tuple-element.70), channel_id=1, source_target_pairs={{0,2},{2,4},{4,6},{6,0},{1,3},{3,5},{5,7},{7,1},{8,10},{10,12},{12... | collective-permute-start | bytes 1253384 | tf_op jit(solution)/shard_map/ppermute | solution.py:17
Sparse Core Ops, SparseCore 0:
  117.7 78.3 all-gather.1
where the time goes:
time: 342 us; the launch traced here: 341 us
  waiting for transfers between devices  141 us (41%)
  other arithmetic  74.8 us (22%)
  blocking collectives  39.6 us (12%)
  matrix products  30.2 us (9%)
  local copies, waits for them, and re-layouts  21.2 us (6%)
  between operations  19.9 us (6%)
  starting transfers between devices  15 us (4%)
    all_gather x1, waiting for transfers between devices, shards(): gathered = lax.all_gather(current, 'sa', axis=1, tiled=True)  78.3 us
    ppermute x8, waiting for transfers between devices, extended(): lax.ppermute(head, axis, [((i + 1) % count, i) for i in range(count)])  43.1 us
    psum x1, blocking collectives, shards(): raw_gram, totals = lax.psum((gram_local, slot_norms), ('gx', 'gz', 'sa'))  39.6 us
    div x1, other arithmetic, upper_inverse(): row_list[pivot_index] = current_row / factor[pivot_index, pivot_index]  22.7 us
    ppermute x8, waiting for transfers between devices, extended(): lax.ppermute(tail, axis, [(i, (i + 1) % count) for i in range(count)])  19.3 us
    sub x7, other arithmetic, upper_factor(): current_row - row_list[other_index][pivot_index] * row_list[other_index]  17.6 us
    div x8, other arithmetic, upper_factor(): jnp.where(column_ids >= pivot_index, current_row, jnp.zeros_like(current_...  17 us
    dot_general x1, matrix products, shards(): jnp.einsum('cixzy,ij->cjxzy', gathered, own_coef, precision=lax.Precision...  11.2 us
  transfers between devices with their start and end apart: 17, of which 16 were waited for; matrix products, arithmetic and copies ran while one was open for 2% of the time, Pallas kernels for 0%

commit v1 on v0

v1 whole, which is shorter than its diff:
```python
import functools

import jax
import jax.numpy as jnp
from jax import lax
from jax.experimental import pallas as pl
from jax.experimental.pallas import tpu as pltpu
from jax.sharding import PartitionSpec as P

step_length = 0.4
viscosity = 0.2
VMEM_LIMIT = 56 * 1024 * 1024
X_CHUNK = 8


def shear_of(velocity):
    inner = (velocity[2:] - velocity[:-2]) * 0.5
    return jnp.concatenate([velocity[1:2] - velocity[0:1], inner, velocity[-1:] - velocity[-2:-1]])


def split_halves(value):
    high = value.astype(jnp.bfloat16)
    low = (value - high.astype(jnp.float32)).astype(jnp.bfloat16)
    return high, low


def wall_product(high, low, wall_ref):
    dot = functools.partial(jnp.dot, preferred_element_type=jnp.float32)
    return dot(low, wall_ref[0]) + dot(high, wall_ref[1]) + dot(high, wall_ref[0])


def stencil_chunk(cur, comp, x0, xlo, xhi, zlo, zhi, coef, adjoint):
    nx = cur.shape[2]
    x1 = x0 + X_CHUNK
    mid = cur[comp, 0, x0:x1]
    if x0 == 0:
        west = jnp.concatenate([xlo[comp, 0][None], cur[comp, 0, 0 : x1 - 1]], axis=0)
    else:
        west = cur[comp, 0, x0 - 1 : x1 - 1]
    if x1 == nx:
        east = jnp.concatenate([cur[comp, 0, x0 + 1 : x1], xhi[comp, 0][None]], axis=0)
    else:
        east = cur[comp, 0, x0 + 1 : x1 + 1]
    nz = mid.shape[1]
    rows = lax.broadcasted_iota(jnp.int32, mid.shape, 1)
    low_face = jnp.broadcast_to(zlo[comp, 0, x0:x1][:, None, :], mid.shape)
    high_face = jnp.broadcast_to(zhi[comp, 0, x0:x1][:, None, :], mid.shape)
    south = jnp.where(rows == 0, low_face, pltpu.roll(mid, 1, 1))
    north = jnp.where(rows == nz - 1, high_face, pltpu.roll(mid, nz - 1, 1))
    side = viscosity * step_length
    plus, minus = coef[0][None], coef[1][None]
    if adjoint:
        plus, minus = minus, plus
    value = (1.0 - 4.0 * side) * mid + plus * east + minus * west + side * (north + south)
    if adjoint and comp == 1:
        value = value - coef[2][None] * cur[0, 0, x0:x1]
    if not adjoint and comp == 0:
        value = value - coef[2][None] * cur[1, 0, x0:x1]
    return value


def put_faces(result, comp, first_x, last_x, first_z, last_z):
    nx, nz = result.shape[0], result.shape[1]
    first_x[comp, 0] = result[0]
    last_x[comp, 0] = result[nx - 1]
    first_z[comp, 0] = result[:, 0, :]
    last_z[comp, 0] = result[:, nz - 1, :]


def stage_body(kind, *refs):
    if kind == "adjoint_last":
        half_ref, *refs = refs
    cur, src, xlo, xhi, zlo, zhi, coef, wall, *rest = refs
    nx, nz, ny = cur.shape[2:]
    if kind == "forward_first":
        out, fx, lx, fz, lz, high, low = rest
    elif kind == "forward_last":
        out, solved, squares, fx, lx, fz, lz, high, low = rest
    elif kind == "adjoint_first":
        out, fx, lx, fz, lz, high, low = rest
    else:
        keep, send = rest
    adjoint = kind.startswith("adjoint")
    for comp in range(3):
        for x0 in range(0, nx, X_CHUNK):
            value = stencil_chunk(cur, comp, x0, xlo, xhi, zlo, zhi, coef, adjoint)
            value = value + step_length * src[comp, 0, x0 : x0 + X_CHUNK]
            if kind == "adjoint_last":
                half_x = nx // 2
                own = half_ref[0] == (1 if x0 >= half_x else 0)
                spot = x0 % half_x

                @pl.when(own)
                def _():
                    keep[comp, 0, spot : spot + X_CHUNK] = value

                @pl.when(jnp.logical_not(own))
                def _():
                    send[comp, 0, spot : spot + X_CHUNK] = value
            else:
                h, l = split_halves(value.reshape(X_CHUNK * nz, ny))
                spot = (comp * nx + x0) * nz
                high[spot : spot + X_CHUNK * nz] = h
                low[spot : spot + X_CHUNK * nz] = l
    if kind == "adjoint_last":
        return
    size = nx * nz
    total = None
    for comp in range(3):
        part = slice(comp * size, (comp + 1) * size)
        result = wall_product(high[part], low[part], wall.at[pl.ds(2, 2)] if adjoint else wall)
        tile = result.reshape(nx, nz, ny)
        out[comp, 0] = tile
        if kind == "forward_last":
            sums = jnp.sum(tile * tile, axis=0)
            total = sums if total is None else total + sums
            h, l = split_halves(result)
            result = wall_product(h, l, wall.at[pl.ds(2, 2)])
            tile = result.reshape(nx, nz, ny)
            solved[comp, 0] = tile
        put_faces(tile, comp, fx, lx, fz, lz)
    if kind == "forward_last":
        squares[0] = total


def run_stage(kind, cur, src, faces, coef, wall, half=None):
    three, columns, nx, nz, ny = cur.shape
    xlo, xhi, zlo, zhi = faces
    whole = pl.BlockSpec((three, 1, nx, nz, ny), lambda j, *_: (0, j, 0, 0, 0))
    half_spec = pl.BlockSpec((three, 1, nx // 2, nz, ny), lambda j, *_: (0, j, 0, 0, 0))
    x_face = pl.BlockSpec((three, 1, nz, ny), lambda j, *_: (0, j, 0, 0))
    z_face = pl.BlockSpec((three, 1, nx, ny), lambda j, *_: (0, j, 0, 0))
    fixed3 = pl.BlockSpec((3, nz, ny), lambda j, *_: (0, 0, 0))
    fixed4 = pl.BlockSpec((4, ny, ny), lambda j, *_: (0, 0, 0))
    square_spec = pl.BlockSpec((1, nz, ny), lambda j, *_: (j, 0, 0))
    f32 = jnp.float32
    field = jax.ShapeDtypeStruct(cur.shape, f32)
    half_field = jax.ShapeDtypeStruct((three, columns, nx // 2, nz, ny), f32)
    x_out = jax.ShapeDtypeStruct((three, columns, nz, ny), f32)
    z_out = jax.ShapeDtypeStruct((three, columns, nx, ny), f32)
    face_outs, face_specs = [x_out, x_out, z_out, z_out], [x_face, x_face, z_face, z_face]
    scratch = [pltpu.VMEM((three * nx * nz, ny), jnp.bfloat16)] * 2
    if kind == "forward_last":
        outs = [field, field, jax.ShapeDtypeStruct((columns, nz, ny), f32)] + face_outs
        specs = [whole, whole, square_spec] + face_specs
    elif kind == "adjoint_last":
        outs, specs, scratch = [half_field, half_field], [half_spec, half_spec], []
    else:
        outs, specs = [field] + face_outs, [whole] + face_specs
    in_specs = [whole, whole, x_face, x_face, z_face, z_face, fixed3, fixed4]
    operands = [cur, src, xlo, xhi, zlo, zhi, coef, wall]
    prefetch = 0
    if kind == "adjoint_last":
        prefetch, operands = 1, [half] + operands
    return pl.pallas_call(
        functools.partial(stage_body, kind),
        out_shape=outs,
        grid_spec=pltpu.PrefetchScalarGridSpec(
            num_scalar_prefetch=prefetch,
            grid=(columns,),
            in_specs=in_specs,
            out_specs=specs,
            scratch_shapes=scratch,
        ),
        compiler_params=pltpu.CompilerParams(vmem_limit_bytes=VMEM_LIMIT),
        name=kind,
    )(*operands)


def gram_body(half_ref, own, other, squares, out, acc, sums):
    step = pl.program_id(0)
    columns = own.shape[1]
    count = 2 * columns
    pairs = [(i, j) for i in range(count) for j in range(i, count)]

    @pl.when(step == 0)
    def _():
        acc[...] = jnp.zeros_like(acc)

    three, _, nx, nz, ny = own.shape
    for lane in range(0, ny, 128):

        def body(k, carry):
            comp = k // nx
            x = k - comp * nx
            cols = [own[comp, i, x, :, lane : lane + 128] for i in range(columns)]
            cols += [other[comp, i, x, :, lane : lane + 128] for i in range(columns)]
            return tuple(c + cols[i] * cols[j] for c, (i, j) in zip(carry, pairs))

        start = tuple(acc[p] for p in range(len(pairs)))
        done = lax.fori_loop(0, three * nx, body, start)
        for p in range(len(pairs)):
            acc[p] = done[p]

    @pl.when(step == pl.num_programs(0) - 1)
    def _():
        for p in range(len(pairs)):
            sums[p : p + 1] = jnp.sum(acc[p], axis=0, keepdims=True)
        spot = {}
        for p, (i, j) in enumerate(pairs):
            spot[i, j] = spot[j, i] = p
        lanes = lax.broadcasted_iota(jnp.int32, (count, 128), 1)
        rows = lax.broadcasted_iota(jnp.int32, (count, 128), 0)
        plain = jnp.zeros((count, 128), jnp.float32)
        moved = jnp.zeros((count, 128), jnp.float32)
        for i in range(count):
            stack = jnp.concatenate([sums[spot[i, j] : spot[i, j] + 1] for j in range(count)], axis=0)
            column = jnp.sum(stack, axis=1, keepdims=True)
            plain = jnp.where(lanes == i, column, plain)
            moved = jnp.where(lanes == (i + columns) % count, column, moved)
        norm_rows = [
            jnp.sum(squares[i, :, 0:128] + squares[i, :, 128:256], axis=0, keepdims=True) for i in range(columns)
        ]
        norm = jnp.sum(jnp.concatenate(norm_rows * 2, axis=0), axis=1, keepdims=True)
        plain = jnp.where(lanes == count, jnp.where(rows < columns, norm, 0.0), plain)
        moved = jnp.where(lanes == count, jnp.where(rows < columns, norm, 0.0), moved)
        moved = pltpu.roll(moved, columns, 0)
        out[...] = jnp.where(half_ref[0] == 0, plain, moved)


def run_gram(half, own, other, squares):
    three, columns, nx, nz, ny = own.shape
    steps = 4
    count = 2 * columns
    npairs = count * (count + 1) // 2
    block = pl.BlockSpec((three, columns, nx // steps, nz, ny), lambda k, *_: (0, 0, k, 0, 0))
    return pl.pallas_call(
        gram_body,
        out_shape=jax.ShapeDtypeStruct((count, 128), jnp.float32),
        grid_spec=pltpu.PrefetchScalarGridSpec(
            num_scalar_prefetch=1,
            grid=(steps,),
            in_specs=[block, block, pl.BlockSpec(squares.shape, lambda k, *_: (0, 0, 0))],
            out_specs=pl.BlockSpec((count, 128), lambda k, *_: (0, 0)),
            scratch_shapes=[pltpu.VMEM((npairs, nz, 128), jnp.float32), pltpu.VMEM((npairs, 128), jnp.float32)],
        ),
        compiler_params=pltpu.CompilerParams(vmem_limit_bytes=VMEM_LIMIT),
        name="gram",
    )(half, own, other, squares)


def basis_body(entries, half_ref, raw, own_keep, other_keep, own_send, other_send, out, factor, coef):
    step = pl.program_id(0)
    columns = own_keep.shape[1]
    count = 2 * columns
    steps = pl.num_programs(0)

    @pl.when(step == 0)
    def _():
        total = raw[...]
        lanes = lax.broadcasted_iota(jnp.int32, (count, 128), 1)
        rows = lax.broadcasted_iota(jnp.int32, (count, 128), 0)
        scale = jnp.sqrt(total[:, count : count + 1] / entries + 1e-06)
        inverse_scale = 1.0 / scale
        scale_row = jnp.sum(jnp.where(lanes == rows, jnp.broadcast_to(scale, (count, 128)), 0.0), axis=0, keepdims=True)
        scale_row = jnp.where(lanes < count, jnp.broadcast_to(scale_row, (count, 128)), 1.0)
        gram = total / entries / (jnp.broadcast_to(scale, (count, 128)) * scale_row)
        work = jnp.where(lanes < count, gram, jnp.where(lanes == rows + count, 1.0, 0.0))
        for k in range(count):
            pivot = work[k : k + 1]
            root = jnp.sqrt(pivot[:, k : k + 1])
            line = pivot / root
            ratio = jnp.where(rows[:, 0:1] > k, work[:, k : k + 1], 0.0) / root
            work = jnp.where(rows == k, jnp.broadcast_to(line, (count, 128)), work - ratio * line)
        factor[...] = jnp.where(lanes >= rows, work, 0.0)[:, :count]
        first = half_ref[0] == 0
        for j in range(columns):
            row = jnp.where(first, work[j : j + 1], work[columns + j : columns + j + 1])
            for i in range(count):
                lo = (i + columns) % count
                pick = jnp.where(first, row[:, count + i : count + i + 1], row[:, count + lo : count + lo + 1])
                norm = jnp.where(first, inverse_scale[i : i + 1], inverse_scale[lo : lo + 1])
                coef[j * count + i] = jnp.broadcast_to(pick * norm, coef.shape[1:])

    three, _, nx, nz, ny = own_keep.shape
    keep_step = (step // (steps // 2)) == half_ref[0]

    def combine(own, other):
        for comp in range(three):

            def body(x, _):
                cols = [own[comp, i, x] for i in range(columns)] + [other[comp, i, x] for i in range(columns)]
                for j in range(columns):
                    value = coef[j * count] * cols[0]
                    for i in range(1, count):
                        value = value + coef[j * count + i] * cols[i]
                    out[comp, j, x] = value
                return 0

            lax.fori_loop(0, nx, body, 0)

    @pl.when(keep_step)
    def _():
        combine(own_keep, other_keep)

    @pl.when(jnp.logical_not(keep_step))
    def _():
        combine(own_send, other_send)


def run_basis(entries, half, raw, own_keep, other_keep, own_send, other_send):
    three, columns, half_x, nz, ny = own_keep.shape
    per = 2
    count = 2 * columns
    block = (three, columns, half_x // per, nz, ny)

    def keep_map(k, h):
        inside = k // per == h[0]
        return (0, 0, jnp.where(inside, k % per, jnp.where(h[0] == 0, per - 1, 0)), 0, 0)

    def send_map(k, h):
        inside = k // per != h[0]
        return (0, 0, jnp.where(inside, k % per, jnp.where(h[0] == 0, 0, per - 1)), 0, 0)

    keep_spec, send_spec = pl.BlockSpec(block, keep_map), pl.BlockSpec(block, send_map)
    return pl.pallas_call(
        functools.partial(basis_body, entries),
        out_shape=[
            jax.ShapeDtypeStruct((three, columns, 2 * half_x, nz, ny), jnp.float32),
            jax.ShapeDtypeStruct((count, count), jnp.float32),
        ],
        grid_spec=pltpu.PrefetchScalarGridSpec(
            num_scalar_prefetch=1,
            grid=(2 * per,),
            in_specs=[
                pl.BlockSpec((count, 128), lambda k, *_: (0, 0)),
                keep_spec,
                keep_spec,
                send_spec,
                send_spec,
            ],
            out_specs=[
                pl.BlockSpec(block, lambda k, *_: (0, 0, k, 0, 0)),
                pl.BlockSpec((count, count), lambda k, *_: (0, 0)),
            ],
            scratch_shapes=[pltpu.VMEM((columns * count, nz, ny), jnp.float32)],
        ),
        compiler_params=pltpu.CompilerParams(vmem_limit_bytes=VMEM_LIMIT),
        name="basis",
    )(half, raw, own_keep, other_keep, own_send, other_send)


def shift(value, axis, amount):
    count = lax.axis_size(axis)
    return lax.ppermute(value, axis, [(i, (i + amount) % count) for i in range(count)])


def exchange(first_x, last_x, first_z, last_z):
    zlo = shift(last_z, "gz", 1)
    zhi = shift(first_z, "gz", -1)
    xlo = shift(last_x, "gx", 1)
    xhi = shift(first_x, "gx", -1)
    return xlo, xhi, zlo, zhi


def all_sum(value, axes):
    for axis in axes:
        count = lax.axis_size(axis)
        if count & (count - 1):
            value = lax.psum(value, axis)
            continue
        mask = 1
        while mask < count:
            value = value + lax.ppermute(value, axis, [(i, i ^ mask) for i in range(count)])
            mask *= 2
    return value


def shards(forcing, velocity, wall_solve):
    columns, nx, nz, ny = forcing.shape[1:]
    entries = float(3 * nx * lax.axis_size("gx") * nz * lax.axis_size("gz") * ny)
    faces = exchange(forcing[:, :, 0], forcing[:, :, nx - 1], forcing[:, :, :, 0], forcing[:, :, :, nz - 1])
    shear_rate = shear_of(velocity)
    side = step_length * viscosity
    coef = jnp.stack([side - 0.5 * step_length * velocity, side + 0.5 * step_length * velocity, step_length * shear_rate])
    coef = jnp.broadcast_to(coef[:, None, :], (3, nz, ny))
    wall_high = lax.reduce_precision(wall_solve, 8, 7)
    wall_low = wall_solve - wall_high
    wall = jnp.stack([wall_high, wall_low, wall_high.T, wall_low.T]).astype(jnp.bfloat16)
    half = lax.axis_index("sa").astype(jnp.int32).reshape(1)

    q1, *edge = run_stage("forward_first", forcing, forcing, faces, coef, wall)
    q2, s1, squares, *edge = run_stage("forward_last", q1, forcing, exchange(*edge), coef, wall)
    s2, *edge = run_stage("adjoint_first", s1, q2, exchange(*edge), coef, wall)
    keep, send = run_stage("adjoint_last", s2, q2, exchange(*edge), coef, wall, half)
    other_keep = lax.ppermute(send, "sa", [(0, 1), (1, 0)])
    other_send = lax.ppermute(keep, "sa", [(0, 1)])
    raw = run_gram(half, keep, other_keep, squares)
    raw = all_sum(raw, ("gx", "gz", "sa"))
    basis, factor = run_basis(entries, half, raw, keep, other_keep, send, other_send)
    return basis, factor


def solution(mesh):
    return jax.shard_map(
        shards,
        mesh=mesh,
        in_specs=(P(None, "sa", "gx", "gz", None), P(), P()),
        out_specs=(P(None, "sa", "gx", "gz", None), P()),
        check_vma=False,
    )
```

time: 342 us -> 162 us (0.47)
  other arithmetic: 74.8 us -> 2.37 us
  waiting for transfers between devices: 141 us -> 68.8 us
  Pallas kernels: 0 us -> 42.1 us
  blocking collectives: 39.6 us -> 0 us
  matrix products: 30.2 us -> 0 us
  starting transfers between devices: 15 us -> 34 us
  between operations: 19.9 us -> 3.41 us
  local copies, waits for them, and re-layouts: 21.2 us -> 11.1 us
    all_gather x1 -> x0, waiting for transfers between devices: 78.3 us -> none  [shards(): gathered = lax.all_gather(current, 'sa', axis=1, tiled=True)]
    pallas_call x0 -> x6, Pallas kernels: none -> 42.1 us  [the longest x4 29.4 us: run_stage(): pl.pallas_call(functools.partial(stage_body, kind), out_shape=outs, grid_...]
    div x11 -> x0, other arithmetic: 39.8 us -> none  [the longest x1 22.7 us: upper_inverse(): row_list[pivot_index] = current_row / factor[pivot_index, pivot_index]]
    psum x1 -> x0, blocking collectives: 39.6 us -> none  [shards(): raw_gram, totals = lax.psum((gram_local, slot_norms), ('gx', 'gz', 'sa'))]
    dot_general x6 -> x0, matrix products: 30.2 us -> none  [the longest x1 11.2 us: shards(): jnp.einsum('cixzy,ij->cjxzy', gathered, own_coef, precision=lax.Precision...]
    ppermute x16 -> x23, starting transfers between devices: 15 us -> 34 us  [the longest x16 24.1 us: shift(): lax.ppermute(value, axis, [(i, (i + amount) % count) for i in range(count)])]
    sub x8 -> x1, other arithmetic: 18.2 us -> 0.01 us  [shards(): side - 0.5 * step_length * velocity]
    slice x24 -> x2, local copies, waits for them, and re-layouts: 13.7 us -> 4.12 us  [the longest x1 3.48 us: shards(): forcing[:, :, :, 0]]
  transfers between devices with their start and end apart: 17 -> 23, of which waited for: 16 -> 14; matrix products, arithmetic and copies ran while one was open for 2% -> 3% of each run, Pallas kernels for 0% -> 3%
where the time goes in v1:
time: 162 us
  waiting for transfers between devices  68.8 us (42%)
  Pallas kernels  42.1 us (26%)
  starting transfers between devices  34 us (21%)
  local copies, waits for them, and re-layouts  11.1 us (7%)
  between operations  3.41 us (2%)
  other arithmetic  2.37 us (1%)
    ppermute x1, waiting for transfers between devices, shards(): other_keep = lax.ppermute(send, 'sa', [(0, 1), (1, 0)])  32.8 us
    pallas_call x4, Pallas kernels, run_stage(): pl.pallas_call(functools.partial(stage_body, kind), out_shape=outs, grid_...  29.4 us
    ppermute x16, starting transfers between devices, shift(): lax.ppermute(value, axis, [(i, (i + amount) % count) for i in range(count)])  24.1 us
    ppermute x5, waiting for transfers between devices, all_sum(): lax.ppermute(value, axis, [(i, i ^ mask) for i in range(count)])  19.8 us
    ppermute x16, waiting for transfers between devices, shift(): lax.ppermute(value, axis, [(i, (i + amount) % count) for i in range(count)])  16.2 us
    pallas_call x1, Pallas kernels, run_basis(): pl.pallas_call(functools.partial(basis_body, entries), out_shape=[jax.Sha...  7.55 us
    ppermute x5, starting transfers between devices, all_sum(): lax.ppermute(value, axis, [(i, i ^ mask) for i in range(count)])  5.89 us
    pallas_call x1, Pallas kernels, run_gram(): pl.pallas_call(gram_body, out_shape=jax.ShapeDtypeStruct((count, 128), jn...  5.15 us
  transfers between devices with their start and end apart: 23, of which 14 were waited for; matrix products, arithmetic and copies ran while one was open for 3% of the time, Pallas kernels for 3%

profile of v1, /device:TPU:0, one launch (start us, length us, event | category | flops | bytes accessed | tf_op | source)
XLA Modules:
  0.0 161.8 jit_solution(9276127564742678135)
XLA Ops:
  0.6 3.5 %fusion.5 = (f32[3,4,32,1,256]{4,3,2,1,0:T(1,128)S(1)}, f32[3,4,32,1,256]{4,3,2,1,0:T(1,128)S(1)}) fusion(f32[3,4,32,8,256]{4,3,2,1,0:T(8,128)} %refs_1_.3), kind=kLoop, calls=%fused_computation.17 | loop fusion | bytes 1572864 | tf_op jit(solution)/shard_map/slice | solution.py:372
  4.2 0.5 collective-permute-start.2
  4.7 2.0 %collective-permute-start.3 = (f32[3,4,32,256]{3,2,1,0:T(8,128)S(1)}, f32[3,4,32,256]{3,2,1,0:T(8,128)S(1)}, u32[]{:S(2)}, u32[]{:S(2)}) collective-permute-start(f32[3,4,32,256]{3,2,1,0:T(8,128)S(1)} %bitcast.33), channel_id=1, source_target_pairs={{0,6},{2,0},{4,2},{6,4},{1,7},{3,1},{5,3},{7,5},{8,14},{10,8},{12,... | collective-permute-start | bytes 1179656 | tf_op jit(solution)/shard_map/ppermute | solution.py:345
  6.8 1.0 slice_bitcast_fusion
  7.7 2.4 %collective-permute-start = (f32[3,4,8,256]{3,2,1,0:T(8,128)S(1)}, f32[3,4,8,256]{3,2,1,0:T(8,128)S(1)}, u32[]{:S(2)}, u32[]{:S(2)}) collective-permute-start(f32[3,4,8,256]{3,2,1,0:T(8,128)S(1)} %get-tuple-element.43), channel_id=1, source_target_pairs={{0,8},{8,16},{16,24},{24,0},{1,9},{9,17},{17,25},{25,1},{2,10},{10... | collective-permute-start | bytes 294920 | tf_op jit(solution)/shard_map/ppermute | solution.py:345
  10.1 2.1 %collective-permute-start.1 = (f32[3,4,8,256]{3,2,1,0:T(8,128)S(1)}, f32[3,4,8,256]{3,2,1,0:T(8,128)S(1)}, u32[]{:S(2)}, u32[]{:S(2)}) collective-permute-start(f32[3,4,8,256]{3,2,1,0:T(8,128)S(1)} %get-tuple-element.42), channel_id=1, source_target_pairs={{0,24},{8,0},{16,8},{24,16},{1,25},{9,1},{17,9},{25,17},{2,26},{10... | collective-permute-start | bytes 294920 | tf_op jit(solution)/shard_map/ppermute | solution.py:345
  12.2 0.6 fusion.6
  12.8 0.1 subtract_multiply_fusion
  12.9 0.1 copy.9
  13.1 0.1 copy.11
  13.2 0.1 copy.12
  15.9 0.9 pad_maximum_fusion.refs_7_.refs_8_
  16.7 0.1 maximum_multiply_fusion
  16.8 0.0 collective-permute-done.refs_2_
  16.9 0.0 collective-permute-done.1.refs_3_
  16.9 0.7 broadcast_in_dim.2.refs_6_.refs_7_
  17.6 0.1 copy-done.2
  17.7 0.2 copy-done.3
  17.9 7.1 %forward_first.1 = (f32[3,4,32,8,256]{4,3,2,1,0:T(8,128)}, f32[3,4,8,256]{3,2,1,0:T(8,128)}, f32[3,4,8,256]{3,2,1,0:T(8,128)}, f32[3,4,32,256]{3,2,1,0:T(8,128)}, f32[3,4,32,256]{3,2,1,0:T(8,128)}) custom-call(f32[3,4,32,8,256]{4,3,2,1,0:T(8,128)} %refs_1_.3, f32[3,4,32,8,256]{4,3,2,1,0:T(8,128)} %refs_1_.3, f32[3,4,8,256]{3,2,1,0:T(8,128)} %copy-done.11, ...), custom_call_target="tpu_custom_call" | custom-call | tf_op jit(solution)/shard_map/forward_first/pallas_call | solution.py:155
  25.0 0.1 collective-permute-start.6
  25.0 1.7 %collective-permute-start.7 = (f32[3,4,32,256]{3,2,1,0:T(8,128)}, f32[3,4,32,256]{3,2,1,0:T(8,128)S(1)}, u32[]{:S(2)}, u32[]{:S(2)}) collective-permute-start(f32[3,4,32,256]{3,2,1,0:T(8,128)} %get-tuple-element.25), channel_id=1, source_target_pairs={{0,6},{2,0},{4,2},{6,4},{1,7},{3,1},{5,3},{7,5},{8,14},{10,8},{12,... | collective-permute-start | bytes 1179656 | tf_op jit(solution)/shard_map/ppermute | solution.py:345
  26.8 0.9 collective-permute-start.4
  27.6 3.0 %collective-permute-start.5 = (f32[3,4,8,256]{3,2,1,0:T(8,128)}, f32[3,4,8,256]{3,2,1,0:T(8,128)S(1)}, u32[]{:S(2)}, u32[]{:S(2)}) collective-permute-start(f32[3,4,8,256]{3,2,1,0:T(8,128)} %get-tuple-element.23), channel_id=1, source_target_pairs={{0,24},{8,0},{16,8},{24,16},{1,25},{9,1},{17,9},{25,17},{2,26},{10... | collective-permute-start | bytes 294920 | tf_op jit(solution)/shard_map/ppermute | solution.py:345
  30.6 3.9 %collective-permute-done.4.refs_2_ = f32[3,4,8,256]{3,2,1,0:T(8,128)S(1)} collective-permute-done((f32[3,4,8,256]{3,2,1,0:T(8,128)}, f32[3,4,8,256]{3,2,1,0:T(8,128)S(1)}, u32[]{:S(2)}, u32[]{:S(2)}) %collective-permute-start.4) | collective-permute-done | bytes 98336 | tf_op jit(solution)/shard_map/ppermute | solution.py:345
  34.5 0.1 collective-permute-done.5.refs_3_
  34.6 0.1 collective-permute-done.6.refs_4_
  34.7 1.3 collective-permute-done.7.refs_5_
  36.0 0.8 copy-done.7
  36.7 8.8 %forward_last.1 = (f32[3,4,32,8,256]{4,3,2,1,0:T(8,128)}, f32[3,4,32,8,256]{4,3,2,1,0:T(8,128)}, f32[4,8,256]{2,1,0:T(8,128)}, f32[3,4,8,256]{3,2,1,0:T(8,128)},...) custom-call(f32[3,4,32,8,256]{4,3,2,1,0:T(8,128)} %get-tuple-element.21.refs_0_, ...), custom_call_target="tpu_custom_call" | custom-call | tf_op jit(solution)/shard_map/forward_last/pallas_call | solution.py:155
  45.5 0.6 collective-permute-start.10
  46.1 1.3 collective-permute-start.11
  47.4 0.7 collective-permute-start.8
  48.2 3.1 %collective-permute-start.9 = (f32[3,4,8,256]{3,2,1,0:T(8,128)}, f32[3,4,8,256]{3,2,1,0:T(8,128)S(1)}, u32[]{:S(2)}, u32[]{:S(2)}) collective-permute-start(f32[3,4,8,256]{3,2,1,0:T(8,128)} %get-tuple-element.29), channel_id=1, source_target_pairs={{0,24},{8,0},{16,8},{24,16},{1,25},{9,1},{17,9},{25,17},{2,26},{10... | collective-permute-start | bytes 294920 | tf_op jit(solution)/shard_map/ppermute | solution.py:345
  51.3 3.9 %collective-permute-done.8.refs_2_ = f32[3,4,8,256]{3,2,1,0:T(8,128)S(1)} collective-permute-done((f32[3,4,8,256]{3,2,1,0:T(8,128)}, f32[3,4,8,256]{3,2,1,0:T(8,128)S(1)}, u32[]{:S(2)}, u32[]{:S(2)}) %collective-permute-start.8) | collective-permute-done | bytes 98336 | tf_op jit(solution)/shard_map/ppermute | solution.py:345
  55.2 0.0 collective-permute-done.9.refs_3_
  55.2 1.5 collective-permute-done.11.refs_5_
  56.7 0.8 copy-done.9
  57.5 7.1 %adjoint_first.1 = (f32[3,4,32,8,256]{4,3,2,1,0:T(8,128)}, f32[3,4,8,256]{3,2,1,0:T(8,128)}, f32[3,4,8,256]{3,2,1,0:T(8,128)}, f32[3,4,32,256]{3,2,1,0:T(8,128)}, f32[3,4,32,256]{3,2,1,0:T(8,128)}) custom-call(f32[3,4,32,8,256]{4,3,2,1,0:T(8,128)} %get-tuple-element.26.refs_0_, f32[3,4,32,8,256]{4,3,2,1,0:T(8,128)} %get-tuple-element.27.refs_1_.refs_2_, ...), custom_call_target="tpu_custom_call" | custom-call | tf_op jit(solution)/shard_map/adjoint_first/pallas_call | solution.py:155
  64.6 0.4 collective-permute-start.14
  65.1 1.5 collective-permute-start.15
  66.5 0.6 collective-permute-start.12
  67.2 3.2 %collective-permute-start.13 = (f32[3,4,8,256]{3,2,1,0:T(8,128)}, f32[3,4,8,256]{3,2,1,0:T(8,128)S(1)}, u32[]{:S(2)}, u32[]{:S(2)}) collective-permute-start(f32[3,4,8,256]{3,2,1,0:T(8,128)} %get-tuple-element.34), channel_id=1, source_target_pairs={{0,24},{8,0},{16,8},{24,16},{1,25},{9,1},{17,9},{25,17},{2,26},{10... | collective-permute-start | bytes 294920 | tf_op jit(solution)/shard_map/ppermute | solution.py:345
  70.4 3.9 %collective-permute-done.12.refs_3_ = f32[3,4,8,256]{3,2,1,0:T(8,128)S(1)} collective-permute-done((f32[3,4,8,256]{3,2,1,0:T(8,128)}, f32[3,4,8,256]{3,2,1,0:T(8,128)S(1)}, u32[]{:S(2)}, u32[]{:S(2)}) %collective-permute-start.12) | collective-permute-done | bytes 98336 | tf_op jit(solution)/shard_map/ppermute | solution.py:345
  74.3 1.6 collective-permute-done.15.refs_6_
  75.8 0.7 copy-done.5
  76.6 6.4 %adjoint_last.1 = (f32[3,4,16,8,256]{4,3,2,1,0:T(8,128)}, f32[3,4,16,8,256]{4,3,2,1,0:T(8,128)}) custom-call(s32[1]{0:T(128)} %bitcast.refs_0_.half_ref, f32[3,4,32,8,256]{4,3,2,1,0:T(8,128)} %get-tuple-element.32.refs_1_, f32[3,4,32,8,256]{4,3,2,1,0:T(8,128)} %get-tuple-element.27.refs_1_.refs_2_, f32[3,4,8,256]{3,2,1,0:T(8,128)} %copy-done.13, ...), custom_call_target="tpu_custom_call" | custom-call | tf_op jit(solution)/shard_map/adjoint_last/pallas_call | solution.py:155
  83.0 1.2 collective-permute-start.16
  84.1 2.8 %collective-permute-start.22 = (f32[3,4,16,8,256]{4,3,2,1,0:T(8,128)}, f32[3,4,16,8,256]{4,3,2,1,0:T(8,128)S(1)}, u32[]{:S(2)}, u32[]{:S(2)}) collective-permute-start(f32[3,4,16,8,256]{4,3,2,1,0:T(8,128)} %get-tuple-element.37.own.own_keep), channel_id=1, source_target_pairs={{0,1},{2,3},{4,5},{6,7},{8,9},{10,11},{12,13},{14,15},{16,17},{18,... | collective-permute-start | bytes 4718600 | tf_op jit(solution)/shard_map/ppermute | solution.py:387
  87.0 32.8 %collective-permute-done.16.other.other_keep = f32[3,4,16,8,256]{4,3,2,1,0:T(8,128)S(1)} collective-permute-done((f32[3,4,16,8,256]{4,3,2,1,0:T(8,128)}, f32[3,4,16,8,256]{4,3,2,1,0:T(8,128)S(1)}, u32[]{:S(2)}, u32[]{:S(2)}) %collective-permute-start.16) | collective-permute-done | bytes 1572896 | tf_op jit(solution)/shard_map/ppermute | solution.py:386
  119.8 1.2 copy-done
  121.0 5.2 %gram.1 = f32[8,128]{1,0:T(8,128)} custom-call(s32[1]{0:T(128)} %bitcast.refs_0_.half_ref, f32[3,4,16,8,256]{4,3,2,1,0:T(8,128)} %get-tuple-element.37.own.own_keep, f32[3,4,16,8,256]{4,3,2,1,0:T(8,128)} %copy-done, f32[4,8,256]{2,1,0:T(8,128)} %get-tuple-element.39.squares), custom_call_target="tpu_custom_call" | custom-call | tf_op jit(solution)/shard_map/gram/pallas_call | solution.py:227
  126.1 0.6 collective-permute-start.17
  126.8 3.2 %collective-permute-done.17 = f32[8,128]{1,0:T(8,128)S(1)} collective-permute-done((f32[8,128]{1,0:T(8,128)}, f32[8,128]{1,0:T(8,128)S(1)}, u32[]{:S(2)}, u32[]{:S(2)}) %collective-permute-start.17) | collective-permute-done | bytes 4128 | tf_op jit(solution)/shard_map/ppermute | solution.py:364
  130.0 0.7 add.19
  130.7 1.6 %collective-permute-start.18 = (f32[8,128]{1,0:T(8,128)S(1)}, f32[8,128]{1,0:T(8,128)S(1)}, u32[]{:S(2)}, u32[]{:S(2)}) collective-permute-start(f32[8,128]{1,0:T(8,128)S(1)} %add.19), channel_id=1, source_target_pairs={{0,16},{8,24},{16,0},{24,8},{1,17},{9,25},{17,1},{25,9},{2,18},{10... | collective-permute-start | bytes 12296 | tf_op jit(solution)/shard_map/ppermute | solution.py:364
  132.3 2.9 %collective-permute-done.18 = f32[8,128]{1,0:T(8,128)S(1)} collective-permute-done((f32[8,128]{1,0:T(8,128)S(1)}, f32[8,128]{1,0:T(8,128)S(1)}, u32[]{:S(2)}, u32[]{:S(2)}) %collective-permute-start.18) | collective-permute-done | bytes 4128 | tf_op jit(solution)/shard_map/ppermute | solution.py:364
  135.2 1.2 collective-permute-done.19
  136.3 1.9 %collective-permute-start.20 = (f32[8,128]{1,0:T(8,128)S(1)}, f32[8,128]{1,0:T(8,128)S(1)}, u32[]{:S(2)}, u32[]{:S(2)}) collective-permute-start(f32[8,128]{1,0:T(8,128)S(1)} %add.21), channel_id=1, source_target_pairs={{0,4},{2,6},{4,0},{6,2},{1,5},{3,7},{5,1},{7,3},{8,12},{10,14},{12... | collective-permute-start | bytes 12296 | tf_op jit(solution)/shard_map/ppermute | solution.py:364
  138.2 1.8 %collective-permute-done.20 = f32[8,128]{1,0:T(8,128)S(1)} collective-permute-done((f32[8,128]{1,0:T(8,128)S(1)}, f32[8,128]{1,0:T(8,128)S(1)}, u32[]{:S(2)}, u32[]{:S(2)}) %collective-permute-start.20) | collective-permute-done | bytes 4128 | tf_op jit(solution)/shard_map/ppermute | solution.py:364
  140.0 1.8 %collective-permute-start.21 = (f32[8,128]{1,0:T(8,128)S(1)}, f32[8,128]{1,0:T(8,128)S(1)}, u32[]{:S(2)}, u32[]{:S(2)}) collective-permute-start(f32[8,128]{1,0:T(8,128)S(1)} %add.22), channel_id=1, source_target_pairs={{0,1},{1,0},{2,3},{3,2},{4,5},{5,4},{6,7},{7,6},{8,9},{9,8},{10,11... | collective-permute-start | bytes 12296 | tf_op jit(solution)/shard_map/ppermute | solution.py:364
  141.7 10.8 %collective-permute-done.21 = f32[8,128]{1,0:T(8,128)S(1)} collective-permute-done((f32[8,128]{1,0:T(8,128)S(1)}, f32[8,128]{1,0:T(8,128)S(1)}, u32[]{:S(2)}, u32[]{:S(2)}) %collective-permute-start.21) | collective-permute-done | bytes 4128 | tf_op jit(solution)/shard_map/ppermute | solution.py:364
  152.5 0.6 add.23.raw
  153.1 1.1 copy-done.1
  154.3 7.6 %basis.1 = (f32[3,4,32,8,256]{4,3,2,1,0:T(8,128)}, f32[8,8]{1,0:T(8,128)}) custom-call(s32[1]{0:T(128)} %bitcast.refs_0_.half_ref, f32[8,128]{1,0:T(8,128)} %add.23.raw, f32[3,4,16,8,256]{4,3,2,1,0:T(8,128)} %get-tuple-element.37.own.own_keep, f32[3,4,16,8,256]{4,3,2,1,0:T(8,128)} %copy-done, f32[3,4,16,8,256]{4,3,2,1,0:T(8,128)} %get-tuple-element.38.own_send, ...), custom_call_target="tpu_custom_call" | custom-call | tf_op jit(solution)/shard_map/basis/pallas_call | solution.py:316
  (48 shorter events, 0.2 us)
Async XLA Ops:
  0.6 11.6 %copy-start.19 = (f32[256]{0:T(256)S(1)}, f32[256]{0:T(256)}, u32[]{:S(2)}) copy-start(f32[256]{0:T(256)} %param.4) | copy-start | bytes 3076
  0.6 12.3 %copy-start.10 = (f32[256,256]{1,0:T(8,128)S(1)}, f32[256,256]{1,0:T(8,128)}, u32[]{:S(2)}) copy-start(f32[256,256]{1,0:T(8,128)} %param.5) | copy-start | bytes 786436
  4.2 12.7 %collective-permute-start.2 = (f32[3,4,32,256]{3,2,1,0:T(8,128)S(1)}, f32[3,4,32,256]{3,2,1,0:T(8,128)S(1)}, u32[]{:S(2)}, u32[]{:S(2)}) collective-permute-start(f32[3,4,32,256]{3,2,1,0:T(8,128)S(1)} %bitcast.32), channel_id=1, source_target_pairs={{0,2},{2,4},{4,6},{6,0},{1,3},{3,5},{5,7},{7,1},{8,10},{10,12},{12... | collective-permute-start | bytes 1179656 | tf_op jit(solution)/shard_map/ppermute | solution.py:345
  4.7 12.2 %collective-permute-start.3 = (f32[3,4,32,256]{3,2,1,0:T(8,128)S(1)}, f32[3,4,32,256]{3,2,1,0:T(8,128)S(1)}, u32[]{:S(2)}, u32[]{:S(2)}) collective-permute-start(f32[3,4,32,256]{3,2,1,0:T(8,128)S(1)} %bitcast.33), channel_id=1, source_target_pairs={{0,6},{2,0},{4,2},{6,4},{1,7},{3,1},{5,3},{7,5},{8,14},{10,8},{12,... | collective-permute-start | bytes 1179656 | tf_op jit(solution)/shard_map/ppermute | solution.py:345
  7.7 9.1 %collective-permute-start = (f32[3,4,8,256]{3,2,1,0:T(8,128)S(1)}, f32[3,4,8,256]{3,2,1,0:T(8,128)S(1)}, u32[]{:S(2)}, u32[]{:S(2)}) collective-permute-start(f32[3,4,8,256]{3,2,1,0:T(8,128)S(1)} %get-tuple-element.43), channel_id=1, source_target_pairs={{0,8},{8,16},{16,24},{24,0},{1,9},{9,17},{17,25},{25,1},{2,10},{10... | collective-permute-start | bytes 294920 | tf_op jit(solution)/shard_map/ppermute | solution.py:345
  10.1 6.7 %collective-permute-start.1 = (f32[3,4,8,256]{3,2,1,0:T(8,128)S(1)}, f32[3,4,8,256]{3,2,1,0:T(8,128)S(1)}, u32[]{:S(2)}, u32[]{:S(2)}) collective-permute-start(f32[3,4,8,256]{3,2,1,0:T(8,128)S(1)} %get-tuple-element.42), channel_id=1, source_target_pairs={{0,24},{8,0},{16,8},{24,16},{1,25},{9,1},{17,9},{25,17},{2,26},{10... | collective-permute-start | bytes 294920 | tf_op jit(solution)/shard_map/ppermute | solution.py:345
  16.8 0.8 copy-start.11
  16.9 0.8 copy-start.12
  16.9 0.8 copy-start.2
  16.9 0.9 copy-start.3
  25.0 9.7 %collective-permute-start.6 = (f32[3,4,32,256]{3,2,1,0:T(8,128)}, f32[3,4,32,256]{3,2,1,0:T(8,128)S(1)}, u32[]{:S(2)}, u32[]{:S(2)}) collective-permute-start(f32[3,4,32,256]{3,2,1,0:T(8,128)} %get-tuple-element.24), channel_id=1, source_target_pairs={{0,2},{2,4},{4,6},{6,0},{1,3},{3,5},{5,7},{7,1},{8,10},{10,12},{12... | collective-permute-start | bytes 1179656 | tf_op jit(solution)/shard_map/ppermute | solution.py:345
  25.0 10.9 %collective-permute-start.7 = (f32[3,4,32,256]{3,2,1,0:T(8,128)}, f32[3,4,32,256]{3,2,1,0:T(8,128)S(1)}, u32[]{:S(2)}, u32[]{:S(2)}) collective-permute-start(f32[3,4,32,256]{3,2,1,0:T(8,128)} %get-tuple-element.25), channel_id=1, source_target_pairs={{0,6},{2,0},{4,2},{6,4},{1,7},{3,1},{5,3},{7,5},{8,14},{10,8},{12,... | collective-permute-start | bytes 1179656 | tf_op jit(solution)/shard_map/ppermute | solution.py:345
  26.8 7.7 %collective-permute-start.4 = (f32[3,4,8,256]{3,2,1,0:T(8,128)}, f32[3,4,8,256]{3,2,1,0:T(8,128)S(1)}, u32[]{:S(2)}, u32[]{:S(2)}) collective-permute-start(f32[3,4,8,256]{3,2,1,0:T(8,128)} %get-tuple-element.22), channel_id=1, source_target_pairs={{0,8},{8,16},{16,24},{24,0},{1,9},{9,17},{17,25},{25,1},{2,10},{10... | collective-permute-start | bytes 294920 | tf_op jit(solution)/shard_map/ppermute | solution.py:345
  27.6 6.9 %collective-permute-start.5 = (f32[3,4,8,256]{3,2,1,0:T(8,128)}, f32[3,4,8,256]{3,2,1,0:T(8,128)S(1)}, u32[]{:S(2)}, u32[]{:S(2)}) collective-permute-start(f32[3,4,8,256]{3,2,1,0:T(8,128)} %get-tuple-element.23), channel_id=1, source_target_pairs={{0,24},{8,0},{16,8},{24,16},{1,25},{9,1},{17,9},{25,17},{2,26},{10... | collective-permute-start | bytes 294920 | tf_op jit(solution)/shard_map/ppermute | solution.py:345
  34.5 1.5 copy-start.15
  34.6 1.4 copy-start.16
  34.7 1.3 copy-start.6
  36.0 0.8 copy-start.7
  45.5 9.7 %collective-permute-start.10 = (f32[3,4,32,256]{3,2,1,0:T(8,128)}, f32[3,4,32,256]{3,2,1,0:T(8,128)S(1)}, u32[]{:S(2)}, u32[]{:S(2)}) collective-permute-start(f32[3,4,32,256]{3,2,1,0:T(8,128)} %get-tuple-element.30), channel_id=1, source_target_pairs={{0,2},{2,4},{4,6},{6,0},{1,3},{3,5},{5,7},{7,1},{8,10},{10,12},{12... | collective-permute-start | bytes 1179656 | tf_op jit(solution)/shard_map/ppermute | solution.py:345
  46.1 10.6 %collective-permute-start.11 = (f32[3,4,32,256]{3,2,1,0:T(8,128)}, f32[3,4,32,256]{3,2,1,0:T(8,128)S(1)}, u32[]{:S(2)}, u32[]{:S(2)}) collective-permute-start(f32[3,4,32,256]{3,2,1,0:T(8,128)} %get-tuple-element.31), channel_id=1, source_target_pairs={{0,6},{2,0},{4,2},{6,4},{1,7},{3,1},{5,3},{7,5},{8,14},{10,8},{12,... | collective-permute-start | bytes 1179656 | tf_op jit(solution)/shard_map/ppermute | solution.py:345
  47.4 7.7 %collective-permute-start.8 = (f32[3,4,8,256]{3,2,1,0:T(8,128)}, f32[3,4,8,256]{3,2,1,0:T(8,128)S(1)}, u32[]{:S(2)}, u32[]{:S(2)}) collective-permute-start(f32[3,4,8,256]{3,2,1,0:T(8,128)} %get-tuple-element.28), channel_id=1, source_target_pairs={{0,8},{8,16},{16,24},{24,0},{1,9},{9,17},{17,25},{25,1},{2,10},{10... | collective-permute-start | bytes 294920 | tf_op jit(solution)/shard_map/ppermute | solution.py:345
  48.2 7.0 %collective-permute-start.9 = (f32[3,4,8,256]{3,2,1,0:T(8,128)}, f32[3,4,8,256]{3,2,1,0:T(8,128)S(1)}, u32[]{:S(2)}, u32[]{:S(2)}) collective-permute-start(f32[3,4,8,256]{3,2,1,0:T(8,128)} %get-tuple-element.29), channel_id=1, source_target_pairs={{0,24},{8,0},{16,8},{24,16},{1,25},{9,1},{17,9},{25,17},{2,26},{10... | collective-permute-start | bytes 294920 | tf_op jit(solution)/shard_map/ppermute | solution.py:345
  55.2 1.5 copy-start.17
  55.2 1.5 copy-start.18
  55.2 1.5 copy-start.8
  56.7 0.8 copy-start.9
  64.6 9.6 %collective-permute-start.14 = (f32[3,4,32,256]{3,2,1,0:T(8,128)}, f32[3,4,32,256]{3,2,1,0:T(8,128)S(1)}, u32[]{:S(2)}, u32[]{:S(2)}) collective-permute-start(f32[3,4,32,256]{3,2,1,0:T(8,128)} %get-tuple-element.35), channel_id=1, source_target_pairs={{0,2},{2,4},{4,6},{6,0},{1,3},{3,5},{5,7},{7,1},{8,10},{10,12},{12... | collective-permute-start | bytes 1179656 | tf_op jit(solution)/shard_map/ppermute | solution.py:345
  65.1 10.8 %collective-permute-start.15 = (f32[3,4,32,256]{3,2,1,0:T(8,128)}, f32[3,4,32,256]{3,2,1,0:T(8,128)S(1)}, u32[]{:S(2)}, u32[]{:S(2)}) collective-permute-start(f32[3,4,32,256]{3,2,1,0:T(8,128)} %get-tuple-element.36), channel_id=1, source_target_pairs={{0,6},{2,0},{4,2},{6,4},{1,7},{3,1},{5,3},{7,5},{8,14},{10,8},{12,... | collective-permute-start | bytes 1179656 | tf_op jit(solution)/shard_map/ppermute | solution.py:345
  66.5 7.7 %collective-permute-start.12 = (f32[3,4,8,256]{3,2,1,0:T(8,128)}, f32[3,4,8,256]{3,2,1,0:T(8,128)S(1)}, u32[]{:S(2)}, u32[]{:S(2)}) collective-permute-start(f32[3,4,8,256]{3,2,1,0:T(8,128)} %get-tuple-element.33), channel_id=1, source_target_pairs={{0,8},{8,16},{16,24},{24,0},{1,9},{9,17},{17,25},{25,1},{2,10},{10... | collective-permute-start | bytes 294920 | tf_op jit(solution)/shard_map/ppermute | solution.py:345
  67.2 7.1 %collective-permute-start.13 = (f32[3,4,8,256]{3,2,1,0:T(8,128)}, f32[3,4,8,256]{3,2,1,0:T(8,128)S(1)}, u32[]{:S(2)}, u32[]{:S(2)}) collective-permute-start(f32[3,4,8,256]{3,2,1,0:T(8,128)} %get-tuple-element.34), channel_id=1, source_target_pairs={{0,24},{8,0},{16,8},{24,16},{1,25},{9,1},{17,9},{25,17},{2,26},{10... | collective-permute-start | bytes 294920 | tf_op jit(solution)/shard_map/ppermute | solution.py:345
  74.3 1.6 copy-start.13
  74.3 1.6 copy-start.14
  74.3 1.6 copy-start.4
  75.8 0.8 copy-start.5
  83.0 36.9 %collective-permute-start.16 = (f32[3,4,16,8,256]{4,3,2,1,0:T(8,128)}, f32[3,4,16,8,256]{4,3,2,1,0:T(8,128)S(1)}, u32[]{:S(2)}, u32[]{:S(2)}) collective-permute-start(f32[3,4,16,8,256]{4,3,2,1,0:T(8,128)} %get-tuple-element.38.own_send), channel_id=1, source_target_pairs={{0,1},{1,0},{2,3},{3,2},{4,5},{5,4},{6,7},{7,6},{8,9},{9,8},{10,11... | collective-permute-start | bytes 4718600 | tf_op jit(solution)/shard_map/ppermute | solution.py:386
  84.1 69.0 %collective-permute-start.22 = (f32[3,4,16,8,256]{4,3,2,1,0:T(8,128)}, f32[3,4,16,8,256]{4,3,2,1,0:T(8,128)S(1)}, u32[]{:S(2)}, u32[]{:S(2)}) collective-permute-start(f32[3,4,16,8,256]{4,3,2,1,0:T(8,128)} %get-tuple-element.37.own.own_keep), channel_id=1, source_target_pairs={{0,1},{2,3},{4,5},{6,7},{8,9},{10,11},{12,13},{14,15},{16,17},{18,... | collective-permute-start | bytes 4718600 | tf_op jit(solution)/shard_map/ppermute | solution.py:387
  119.8 1.2 copy-start
  126.1 3.8 %collective-permute-start.17 = (f32[8,128]{1,0:T(8,128)}, f32[8,128]{1,0:T(8,128)S(1)}, u32[]{:S(2)}, u32[]{:S(2)}) collective-permute-start(f32[8,128]{1,0:T(8,128)} %gram.1), channel_id=1, source_target_pairs={{0,8},{8,0},{16,24},{24,16},{1,9},{9,1},{17,25},{25,17},{2,10},{10... | collective-permute-start | bytes 12296 | tf_op jit(solution)/shard_map/ppermute | solution.py:364
  130.7 4.5 %collective-permute-start.18 = (f32[8,128]{1,0:T(8,128)S(1)}, f32[8,128]{1,0:T(8,128)S(1)}, u32[]{:S(2)}, u32[]{:S(2)}) collective-permute-start(f32[8,128]{1,0:T(8,128)S(1)} %add.19), channel_id=1, source_target_pairs={{0,16},{8,24},{16,0},{24,8},{1,17},{9,25},{17,1},{25,9},{2,18},{10... | collective-permute-start | bytes 12296 | tf_op jit(solution)/shard_map/ppermute | solution.py:364
  135.2 1.2 collective-permute-start.19
  136.3 3.6 %collective-permute-start.20 = (f32[8,128]{1,0:T(8,128)S(1)}, f32[8,128]{1,0:T(8,128)S(1)}, u32[]{:S(2)}, u32[]{:S(2)}) collective-permute-start(f32[8,128]{1,0:T(8,128)S(1)} %add.21), channel_id=1, source_target_pairs={{0,4},{2,6},{4,0},{6,2},{1,5},{3,7},{5,1},{7,3},{8,12},{10,14},{12... | collective-permute-start | bytes 12296 | tf_op jit(solution)/shard_map/ppermute | solution.py:364
  140.0 12.6 %collective-permute-start.21 = (f32[8,128]{1,0:T(8,128)S(1)}, f32[8,128]{1,0:T(8,128)S(1)}, u32[]{:S(2)}, u32[]{:S(2)}) collective-permute-start(f32[8,128]{1,0:T(8,128)S(1)} %add.22), channel_id=1, source_target_pairs={{0,1},{1,0},{2,3},{3,2},{4,5},{5,4},{6,7},{7,6},{8,9},{9,8},{10,11... | collective-permute-start | bytes 12296 | tf_op jit(solution)/shard_map/ppermute | solution.py:364
  153.1 1.1 copy-start.1

commit v2 on v0

v2 whole, which is shorter than its diff:
```python
import functools

import jax
import jax.numpy as jnp
from jax import lax
from jax.experimental import pallas as pl
from jax.experimental.pallas import tpu as pltpu
from jax.sharding import PartitionSpec as P


step_length = 0.4
viscosity = 0.2
VMEM_LIMIT = 8 * 1024 * 1024
X_CHUNK = 4


def split_halves(value):
    high = value.astype(jnp.bfloat16)
    low = (value - high.astype(jnp.float32)).astype(jnp.bfloat16)
    return high, low


def wall_product(high, low, wall_ref):
    dot = functools.partial(jnp.dot, preferred_element_type=jnp.float32)
    return dot(low, wall_ref[0]) + dot(high, wall_ref[1]) + dot(high, wall_ref[0])


def side_row(face, comp, x0, count, nz):
    lanes = face.shape[2]
    rows = [
        jnp.concatenate([face[comp, 0, h, pl.ds(x0 + k, nz, stride=0), :] for h in range(lanes)], axis=1)
        for k in range(count)
    ]
    return jnp.stack(rows, axis=0)


def stencil_chunk(cur, comp, x0, edges, zlo, zhi, coef, adjoint, center):
    mid = cur[comp, 0, pl.ds(x0, X_CHUNK)]
    west = jnp.concatenate([edges[0][None], mid[: X_CHUNK - 1]], axis=0)
    east = jnp.concatenate([mid[1:], edges[1][None]], axis=0)
    nz = mid.shape[1]
    rows = lax.broadcasted_iota(jnp.int32, mid.shape, 1)
    south = jnp.where(rows == 0, side_row(zlo, comp, x0, X_CHUNK, nz), pltpu.roll(mid, 1, 1))
    north = jnp.where(rows == nz - 1, side_row(zhi, comp, x0, X_CHUNK, nz), pltpu.roll(mid, nz - 1, 1))
    plus, minus = coef[0][None], coef[1][None]
    if adjoint:
        plus, minus = minus, plus
    value = center * mid + plus * east + minus * west + (north + south)
    if adjoint and comp == 1:
        value = value - coef[2][None] * cur[0, 0, pl.ds(x0, X_CHUNK)]
    if not adjoint and comp == 0:
        value = value - coef[2][None] * cur[1, 0, pl.ds(x0, X_CHUNK)]
    return value


def put_faces(result, comp, lanes_ref, first_x, last_x, first_z, last_z):
    size = result.shape[0]
    nx, nz = first_z.shape[3], first_x.shape[2]
    first_x[comp, 0] = result[:nz]
    last_x[comp, 0] = result[size - nz :]
    for h in range(lanes_ref.shape[0]):
        lanes_ref[h] = result[:, h * 128 : (h + 1) * 128]
        first_z[comp, 0, h] = lanes_ref[h, pl.ds(0, nx, stride=nz), :]
        last_z[comp, 0, h] = lanes_ref[h, pl.ds(nz - 1, nx, stride=nz), :]


def stage_body(kind, span, *refs):
    half_ref, *refs = refs
    src = None
    if kind == "forward_first":
        cur, *refs = refs
    else:
        cur, src, *refs = refs
    xlo, xhi, zlo, zhi, coef, wall, *rest = refs

    def one(j, _):
        view = lambda ref: ref.at[:, pl.ds(j, 1)]
        fields = [view(cur), None if src is None else view(src), view(xlo), view(xhi), view(zlo), view(zhi), coef, wall]
        if kind == "adjoint_last":
            last_column(half_ref, *fields[:7], *[r.at[:, pl.ds(j - span[0], 1)] for r in rest])
        elif kind == "forward_last":
            out, solved, squares, *more = rest
            faces, work = more[:4], more[4:]
            outs = [view(out), view(solved), squares.at[pl.ds(j, 1)]] + [view(r) for r in faces]
            stage_column(kind, *fields, outs, *work)
        else:
            stage_column(kind, *fields, [view(r) for r in rest[:5]], *rest[5:])
        return 0

    lax.fori_loop(span[0], span[1], one, 0)


def last_column(half_ref, cur, src, xlo, xhi, zlo, zhi, coef, keep, send):
    nx = cur.shape[2]
    half_x = nx // 2
    center = 1.0 / (step_length * viscosity) - 4.0
    for role, target in ((half_ref[0], keep), (1 - half_ref[0], send)):
        base = pl.multiple_of(role * half_x, half_x)
        for comp in range(3):
            for spot in range(0, half_x, X_CHUNK):
                x0 = base + spot
                if spot == 0:
                    west = jnp.where(role == 0, xlo[comp, 0], cur[comp, 0, jnp.maximum(x0 - 1, 0)])
                else:
                    west = cur[comp, 0, x0 - 1]
                if spot + X_CHUNK == half_x:
                    east = jnp.where(role == 1, xhi[comp, 0], cur[comp, 0, jnp.minimum(x0 + X_CHUNK, nx - 1)])
                else:
                    east = cur[comp, 0, x0 + X_CHUNK]
                value = stencil_chunk(cur, comp, x0, (west, east), zlo, zhi, coef, True, center)
                target[comp, 0, spot : spot + X_CHUNK] = value + src[comp, 0, pl.ds(x0, X_CHUNK)]


def stage_column(kind, cur, src, xlo, xhi, zlo, zhi, coef, wall, outs, high, low, lanes):
    nx, nz, ny = cur.shape[2:]
    adjoint = kind.startswith("adjoint")
    center = 1.0 / (step_length * viscosity) - 4.0
    if kind == "forward_first":
        center = center + 1.0 / viscosity
    size = nx * nz
    total = None
    for comp in range(3):
        for x0 in range(0, nx, X_CHUNK):
            west = xlo[comp, 0] if x0 == 0 else cur[comp, 0, x0 - 1]
            east = xhi[comp, 0] if x0 + X_CHUNK == nx else cur[comp, 0, x0 + X_CHUNK]
            value = stencil_chunk(cur, comp, x0, (west, east), zlo, zhi, coef, adjoint, center)
            if kind == "forward_last":
                value = value + (1.0 / viscosity) * src[comp, 0, x0 : x0 + X_CHUNK]
            elif adjoint:
                value = value + src[comp, 0, x0 : x0 + X_CHUNK]
            h, l = split_halves(value.reshape(X_CHUNK * nz, ny))
            spot = (comp * nx + x0) * nz
            high[spot : spot + X_CHUNK * nz] = h
            low[spot : spot + X_CHUNK * nz] = l
        part = slice(comp * size, (comp + 1) * size)
        result = wall_product(high[part], low[part], wall.at[pl.ds(2, 2)] if adjoint else wall.at[pl.ds(0, 2)])
        if kind == "forward_last":
            tile = result.reshape(nx, nz, ny)
            sums = jnp.sum(tile * tile, axis=0)
            total = sums if total is None else total + sums
            scaled = result * (1.0 / viscosity)
            outs[0][comp, 0] = scaled.reshape(nx, nz, ny)
            h, l = split_halves(scaled)
            result = wall_product(h, l, wall.at[pl.ds(4, 2)])
            outs[1][comp, 0] = result.reshape(nx, nz, ny)
        else:
            outs[0][comp, 0] = result.reshape(nx, nz, ny)
        put_faces(result, comp, lanes, *outs[-4:])
    if kind == "forward_last":
        outs[2][0] = total


def in_vmem(shape):
    return pltpu.VMEM(shape, jnp.float32)


def hold(value):
    return pltpu.with_memory_space_constraint(value, pltpu.VMEM)


def run_stage(kind, half, cur, src, faces, coef, wall, span=None):
    three, columns, nx, nz, ny = cur.shape
    span = span or (0, columns)
    field = in_vmem(cur.shape)
    half_field = in_vmem((three, span[1] - span[0], nx // 2, nz, ny))
    x_out = in_vmem((three, columns, nz, ny))
    z_out = in_vmem((three, columns, ny // 128, nx, 128))
    face_outs = [x_out, x_out, z_out, z_out]
    scratch = [pltpu.VMEM((three * nx * nz, ny), jnp.bfloat16)] * 2
    scratch += [pltpu.VMEM((ny // 128, nx * nz, 128), jnp.float32)]
    if kind == "forward_last":
        outs = [field, field, in_vmem((columns, nz, ny))] + face_outs
    elif kind == "adjoint_last":
        outs, scratch = [half_field, half_field], []
    else:
        outs = [field] + face_outs
    fields = (cur,) if src is None else (cur, src)
    operands = [half] + [hold(v) for v in (*fields, *faces, coef, wall)]
    vmem = pl.BlockSpec(memory_space=pltpu.VMEM)
    return pl.pallas_call(
        functools.partial(stage_body, kind, span),
        out_shape=outs,
        in_specs=[pl.BlockSpec(memory_space=pltpu.SMEM)] + [vmem] * (len(operands) - 1),
        out_specs=[vmem] * len(outs),
        scratch_shapes=scratch,
        compiler_params=pltpu.CompilerParams(vmem_limit_bytes=VMEM_LIMIT),
    )(*operands)


def setup_body(wall_solve, velocity, coef, wall):
    ny = wall_solve.shape[0]
    speed = velocity[...]
    lanes = lax.broadcasted_iota(jnp.int32, (1, ny), 1)
    after, before = pltpu.roll(speed, ny - 1, 1), pltpu.roll(speed, 1, 1)
    shear = (after - before) * 0.5
    shear = jnp.where(lanes == 0, after - speed, jnp.where(lanes == ny - 1, speed - before, shear))
    advect = (0.5 / viscosity) * speed
    for k, row in enumerate((1.0 - advect, 1.0 + advect, (1.0 / viscosity) * shear)):
        coef[k] = jnp.broadcast_to(row, coef.shape[1:])
    plain = wall_solve[...]
    turned = plain.T
    for k, value in enumerate((step_length * viscosity * plain, step_length * viscosity * turned, viscosity * turned)):
        wall[2 * k], wall[2 * k + 1] = split_halves(value)


def run_setup(wall_solve, velocity, nz):
    ny = wall_solve.shape[0]
    vmem = pl.BlockSpec(memory_space=pltpu.VMEM)
    return pl.pallas_call(
        setup_body,
        out_shape=[in_vmem((3, nz, ny)), pltpu.VMEM((6, ny, ny), jnp.bfloat16)],
        in_specs=[vmem] * 2,
        out_specs=[vmem] * 2,
        compiler_params=pltpu.CompilerParams(vmem_limit_bytes=VMEM_LIMIT),
        name="setup",
    )(wall_solve, velocity.reshape(1, ny))


def edges_body(source, *refs):
    *outs, lanes, sems = refs
    field, first_x, last_x, first_z, last_z = outs[:5]
    three, columns, nx, nz, ny = field.shape

    def fetch(j):
        return pltpu.make_async_copy(source.at[:, j], field.at[:, j], sems.at[j])

    for j in range(columns):
        fetch(j).start()
    for j in range(columns):
        fetch(j).wait()
        view = lambda ref: ref.at[:, pl.ds(j, 1)]
        for comp in range(three):
            tile = field[comp, j].reshape(nx * nz, ny)
            put_faces(tile, comp, lanes, view(first_x), view(last_x), view(first_z), view(last_z))
            if len(outs) > 5 and j < outs[5].shape[1]:
                outs[5][comp, j] = field[comp, j]


def run_edges(source, front=None):
    three, columns, nx, nz, ny = source.shape
    x_out = in_vmem((three, columns, nz, ny))
    z_out = in_vmem((three, columns, ny // 128, nx, 128))
    outs = [in_vmem(source.shape), x_out, x_out, z_out, z_out]
    if front is not None:
        outs += [in_vmem((three, front, nx, nz, ny))]
    vmem = pl.BlockSpec(memory_space=pltpu.VMEM)
    return pl.pallas_call(
        edges_body,
        out_shape=outs,
        in_specs=[pl.BlockSpec(memory_space=pltpu.HBM)],
        out_specs=[vmem] * len(outs),
        scratch_shapes=[pltpu.VMEM((ny // 128, nx * nz, 128), jnp.float32), pltpu.SemaphoreType.DMA((columns,))],
        compiler_params=pltpu.CompilerParams(vmem_limit_bytes=VMEM_LIMIT),
        name="edges",
    )(pltpu.with_memory_space_constraint(source, pltpu.HBM))


def rows_to_matrix(sums, table, count, columns):
    lanes = lax.broadcasted_iota(jnp.int32, (count, 128), 1)
    zero = jnp.zeros((1, 128), jnp.float32)
    plain = jnp.zeros((count, 128), jnp.float32)
    moved = plain
    for i in range(count):
        if not any((i, j) in table for j in range(count)):
            continue
        stack = jnp.concatenate(
            [sums[table[i, j] : table[i, j] + 1] if (i, j) in table else zero for j in range(count)], axis=0
        )
        column = jnp.sum(stack, axis=1, keepdims=True)
        plain = jnp.where(lanes == i, column, plain)
        moved = jnp.where(lanes == (i + columns) % count, column, moved)
    return plain, moved


def pick_order(plain, moved, half_ref, columns):
    return jnp.where(half_ref[0] == 0, plain, pltpu.roll(moved, columns, 0))


def pair_sums(fields, pairs, acc, nx, three, ny):
    used = sorted({i for pair in pairs for i in pair})
    for lane in range(0, ny, 128):

        def body(k, carry):
            comp = k // nx
            x = k - comp * nx
            cols = {i: fields[i][0][comp, fields[i][1], x, :, lane : lane + 128] for i in used}
            return tuple(c + cols[i] * cols[j] for c, (i, j) in zip(carry, pairs))

        done = lax.fori_loop(0, three * nx, body, tuple(acc[p] for p in range(len(pairs))), unroll=4)
        for p in range(len(pairs)):
            acc[p] = done[p]


def gram_tables(sums, acc, pairs):
    table = {}
    for p, (i, j) in enumerate(pairs):
        sums[p : p + 1] = jnp.sum(acc[p], axis=0, keepdims=True)
        table[i, j] = table[j, i] = p
    return table


def own_gram_body(half_ref, front_keep, front_send, late_keep, late_send, squares, out, acc, sums):
    three, front, nx, _, ny = front_keep.shape
    columns = front + late_keep.shape[1]
    count = 2 * columns
    pairs = [(i, j) for i in range(columns) for j in range(i, columns)]
    acc[...] = jnp.zeros_like(acc)
    for ahead, behind in ((front_keep, late_keep), (front_send, late_send)):
        fields = [(ahead, i) for i in range(front)] + [(behind, i) for i in range(columns - front)]
        pair_sums(fields, pairs, acc, nx, three, ny)
    plain, moved = rows_to_matrix(sums, gram_tables(sums, acc, pairs), count, columns)
    lanes = lax.broadcasted_iota(jnp.int32, (count, 128), 1)
    norm_rows = []
    for i in range(columns):
        rows = sum(squares[i, :, k : k + 128] for k in range(0, ny, 128))
        norm_rows.append(jnp.sum(rows, axis=0, keepdims=True))
    norm_rows += [jnp.zeros((1, 128), jnp.float32)] * columns
    norm = jnp.sum(jnp.concatenate(norm_rows, axis=0), axis=1, keepdims=True)
    plain = jnp.where(lanes == count, norm, plain)
    moved = jnp.where(lanes == count, norm, moved)
    out[...] = pick_order(plain, moved, half_ref, columns)


def cross_gram_body(half_ref, fk, fs, lk, ls, ek, es, other, base, out, acc, sums):
    three, front, nx, _, ny = fk.shape
    late = lk.shape[1]
    columns = front + late
    early = ek.shape[1]
    count = 2 * columns
    wide = [(i, columns + j) for i in range(columns) for j in range(early)]
    narrow = [(front + i, columns + early + j) for i in range(late) for j in range(columns - early)]
    acc[...] = jnp.zeros_like(acc)

    def own(ahead, behind):
        return [(ahead, i) for i in range(front)] + [(behind, i) for i in range(late)]

    for ahead, behind, extra in ((fk, lk, ek), (fs, ls, es)):
        pair_sums(own(ahead, behind) + [(extra, j) for j in range(early)], wide, acc, nx, three, ny)
    rest = acc.at[pl.ds(len(wide), len(narrow))]
    pair_sums(own(fk, lk) + [None] * early + [(other, j) for j in range(columns - early)], narrow, rest, nx, three, ny)
    for p, (i, j) in enumerate(wide):
        if i < early:
            acc[p] = jnp.where(half_ref[0] == 0, acc[p], 0.0)
    plain, moved = rows_to_matrix(sums, gram_tables(sums, acc, wide + narrow), count, columns)
    out[...] = base[...] + pick_order(plain, moved, half_ref, columns)


def run_gram(body, half, fields, npairs, count):
    nz = fields[0].shape[3]
    vmem = pl.BlockSpec(memory_space=pltpu.VMEM)
    return pl.pallas_call(
        body,
        out_shape=jax.ShapeDtypeStruct((count, 128), jnp.float32),
        in_specs=[pl.BlockSpec(memory_space=pltpu.SMEM)] + [vmem] * len(fields),
        out_specs=vmem,
        scratch_shapes=[pltpu.VMEM((npairs, nz, 128), jnp.float32), pltpu.VMEM((npairs, 128), jnp.float32)],
        compiler_params=pltpu.CompilerParams(vmem_limit_bytes=VMEM_LIMIT),
    )(half, *[hold(v) for v in fields])


def factor_body(entries, columns, half_ref, raw, factor, coef):
    side = step_length * viscosity
    count = 2 * columns
    total = raw[...]
    lanes = lax.broadcasted_iota(jnp.int32, (count, 128), 1)
    rows = lax.broadcasted_iota(jnp.int32, (count, 128), 0)
    scale = jnp.sqrt(total[:, count : count + 1] / entries + 1e-06)
    inverse_scale = side / scale
    scale_row = jnp.sum(jnp.where(lanes == rows, jnp.broadcast_to(scale, (count, 128)), 0.0), axis=0, keepdims=True)
    scale_row = jnp.where(lanes < count, jnp.broadcast_to(scale_row, (count, 128)), 1.0)
    gram = total * (side * side / entries) / (jnp.broadcast_to(scale, (count, 128)) * scale_row)
    work = jnp.where(lanes < count, gram, jnp.where(lanes == rows + count, 1.0, 0.0))
    for k in range(count):
        pivot = work[k : k + 1]
        root = jnp.sqrt(pivot[:, k : k + 1])
        line = pivot / root
        ratio = jnp.where(rows[:, 0:1] > k, work[:, k : k + 1], 0.0) / root
        work = jnp.where(rows == k, jnp.broadcast_to(line, (count, 128)), work - ratio * line)
    factor[...] = jnp.where(lanes >= rows, work, 0.0)[:, :count]
    first = half_ref[0] == 0
    for j in range(columns):
        row = jnp.where(first, work[j : j + 1], work[columns + j : columns + j + 1])
        for i in range(count):
            lo = (i + columns) % count
            pick = jnp.where(first, row[:, count + i : count + i + 1], row[:, count + lo : count + lo + 1])
            norm = jnp.where(first, inverse_scale[i : i + 1], inverse_scale[lo : lo + 1])
            coef[j * count + i] = jnp.broadcast_to(pick * norm, coef.shape[1:])


def run_factor(entries, columns, half, raw):
    count = 2 * columns
    vmem = pl.BlockSpec(memory_space=pltpu.VMEM)
    return pl.pallas_call(
        functools.partial(factor_body, entries, columns),
        out_shape=[
            jax.ShapeDtypeStruct((count, count), jnp.float32),
            jax.ShapeDtypeStruct((columns * count, 8, 128), jnp.float32),
        ],
        in_specs=[pl.BlockSpec(memory_space=pltpu.SMEM), vmem],
        out_specs=[vmem, vmem],
        compiler_params=pltpu.CompilerParams(vmem_limit_bytes=VMEM_LIMIT),
        name="factor",
    )(half, raw)


def basis_body(count, aliased, half_ref, coef, *refs):
    fields, out = (refs[:-2], refs[-1]) if aliased else (refs[:-1], refs[-1])
    three, columns, nx, _, ny = out.shape
    base = pl.program_id(0) * nx
    spots = [(ref, i) for ref in fields for i in range(ref.shape[1])]

    def body(k, _):
        comp = k // nx
        x = k - comp * nx
        for lane in range(0, ny, 128):
            part = slice(lane, lane + 128)
            cols = [ref[comp, i, base + x, :, part] for ref, i in spots]
            for j in range(columns):
                terms = [coef[j * count + i] * cols[i] for i in range(count)]
                while len(terms) > 1:
                    terms = [a + b for a, b in zip(terms[::2], terms[1::2])]
                out[comp, j, x, :, part] = terms[0]
        return 0

    lax.fori_loop(0, three * nx, body, 0, unroll=2)


def run_basis(half, coef, fields, columns, keep, target=None):
    three, _, half_x, nz, ny = fields[0].shape
    per = 2
    block = (three, columns, half_x // per, nz, ny)
    vmem = pl.BlockSpec(memory_space=pltpu.VMEM)

    def place(k, h):
        return (0, 0, k + per * (h[0] if keep else 1 - h[0]), 0, 0)

    operands = [hold(v) for v in (coef, *fields)]
    specs = [vmem] * len(operands)
    if target is not None:
        operands, specs = operands + [target], specs + [pl.BlockSpec(memory_space=pl.ANY)]
    return pl.pallas_call(
        functools.partial(basis_body, 2 * columns, target is not None),
        out_shape=jax.ShapeDtypeStruct((three, columns, 2 * half_x, nz, ny), jnp.float32),
        grid_spec=pltpu.PrefetchScalarGridSpec(
            num_scalar_prefetch=1, grid=(per,), in_specs=specs, out_specs=pl.BlockSpec(block, place)
        ),
        input_output_aliases={} if target is None else {len(operands): 0},
        compiler_params=pltpu.CompilerParams(vmem_limit_bytes=VMEM_LIMIT),
        name="basis",
    )(half, *operands)


def shift(value, axis, amount):
    count = lax.axis_size(axis)
    return lax.ppermute(value, axis, [(i, (i + amount) % count) for i in range(count)])


def exchange(first_x, last_x, first_z, last_z):
    zlo = shift(last_z, "gz", 1)
    zhi = shift(first_z, "gz", -1)
    xlo = shift(last_x, "gx", 1)
    xhi = shift(first_x, "gx", -1)
    return xlo, xhi, zlo, zhi


def all_sum(value, axes):
    for axis in axes:
        count = lax.axis_size(axis)
        if count & (count - 1):
            value = lax.psum(value, axis)
            continue
        mask = 1
        while mask < count:
            value = value + lax.ppermute(value, axis, [(i, i ^ mask) for i in range(count)])
            mask *= 2
    return value


def swap(value):
    return lax.ppermute(value, "sa", [(0, 1), (1, 0)])


def shards(forcing, velocity, wall_solve):
    columns, nx, nz, ny = forcing.shape[1:]
    entries = float(3 * nx * lax.axis_size("gx") * nz * lax.axis_size("gz") * ny)
    half = lax.axis_index("sa").astype(jnp.int32).reshape(1)
    early = columns // 2
    count = 2 * columns
    forcing, *edge, front = run_edges(forcing, early)
    guest = swap(front)
    faces = exchange(*edge)
    coef, wall = run_setup(wall_solve, velocity, nz)

    def stage(kind, *args):
        return run_stage(kind, half, *args)

    q1, *edge = stage("forward_first", forcing, None, faces, coef, wall)
    faces = exchange(*edge)
    q2, s1, squares, *edge = stage("forward_last", q1, forcing, faces, coef, wall)
    faces = exchange(*edge)
    s2, *edge = stage("adjoint_first", s1, q2, faces, coef, wall)
    faces = exchange(*edge)
    late_keep, late_send = stage("adjoint_last", s2, q2, faces, coef, wall, (early, columns))
    other_keep = swap(late_send)
    front_keep, front_send = stage("adjoint_last", s2, q2, faces, coef, wall, (0, early))

    guest, *edge = run_edges(guest)
    faces = exchange(*edge)
    g1, *edge = stage("forward_first", guest, None, faces, coef, wall)
    faces = exchange(*edge)
    g2, h1, _, *edge = stage("forward_last", g1, guest, faces, coef, wall)
    faces = exchange(*edge)
    h2, *edge = stage("adjoint_first", h1, g2, faces, coef, wall)
    faces = exchange(*edge)
    early_keep, early_send = stage("adjoint_last", h2, g2, faces, coef, wall)

    own = (front_keep, front_send, late_keep, late_send)
    base = run_gram(own_gram_body, half, (*own, squares), columns * (columns + 1) // 2, count)
    late_keep, other_keep = lax.optimization_barrier((late_keep, other_keep))
    other_send = swap(late_keep)
    cross = (*own, early_keep, early_send, other_keep, base)
    npairs = columns * early + (columns - early) ** 2
    raw = run_gram(cross_gram_body, half, cross, npairs, count)
    raw = all_sum(raw, ("gx", "gz", "sa"))
    factor, coef = run_factor(entries, columns, half, raw)
    basis = run_basis(half, coef, (front_keep, late_keep, early_keep, other_keep), columns, True)
    basis = run_basis(half, coef, (front_send, late_send, early_send, other_send), columns, False, basis)
    return basis, factor


def solution(mesh):
    return jax.shard_map(
        shards,
        mesh=mesh,
        in_specs=(P(None, "sa", "gx", "gz", None), P(), P()),
        out_specs=(P(None, "sa", "gx", "gz", None), P()),
        check_vma=False,
    )
```

time: 342 us -> 144 us (0.42)
  waiting for transfers between devices: 141 us -> 50.7 us
  other arithmetic: 74.8 us -> 0.02 us
  starting transfers between devices: 15 us -> 55.1 us
  blocking collectives: 39.6 us -> 0 us
  Pallas kernels: 0 us -> 33.9 us
  matrix products: 30.2 us -> 0 us
  between operations: 19.9 us -> 0.81 us
  local copies, waits for them, and re-layouts: 21.2 us -> 3.24 us
    all_gather x1 -> x0, waiting for transfers between devices: 78.3 us -> none  [shards(): gathered = lax.all_gather(current, 'sa', axis=1, tiled=True)]
    ppermute x16 -> x40, starting transfers between devices: 15 us -> 55.1 us  [the longest x32 47.5 us: shift(): lax.ppermute(value, axis, [(i, (i + amount) % count) for i in range(count)])]
    div x11 -> x0, other arithmetic: 39.8 us -> none  [the longest x1 22.7 us: upper_inverse(): row_list[pivot_index] = current_row / factor[pivot_index, pivot_index]]
    psum x1 -> x0, blocking collectives: 39.6 us -> none  [shards(): raw_gram, totals = lax.psum((gram_local, slot_norms), ('gx', 'gz', 'sa'))]
    pallas_call x0 -> x17, Pallas kernels: none -> 33.9 us  [the longest x9 19.5 us: run_stage(): pl.pallas_call(functools.partial(stage_body, kind, span), out_shape=outs,...]
    dot_general x6 -> x0, matrix products: 30.2 us -> none  [the longest x1 11.2 us: shards(): jnp.einsum('cixzy,ij->cjxzy', gathered, own_coef, precision=lax.Precision...]
    sub x8 -> x0, other arithmetic: 18.2 us -> none  [the longest x7 17.6 us: upper_factor(): current_row - row_list[other_index][pivot_index] * row_list[other_index]]
    slice x24 -> x0, local copies, waits for them, and re-layouts: 13.7 us -> none  [the longest x8 4.88 us: upper_factor(): current_row[pivot_index]]
  transfers between devices with their start and end apart: 17 -> 40, of which waited for: 16 -> 24; matrix products, arithmetic and copies ran while one was open for 2% -> 0% of each run, Pallas kernels for 0% -> 17%
where the time goes in v2:
time: 144 us
  starting transfers between devices  55.1 us (38%)
  waiting for transfers between devices  50.7 us (35%)
  Pallas kernels  33.9 us (24%)
  local copies, waits for them, and re-layouts  3.24 us (2%)
    ppermute x32, starting transfers between devices, shift(): lax.ppermute(value, axis, [(i, (i + amount) % count) for i in range(count)])  47.5 us
    ppermute x32, waiting for transfers between devices, shift(): lax.ppermute(value, axis, [(i, (i + amount) % count) for i in range(count)])  24.6 us
    pallas_call x9, Pallas kernels, run_stage(): pl.pallas_call(functools.partial(stage_body, kind, span), out_shape=outs,...  19.5 us
    ppermute x3, waiting for transfers between devices, swap(): return lax.ppermute(value, 'sa', [(0, 1), (1, 0)])  15.7 us
    ppermute x5, waiting for transfers between devices, all_sum(): lax.ppermute(value, axis, [(i, i ^ mask) for i in range(count)])  10.4 us
    ppermute x5, starting transfers between devices, all_sum(): lax.ppermute(value, axis, [(i, i ^ mask) for i in range(count)])  6.14 us
    pallas_call x2, Pallas kernels, run_edges(): pl.pallas_call(edges_body, out_shape=outs, in_specs=[pl.BlockSpec(memory_...  4.38 us
    pallas_call x2, Pallas kernels, run_gram(): pl.pallas_call(body, out_shape=jax.ShapeDtypeStruct((count, 128), jnp.flo...  4.35 us
  transfers between devices with their start and end apart: 40, of which 24 were waited for; matrix products, arithmetic and copies ran while one was open for 0% of the time, Pallas kernels for 17%

profile of v2, /device:TPU:0, one launch (start us, length us, event | category | flops | bytes accessed | tf_op | source)
XLA Modules:
  0.0 143.7 jit_solution(12041579392734386037)
XLA Ops:
  0.6 2.9 %edges.2 = (f32[3,4,32,8,256]{4,3,2,1,0:T(8,128)S(1)}, f32[3,4,8,256]{3,2,1,0:T(8,128)}, f32[3,4,8,256]{3,2,1,0:T(8,128)}, f32[3,4,2,32,128]{4,3,2,1,0:T(8,128)}...) custom-call(f32[3,4,32,8,256]{4,3,2,1,0:T(8,128)} %source.1), custom_call_target="tpu_custom_call" | custom-call | tf_op jit(solution)/shard_map/edges/pallas_call | solution.py:247
  3.6 1.1 copy-done.2
  5.2 1.9 %collective-permute-start.3 = (f32[3,4,2,32,128]{4,3,2,1,0:T(8,128)}, f32[3,4,2,32,128]{4,3,2,1,0:T(8,128)}, u32[]{:S(2)}, u32[]{:S(2)}) collective-permute-start(f32[3,4,2,32,128]{4,3,2,1,0:T(8,128)} %get-tuple-element.62), channel_id=1, source_target_pairs={{0,6},{2,0},{4,2},{6,4},{1,7},{3,1},{5,3},{7,5},{8,14},{10,8},{12,... | collective-permute-start | bytes 1179656 | tf_op jit(solution)/shard_map/ppermute | solution.py:455
  7.1 2.4 %collective-permute-start = (f32[3,4,8,256]{3,2,1,0:T(8,128)}, f32[3,4,8,256]{3,2,1,0:T(8,128)}, u32[]{:S(2)}, u32[]{:S(2)}) collective-permute-start(f32[3,4,8,256]{3,2,1,0:T(8,128)} %get-tuple-element.59), channel_id=1, source_target_pairs={{0,8},{8,16},{16,24},{24,0},{1,9},{9,17},{17,25},{25,1},{2,10},{10... | collective-permute-start | bytes 294920 | tf_op jit(solution)/shard_map/ppermute | solution.py:455
  9.5 2.0 %collective-permute-start.1 = (f32[3,4,8,256]{3,2,1,0:T(8,128)}, f32[3,4,8,256]{3,2,1,0:T(8,128)}, u32[]{:S(2)}, u32[]{:S(2)}) collective-permute-start(f32[3,4,8,256]{3,2,1,0:T(8,128)} %get-tuple-element.60), channel_id=1, source_target_pairs={{0,24},{8,0},{16,8},{24,16},{1,25},{9,1},{17,9},{25,17},{2,26},{10... | collective-permute-start | bytes 294920 | tf_op jit(solution)/shard_map/ppermute | solution.py:455
  11.5 0.9 copy-done
  12.7 2.6 %collective-permute-done.refs_2_ = f32[3,4,8,256]{3,2,1,0:T(8,128)} collective-permute-done((f32[3,4,8,256]{3,2,1,0:T(8,128)}, f32[3,4,8,256]{3,2,1,0:T(8,128)}, u32[]{:S(2)}, u32[]{:S(2)}) %collective-permute-start) | collective-permute-done | bytes 98336 | tf_op jit(solution)/shard_map/ppermute | solution.py:455
  15.3 0.9 collective-permute-done.1.refs_3_
  16.9 3.9 %shard_map.50 = (f32[3,4,32,8,256]{4,3,2,1,0:T(8,128)S(1)}, f32[3,4,8,256]{3,2,1,0:T(8,128)S(1)}, f32[3,4,8,256]{3,2,1,0:T(8,128)S(1)}, f32[3,4,2,32,128]{4,3,2,1,0:T(8,128)S(1)}, f32[3,4,2,32,128]{4,3,2,1,0:T(8,128)S(1)}) custom-call(s32[1]{0:T(128)} %bitcast.refs_0_.half_ref, f32[3,4,32,8,256]{4,3,2,1,0:T(8,128)S(1)} %get-tuple-element.58.refs_1_.refs_2_, ...), custom_call_target="tpu_custom_call" | custom-call | tf_op jit(solution)/shard_map/pallas_call | solution.py:180
  21.0 2.0 %collective-permute-start.7 = (f32[3,4,2,32,128]{4,3,2,1,0:T(8,128)S(1)}, f32[3,4,2,32,128]{4,3,2,1,0:T(8,128)S(1)}, u32[]{:S(2)}, u32[]{:S(2)}) collective-permute-start(f32[3,4,2,32,128]{4,3,2,1,0:T(8,128)S(1)} %get-tuple-element.69), channel_id=1, source_target_pairs={{0,6},{2,0},{4,2},{6,4},{1,7},{3,1},{5,3},{7,5},{8,14},{10,8},{12,... | collective-permute-start | bytes 1179656 | tf_op jit(solution)/shard_map/ppermute | solution.py:455
  23.0 1.4 collective-permute-start.4
  24.4 2.4 %collective-permute-start.5 = (f32[3,4,8,256]{3,2,1,0:T(8,128)S(1)}, f32[3,4,8,256]{3,2,1,0:T(8,128)S(1)}, u32[]{:S(2)}, u32[]{:S(2)}) collective-permute-start(f32[3,4,8,256]{3,2,1,0:T(8,128)S(1)} %get-tuple-element.67), channel_id=1, source_target_pairs={{0,24},{8,0},{16,8},{24,16},{1,25},{9,1},{17,9},{25,17},{2,26},{10... | collective-permute-start | bytes 294920 | tf_op jit(solution)/shard_map/ppermute | solution.py:455
  26.9 1.3 collective-permute-start.16
  28.2 2.4 %collective-permute-done.4.refs_3_ = f32[3,4,8,256]{3,2,1,0:T(8,128)S(1)} collective-permute-done((f32[3,4,8,256]{3,2,1,0:T(8,128)S(1)}, f32[3,4,8,256]{3,2,1,0:T(8,128)S(1)}, u32[]{:S(2)}, u32[]{:S(2)}) %collective-permute-start.4) | collective-permute-done | bytes 98336 | tf_op jit(solution)/shard_map/ppermute | solution.py:455
  31.0 1.2 collective-permute-done.7.refs_6_
  32.2 4.7 %shard_map.51 = (f32[3,4,32,8,256]{4,3,2,1,0:T(8,128)S(1)}, f32[3,4,32,8,256]{4,3,2,1,0:T(8,128)S(1)}, f32[4,8,256]{2,1,0:T(8,128)S(1)}, f32[3,4,8,256]{3,2,1,0:...) custom-call(s32[1]{0:T(128)} %bitcast.refs_0_.half_ref, ...), custom_call_target="tpu_custom_call" | custom-call | tf_op jit(solution)/shard_map/pallas_call | solution.py:180
  37.5 1.7 %collective-permute-start.11 = (f32[3,4,2,32,128]{4,3,2,1,0:T(8,128)S(1)}, f32[3,4,2,32,128]{4,3,2,1,0:T(8,128)S(1)}, u32[]{:S(2)}, u32[]{:S(2)}) collective-permute-start(f32[3,4,2,32,128]{4,3,2,1,0:T(8,128)S(1)} %get-tuple-element.75), channel_id=1, source_target_pairs={{0,6},{2,0},{4,2},{6,4},{1,7},{3,1},{5,3},{7,5},{8,14},{10,8},{12,... | collective-permute-start | bytes 1179656 | tf_op jit(solution)/shard_map/ppermute | solution.py:455
  39.2 0.8 collective-permute-start.8
  40.0 3.0 %collective-permute-start.9 = (f32[3,4,8,256]{3,2,1,0:T(8,128)S(1)}, f32[3,4,8,256]{3,2,1,0:T(8,128)S(1)}, u32[]{:S(2)}, u32[]{:S(2)}) collective-permute-start(f32[3,4,8,256]{3,2,1,0:T(8,128)S(1)} %get-tuple-element.73), channel_id=1, source_target_pairs={{0,24},{8,0},{16,8},{24,16},{1,25},{9,1},{17,9},{25,17},{2,26},{10... | collective-permute-start | bytes 294920 | tf_op jit(solution)/shard_map/ppermute | solution.py:455
  43.1 3.7 %collective-permute-done.8.refs_3_ = f32[3,4,8,256]{3,2,1,0:T(8,128)S(1)} collective-permute-done((f32[3,4,8,256]{3,2,1,0:T(8,128)S(1)}, f32[3,4,8,256]{3,2,1,0:T(8,128)S(1)}, u32[]{:S(2)}, u32[]{:S(2)}) %collective-permute-start.8) | collective-permute-done | bytes 98336 | tf_op jit(solution)/shard_map/ppermute | solution.py:455
  46.9 1.1 collective-permute-done.11.refs_6_
  48.0 2.9 %shard_map.52 = (f32[3,4,32,8,256]{4,3,2,1,0:T(8,128)S(1)}, f32[3,4,8,256]{3,2,1,0:T(8,128)S(1)}, f32[3,4,8,256]{3,2,1,0:T(8,128)S(1)}, f32[3,4,2,32,128]{4,3,2,1,0:T(8,128)S(1)}, f32[3,4,2,32,128]{4,3,2,1,0:T(8,128)S(1)}) custom-call(s32[1]{0:T(128)} %bitcast.refs_0_.half_ref, f32[3,4,32,8,256]{4,3,2,1,0:T(8,128)S(1)} %get-tuple-element.70.refs_1_, ...), custom_call_target="tpu_custom_call" | custom-call | tf_op jit(solution)/shard_map/pallas_call | solution.py:180
  51.0 1.0 collective-permute-start.14
  51.9 1.3 collective-permute-start.15
  53.5 3.6 %collective-permute-start.13 = (f32[3,4,8,256]{3,2,1,0:T(8,128)S(1)}, f32[3,4,8,256]{3,2,1,0:T(8,128)S(1)}, u32[]{:S(2)}, u32[]{:S(2)}) collective-permute-start(f32[3,4,8,256]{3,2,1,0:T(8,128)S(1)} %get-tuple-element.78), channel_id=1, source_target_pairs={{0,24},{8,0},{16,8},{24,16},{1,25},{9,1},{17,9},{25,17},{2,26},{10... | collective-permute-start | bytes 294920 | tf_op jit(solution)/shard_map/ppermute | solution.py:455
  57.1 3.4 %collective-permute-done.12.refs_3_ = f32[3,4,8,256]{3,2,1,0:T(8,128)S(1)} collective-permute-done((f32[3,4,8,256]{3,2,1,0:T(8,128)S(1)}, f32[3,4,8,256]{3,2,1,0:T(8,128)S(1)}, u32[]{:S(2)}, u32[]{:S(2)}) %collective-permute-start.12) | collective-permute-done | bytes 98336 | tf_op jit(solution)/shard_map/ppermute | solution.py:455
  60.5 0.8 collective-permute-done.14.refs_5_
  61.7 0.7 shard_map.54
  62.9 1.1 copy-done.4
  64.1 1.5 %edges.3 = (f32[3,2,32,8,256]{4,3,2,1,0:T(8,128)S(1)}, f32[3,2,8,256]{3,2,1,0:T(8,128)S(1)}, f32[3,2,8,256]{3,2,1,0:T(8,128)S(1)}, f32[3,2,2,32,128]{4,3,2,1,0:T(8,128)S(1)}, f32[3,2,2,32,128]{4,3,2,1,0:T(8,128)S(1)}) custom-call(f32[3,2,32,8,256]{4,3,2,1,0:T(8,128)} %copy-done.4), custom_call_target="tpu_custom_call" | custom-call | tf_op jit(solution)/shard_map/edges/pallas_call | solution.py:247
  65.6 1.0 collective-permute-start.19
  66.5 0.8 collective-permute-start.20
  67.4 15.3 %collective-permute-done.33.other.refs_3_ = f32[3,2,16,8,256]{4,3,2,1,0:T(8,128)S(1)} collective-permute-done((f32[3,2,16,8,256]{4,3,2,1,0:T(8,128)S(1)}, f32[3,2,16,8,256]{4,3,2,1,0:T(8,128)S(1)}, u32[]{:S(2)}, u32[]{:S(2)}) %collective-permute-start.33) | collective-permute-done | bytes 786464 | tf_op jit(solution)/shard_map/ppermute | solution.py:480
  82.6 1.6 %collective-permute-start.17 = (f32[3,2,8,256]{3,2,1,0:T(8,128)S(1)}, f32[3,2,8,256]{3,2,1,0:T(8,128)S(1)}, u32[]{:S(2)}, u32[]{:S(2)}) collective-permute-start(f32[3,2,8,256]{3,2,1,0:T(8,128)S(1)} %get-tuple-element.87), channel_id=1, source_target_pairs={{0,8},{8,16},{16,24},{24,0},{1,9},{9,17},{17,25},{25,1},{2,10},{10... | collective-permute-start | bytes 147464 | tf_op jit(solution)/shard_map/ppermute | solution.py:455
  84.3 2.2 %collective-permute-start.18 = (f32[3,2,8,256]{3,2,1,0:T(8,128)S(1)}, f32[3,2,8,256]{3,2,1,0:T(8,128)S(1)}, u32[]{:S(2)}, u32[]{:S(2)}) collective-permute-start(f32[3,2,8,256]{3,2,1,0:T(8,128)S(1)} %get-tuple-element.88), channel_id=1, source_target_pairs={{0,24},{8,0},{16,8},{24,16},{1,25},{9,1},{17,9},{25,17},{2,26},{10... | collective-permute-start | bytes 147464 | tf_op jit(solution)/shard_map/ppermute | solution.py:455
  86.4 2.2 %collective-permute-done.17.refs_2_ = f32[3,2,8,256]{3,2,1,0:T(8,128)S(1)} collective-permute-done((f32[3,2,8,256]{3,2,1,0:T(8,128)S(1)}, f32[3,2,8,256]{3,2,1,0:T(8,128)S(1)}, u32[]{:S(2)}, u32[]{:S(2)}) %collective-permute-start.17) | collective-permute-done | bytes 49184 | tf_op jit(solution)/shard_map/ppermute | solution.py:455
  88.9 1.4 shard_map.55
  90.3 1.7 %collective-permute-start.24 = (f32[3,2,2,32,128]{4,3,2,1,0:T(8,128)S(1)}, f32[3,2,2,32,128]{4,3,2,1,0:T(8,128)S(1)}, u32[]{:S(2)}, u32[]{:S(2)}) collective-permute-start(f32[3,2,2,32,128]{4,3,2,1,0:T(8,128)S(1)} %get-tuple-element.95), channel_id=1, source_target_pairs={{0,6},{2,0},{4,2},{6,4},{1,7},{3,1},{5,3},{7,5},{8,14},{10,8},{12,... | collective-permute-start | bytes 589832 | tf_op jit(solution)/shard_map/ppermute | solution.py:455
  92.1 1.1 collective-permute-start.21
  93.1 2.8 %collective-permute-start.22 = (f32[3,2,8,256]{3,2,1,0:T(8,128)S(1)}, f32[3,2,8,256]{3,2,1,0:T(8,128)S(1)}, u32[]{:S(2)}, u32[]{:S(2)}) collective-permute-start(f32[3,2,8,256]{3,2,1,0:T(8,128)S(1)} %get-tuple-element.93), channel_id=1, source_target_pairs={{0,24},{8,0},{16,8},{24,16},{1,25},{9,1},{17,9},{25,17},{2,26},{10... | collective-permute-start | bytes 147464 | tf_op jit(solution)/shard_map/ppermute | solution.py:455
  95.9 2.1 %collective-permute-done.21.refs_3_ = f32[3,2,8,256]{3,2,1,0:T(8,128)S(1)} collective-permute-done((f32[3,2,8,256]{3,2,1,0:T(8,128)S(1)}, f32[3,2,8,256]{3,2,1,0:T(8,128)S(1)}, u32[]{:S(2)}, u32[]{:S(2)}) %collective-permute-start.21) | collective-permute-done | bytes 49184 | tf_op jit(solution)/shard_map/ppermute | solution.py:455
  98.1 3.0 %shard_map.56 = (f32[3,2,32,8,256]{4,3,2,1,0:T(8,128)S(1)}, f32[3,2,32,8,256]{4,3,2,1,0:T(8,128)S(1)}, f32[2,8,256]{2,1,0:T(8,128)}, f32[3,2,8,256]{3,2,1,0:T(8,...) custom-call(s32[1]{0:T(128)} %bitcast.refs_0_.half_ref, ...), custom_call_target="tpu_custom_call" | custom-call | tf_op jit(solution)/shard_map/pallas_call | solution.py:180
  101.0 1.7 %collective-permute-start.28 = (f32[3,2,2,32,128]{4,3,2,1,0:T(8,128)S(1)}, f32[3,2,2,32,128]{4,3,2,1,0:T(8,128)S(1)}, u32[]{:S(2)}, u32[]{:S(2)}) collective-permute-start(f32[3,2,2,32,128]{4,3,2,1,0:T(8,128)S(1)} %get-tuple-element.101), channel_id=1, source_target_pairs={{0,6},{2,0},{4,2},{6,4},{1,7},{3,1},{5,3},{7,5},{8,14},{10,8},{12,... | collective-permute-start | bytes 589832 | tf_op jit(solution)/shard_map/ppermute | solution.py:455
  102.8 1.0 collective-permute-start.25
  103.8 2.8 %collective-permute-start.26 = (f32[3,2,8,256]{3,2,1,0:T(8,128)S(1)}, f32[3,2,8,256]{3,2,1,0:T(8,128)S(1)}, u32[]{:S(2)}, u32[]{:S(2)}) collective-permute-start(f32[3,2,8,256]{3,2,1,0:T(8,128)S(1)} %get-tuple-element.99), channel_id=1, source_target_pairs={{0,24},{8,0},{16,8},{24,16},{1,25},{9,1},{17,9},{25,17},{2,26},{10... | collective-permute-start | bytes 147464 | tf_op jit(solution)/shard_map/ppermute | solution.py:455
  106.6 2.1 %collective-permute-done.25.refs_3_ = f32[3,2,8,256]{3,2,1,0:T(8,128)S(1)} collective-permute-done((f32[3,2,8,256]{3,2,1,0:T(8,128)S(1)}, f32[3,2,8,256]{3,2,1,0:T(8,128)S(1)}, u32[]{:S(2)}, u32[]{:S(2)}) %collective-permute-start.25) | collective-permute-done | bytes 49184 | tf_op jit(solution)/shard_map/ppermute | solution.py:455
  108.8 1.5 %shard_map.57 = (f32[3,2,32,8,256]{4,3,2,1,0:T(8,128)S(1)}, f32[3,2,8,256]{3,2,1,0:T(8,128)S(1)}, f32[3,2,8,256]{3,2,1,0:T(8,128)S(1)}, f32[3,2,2,32,128]{4,3,2,1,0:T(8,128)S(1)}, f32[3,2,2,32,128]{4,3,2,1,0:T(8,128)S(1)}) custom-call(s32[1]{0:T(128)} %bitcast.refs_0_.half_ref, f32[3,2,32,8,256]{4,3,2,1,0:T(8,128)S(1)} %get-tuple-element.96.refs_1_, ...), custom_call_target="tpu_custom_call" | custom-call | tf_op jit(solution)/shard_map/pallas_call | solution.py:180
  110.3 1.7 %collective-permute-start.32 = (f32[3,2,2,32,128]{4,3,2,1,0:T(8,128)S(1)}, f32[3,2,2,32,128]{4,3,2,1,0:T(8,128)S(1)}, u32[]{:S(2)}, u32[]{:S(2)}) collective-permute-start(f32[3,2,2,32,128]{4,3,2,1,0:T(8,128)S(1)} %get-tuple-element.106), channel_id=1, source_target_pairs={{0,6},{2,0},{4,2},{6,4},{1,7},{3,1},{5,3},{7,5},{8,14},{10,8},{12,... | collective-permute-start | bytes 589832 | tf_op jit(solution)/shard_map/ppermute | solution.py:455
  112.1 1.1 collective-permute-start.29
  113.2 2.7 %collective-permute-start.30 = (f32[3,2,8,256]{3,2,1,0:T(8,128)S(1)}, f32[3,2,8,256]{3,2,1,0:T(8,128)S(1)}, u32[]{:S(2)}, u32[]{:S(2)}) collective-permute-start(f32[3,2,8,256]{3,2,1,0:T(8,128)S(1)} %get-tuple-element.104), channel_id=1, source_target_pairs={{0,24},{8,0},{16,8},{24,16},{1,25},{9,1},{17,9},{25,17},{2,26},{10... | collective-permute-start | bytes 147464 | tf_op jit(solution)/shard_map/ppermute | solution.py:455
  116.6 1.8 %shard_map.59.base = f32[8,128]{1,0:T(8,128)S(1)} custom-call(s32[1]{0:T(128)} %bitcast.refs_0_.half_ref, f32[3,2,16,8,256]{4,3,2,1,0:T(8,128)S(1)} %get-tuple-element.81.front_keep.fk.refs_0_, f32[3,2,16,8,256]{4,3,2,1,0:T(8,128)S(1)} %get-tuple-element.82.front_send.fs.refs_0_, f32[3,2,16,8,256]{4,3,2,1,0:T(8,128)S(1)} %get-tuple-element.112.late_keep.lk.refs_1_, ...), custom_call_target="tpu_custom_call" | custom-call | tf_op jit(solution)/shard_map/pallas_call | solution.py:351
  119.1 2.6 %shard_map.60 = f32[8,128]{1,0:T(8,128)S(1)} custom-call(s32[1]{0:T(128)} %bitcast.refs_0_.half_ref, f32[3,2,16,8,256]{4,3,2,1,0:T(8,128)S(1)} %get-tuple-element.81.front_keep.fk.refs_0_, f32[3,2,16,8,256]{4,3,2,1,0:T(8,128)S(1)} %get-tuple-element.82.front_send.fs.refs_0_, f32[3,2,16,8,256]{4,3,2,1,0:T(8,128)S(1)} %get-tuple-element.112.late_keep.lk.refs_1_, ...), custom_call_target="tpu_custom_call" | custom-call | tf_op jit(solution)/shard_map/pallas_call | solution.py:351
  121.7 0.8 collective-permute-start.34
  122.5 2.9 %collective-permute-done.34 = f32[8,128]{1,0:T(8,128)S(1)} collective-permute-done((f32[8,128]{1,0:T(8,128)S(1)}, f32[8,128]{1,0:T(8,128)S(1)}, u32[]{:S(2)}, u32[]{:S(2)}) %collective-permute-start.34) | collective-permute-done | bytes 4128 | tf_op jit(solution)/shard_map/ppermute | solution.py:474
  125.4 2.0 %collective-permute-start.35 = (f32[8,128]{1,0:T(8,128)S(1)}, f32[8,128]{1,0:T(8,128)S(1)}, u32[]{:S(2)}, u32[]{:S(2)}) collective-permute-start(f32[8,128]{1,0:T(8,128)S(1)} %add.15), channel_id=1, source_target_pairs={{0,16},{8,24},{16,0},{24,8},{1,17},{9,25},{17,1},{25,9},{2,18},{10... | collective-permute-start | bytes 12296 | tf_op jit(solution)/shard_map/ppermute | solution.py:474
  127.4 2.5 %collective-permute-done.35 = f32[8,128]{1,0:T(8,128)S(1)} collective-permute-done((f32[8,128]{1,0:T(8,128)S(1)}, f32[8,128]{1,0:T(8,128)S(1)}, u32[]{:S(2)}, u32[]{:S(2)}) %collective-permute-start.35) | collective-permute-done | bytes 4128 | tf_op jit(solution)/shard_map/ppermute | solution.py:474
  129.9 1.2 collective-permute-done.36
  131.1 1.5 %collective-permute-start.37 = (f32[8,128]{1,0:T(8,128)S(1)}, f32[8,128]{1,0:T(8,128)S(1)}, u32[]{:S(2)}, u32[]{:S(2)}) collective-permute-start(f32[8,128]{1,0:T(8,128)S(1)} %add.17), channel_id=1, source_target_pairs={{0,4},{2,6},{4,0},{6,2},{1,5},{3,7},{5,1},{7,3},{8,12},{10,14},{12... | collective-permute-start | bytes 12296 | tf_op jit(solution)/shard_map/ppermute | solution.py:474
  132.6 2.1 %collective-permute-done.37 = f32[8,128]{1,0:T(8,128)S(1)} collective-permute-done((f32[8,128]{1,0:T(8,128)S(1)}, f32[8,128]{1,0:T(8,128)S(1)}, u32[]{:S(2)}, u32[]{:S(2)}) %collective-permute-start.37) | collective-permute-done | bytes 4128 | tf_op jit(solution)/shard_map/ppermute | solution.py:474
  134.7 1.8 %collective-permute-start.38 = (f32[8,128]{1,0:T(8,128)S(1)}, f32[8,128]{1,0:T(8,128)S(1)}, u32[]{:S(2)}, u32[]{:S(2)}) collective-permute-start(f32[8,128]{1,0:T(8,128)S(1)} %add.18), channel_id=1, source_target_pairs={{0,1},{1,0},{2,3},{3,2},{4,5},{5,4},{6,7},{7,6},{8,9},{9,8},{10,11... | collective-permute-start | bytes 12296 | tf_op jit(solution)/shard_map/ppermute | solution.py:474
  136.5 1.8 %collective-permute-done.38 = f32[8,128]{1,0:T(8,128)S(1)} collective-permute-done((f32[8,128]{1,0:T(8,128)S(1)}, f32[8,128]{1,0:T(8,128)S(1)}, u32[]{:S(2)}, u32[]{:S(2)}) %collective-permute-start.38) | collective-permute-done | bytes 4128 | tf_op jit(solution)/shard_map/ppermute | solution.py:474
  138.3 1.4 factor.1
  139.7 2.0 %basis.2.refs_4_ = f32[3,4,32,8,256]{4,3,2,1,0:T(8,128)} custom-call(s32[1]{0:T(128)} %bitcast.refs_0_.half_ref, f32[32,8,128]{2,1,0:T(8,128)S(1)} %get-tuple-element.111.coef, f32[3,2,16,8,256]{4,3,2,1,0:T(8,128)S(1)} %get-tuple-element.81.front_keep.fk.refs_0_, f32[3,2,16,8,256]{4,3,2,1,0:T(8,128)S(1)} %get-tuple-element.112.late_keep.lk.refs_1_, ...), custom_call_target="tpu_custom_call" | custom-call | tf_op jit(solution)/shard_map/basis/pallas_call | solution.py:441
  141.7 2.0 %basis.3 = f32[3,4,32,8,256]{4,3,2,1,0:T(8,128)} custom-call(s32[1]{0:T(128)} %bitcast.refs_0_.half_ref, f32[32,8,128]{2,1,0:T(8,128)S(1)} %get-tuple-element.111.coef, f32[3,2,16,8,256]{4,3,2,1,0:T(8,128)S(1)} %get-tuple-element.82.front_send.fs.refs_0_, ...), custom_call_target="tpu_custom_call", output_to_operand_aliasing={{}: (6, {})} | custom-call | tf_op jit(solution)/shard_map/basis/pallas_call | solution.py:441
  (48 shorter events, 5.9 us)
Async XLA Ops:
  0.6 10.9 %copy-start.1 = (f32[256]{0:T(256)S(1)}, f32[256]{0:T(256)}, u32[]{:S(2)}) copy-start(f32[256]{0:T(256)} %param.4) | copy-start | bytes 3076
  3.6 1.1 copy-start.2
  4.7 11.5 %collective-permute-start.2 = (f32[3,4,2,32,128]{4,3,2,1,0:T(8,128)}, f32[3,4,2,32,128]{4,3,2,1,0:T(8,128)S(1)}, u32[]{:S(2)}, u32[]{:S(2)}) collective-permute-start(f32[3,4,2,32,128]{4,3,2,1,0:T(8,128)} %get-tuple-element.61), channel_id=1, source_target_pairs={{0,2},{2,4},{4,6},{6,0},{1,3},{3,5},{5,7},{7,1},{8,10},{10,12},{12... | collective-permute-start | bytes 1179656 | tf_op jit(solution)/shard_map/ppermute | solution.py:455
  5.2 11.8 %collective-permute-start.3 = (f32[3,4,2,32,128]{4,3,2,1,0:T(8,128)}, f32[3,4,2,32,128]{4,3,2,1,0:T(8,128)}, u32[]{:S(2)}, u32[]{:S(2)}) collective-permute-start(f32[3,4,2,32,128]{4,3,2,1,0:T(8,128)} %get-tuple-element.62), channel_id=1, source_target_pairs={{0,6},{2,0},{4,2},{6,4},{1,7},{3,1},{5,3},{7,5},{8,14},{10,8},{12,... | collective-permute-start | bytes 1179656 | tf_op jit(solution)/shard_map/ppermute | solution.py:455
  7.1 8.2 %collective-permute-start = (f32[3,4,8,256]{3,2,1,0:T(8,128)}, f32[3,4,8,256]{3,2,1,0:T(8,128)}, u32[]{:S(2)}, u32[]{:S(2)}) collective-permute-start(f32[3,4,8,256]{3,2,1,0:T(8,128)} %get-tuple-element.59), channel_id=1, source_target_pairs={{0,8},{8,16},{16,24},{24,0},{1,9},{9,17},{17,25},{25,1},{2,10},{10... | collective-permute-start | bytes 294920 | tf_op jit(solution)/shard_map/ppermute | solution.py:455
  9.5 6.7 %collective-permute-start.1 = (f32[3,4,8,256]{3,2,1,0:T(8,128)}, f32[3,4,8,256]{3,2,1,0:T(8,128)}, u32[]{:S(2)}, u32[]{:S(2)}) collective-permute-start(f32[3,4,8,256]{3,2,1,0:T(8,128)} %get-tuple-element.60), channel_id=1, source_target_pairs={{0,24},{8,0},{16,8},{24,16},{1,25},{9,1},{17,9},{25,17},{2,26},{10... | collective-permute-start | bytes 294920 | tf_op jit(solution)/shard_map/ppermute | solution.py:455
  11.5 1.0 copy-start
  12.5 14.4 %copy-start.3 = (f32[3,2,32,8,256]{4,3,2,1,0:T(8,128)S(1)}, f32[3,2,32,8,256]{4,3,2,1,0:T(8,128)}, u32[]{:S(2)}) copy-start(f32[3,2,32,8,256]{4,3,2,1,0:T(8,128)} %copy-done.2) | copy-start | bytes 4718596
  20.8 10.2 %collective-permute-start.6 = (f32[3,4,2,32,128]{4,3,2,1,0:T(8,128)S(1)}, f32[3,4,2,32,128]{4,3,2,1,0:T(8,128)S(1)}, u32[]{:S(2)}, u32[]{:S(2)}) collective-permute-start(f32[3,4,2,32,128]{4,3,2,1,0:T(8,128)S(1)} %get-tuple-element.68), channel_id=1, source_target_pairs={{0,2},{2,4},{4,6},{6,0},{1,3},{3,5},{5,7},{7,1},{8,10},{10,12},{12... | collective-permute-start | bytes 1179656 | tf_op jit(solution)/shard_map/ppermute | solution.py:455
  21.0 11.2 %collective-permute-start.7 = (f32[3,4,2,32,128]{4,3,2,1,0:T(8,128)S(1)}, f32[3,4,2,32,128]{4,3,2,1,0:T(8,128)S(1)}, u32[]{:S(2)}, u32[]{:S(2)}) collective-permute-start(f32[3,4,2,32,128]{4,3,2,1,0:T(8,128)S(1)} %get-tuple-element.69), channel_id=1, source_target_pairs={{0,6},{2,0},{4,2},{6,4},{1,7},{3,1},{5,3},{7,5},{8,14},{10,8},{12,... | collective-permute-start | bytes 1179656 | tf_op jit(solution)/shard_map/ppermute | solution.py:455
  23.0 7.5 %collective-permute-start.4 = (f32[3,4,8,256]{3,2,1,0:T(8,128)S(1)}, f32[3,4,8,256]{3,2,1,0:T(8,128)S(1)}, u32[]{:S(2)}, u32[]{:S(2)}) collective-permute-start(f32[3,4,8,256]{3,2,1,0:T(8,128)S(1)} %get-tuple-element.66), channel_id=1, source_target_pairs={{0,8},{8,16},{16,24},{24,0},{1,9},{9,17},{17,25},{25,1},{2,10},{10... | collective-permute-start | bytes 294920 | tf_op jit(solution)/shard_map/ppermute | solution.py:455
  24.4 6.6 %collective-permute-start.5 = (f32[3,4,8,256]{3,2,1,0:T(8,128)S(1)}, f32[3,4,8,256]{3,2,1,0:T(8,128)S(1)}, u32[]{:S(2)}, u32[]{:S(2)}) collective-permute-start(f32[3,4,8,256]{3,2,1,0:T(8,128)S(1)} %get-tuple-element.67), channel_id=1, source_target_pairs={{0,24},{8,0},{16,8},{24,16},{1,25},{9,1},{17,9},{25,17},{2,26},{10... | collective-permute-start | bytes 294920 | tf_op jit(solution)/shard_map/ppermute | solution.py:455
  26.9 36.1 %collective-permute-start.16 = (f32[3,2,32,8,256]{4,3,2,1,0:T(8,128)S(1)}, f32[3,2,32,8,256]{4,3,2,1,0:T(8,128)S(1)}, u32[]{:S(2)}, u32[]{:S(2)}) collective-permute-start(f32[3,2,32,8,256]{4,3,2,1,0:T(8,128)S(1)} %copy-done.3), channel_id=1, source_target_pairs={{0,1},{1,0},{2,3},{3,2},{4,5},{5,4},{6,7},{7,6},{8,9},{9,8},{10,11... | collective-permute-start | bytes 4718600 | tf_op jit(solution)/shard_map/ppermute | solution.py:480
  36.9 10.0 %collective-permute-start.10 = (f32[3,4,2,32,128]{4,3,2,1,0:T(8,128)S(1)}, f32[3,4,2,32,128]{4,3,2,1,0:T(8,128)S(1)}, u32[]{:S(2)}, u32[]{:S(2)}) collective-permute-start(f32[3,4,2,32,128]{4,3,2,1,0:T(8,128)S(1)} %get-tuple-element.74), channel_id=1, source_target_pairs={{0,2},{2,4},{4,6},{6,0},{1,3},{3,5},{5,7},{7,1},{8,10},{10,12},{12... | collective-permute-start | bytes 1179656 | tf_op jit(solution)/shard_map/ppermute | solution.py:455
  37.5 10.5 %collective-permute-start.11 = (f32[3,4,2,32,128]{4,3,2,1,0:T(8,128)S(1)}, f32[3,4,2,32,128]{4,3,2,1,0:T(8,128)S(1)}, u32[]{:S(2)}, u32[]{:S(2)}) collective-permute-start(f32[3,4,2,32,128]{4,3,2,1,0:T(8,128)S(1)} %get-tuple-element.75), channel_id=1, source_target_pairs={{0,6},{2,0},{4,2},{6,4},{1,7},{3,1},{5,3},{7,5},{8,14},{10,8},{12,... | collective-permute-start | bytes 1179656 | tf_op jit(solution)/shard_map/ppermute | solution.py:455
  39.2 7.5 %collective-permute-start.8 = (f32[3,4,8,256]{3,2,1,0:T(8,128)S(1)}, f32[3,4,8,256]{3,2,1,0:T(8,128)S(1)}, u32[]{:S(2)}, u32[]{:S(2)}) collective-permute-start(f32[3,4,8,256]{3,2,1,0:T(8,128)S(1)} %get-tuple-element.72), channel_id=1, source_target_pairs={{0,8},{8,16},{16,24},{24,0},{1,9},{9,17},{17,25},{25,1},{2,10},{10... | collective-permute-start | bytes 294920 | tf_op jit(solution)/shard_map/ppermute | solution.py:455
  40.0 6.7 %collective-permute-start.9 = (f32[3,4,8,256]{3,2,1,0:T(8,128)S(1)}, f32[3,4,8,256]{3,2,1,0:T(8,128)S(1)}, u32[]{:S(2)}, u32[]{:S(2)}) collective-permute-start(f32[3,4,8,256]{3,2,1,0:T(8,128)S(1)} %get-tuple-element.73), channel_id=1, source_target_pairs={{0,24},{8,0},{16,8},{24,16},{1,25},{9,1},{17,9},{25,17},{2,26},{10... | collective-permute-start | bytes 294920 | tf_op jit(solution)/shard_map/ppermute | solution.py:455
  51.0 10.3 %collective-permute-start.14 = (f32[3,4,2,32,128]{4,3,2,1,0:T(8,128)S(1)}, f32[3,4,2,32,128]{4,3,2,1,0:T(8,128)S(1)}, u32[]{:S(2)}, u32[]{:S(2)}) collective-permute-start(f32[3,4,2,32,128]{4,3,2,1,0:T(8,128)S(1)} %get-tuple-element.79), channel_id=1, source_target_pairs={{0,2},{2,4},{4,6},{6,0},{1,3},{3,5},{5,7},{7,1},{8,10},{10,12},{12... | collective-permute-start | bytes 1179656 | tf_op jit(solution)/shard_map/ppermute | solution.py:455
  51.9 9.8 %collective-permute-start.15 = (f32[3,4,2,32,128]{4,3,2,1,0:T(8,128)S(1)}, f32[3,4,2,32,128]{4,3,2,1,0:T(8,128)S(1)}, u32[]{:S(2)}, u32[]{:S(2)}) collective-permute-start(f32[3,4,2,32,128]{4,3,2,1,0:T(8,128)S(1)} %get-tuple-element.80), channel_id=1, source_target_pairs={{0,6},{2,0},{4,2},{6,4},{1,7},{3,1},{5,3},{7,5},{8,14},{10,8},{12,... | collective-permute-start | bytes 1179656 | tf_op jit(solution)/shard_map/ppermute | solution.py:455
  53.3 7.2 %collective-permute-start.12 = (f32[3,4,8,256]{3,2,1,0:T(8,128)S(1)}, f32[3,4,8,256]{3,2,1,0:T(8,128)S(1)}, u32[]{:S(2)}, u32[]{:S(2)}) collective-permute-start(f32[3,4,8,256]{3,2,1,0:T(8,128)S(1)} %get-tuple-element.77), channel_id=1, source_target_pairs={{0,8},{8,16},{16,24},{24,0},{1,9},{9,17},{17,25},{25,1},{2,10},{10... | collective-permute-start | bytes 294920 | tf_op jit(solution)/shard_map/ppermute | solution.py:455
  53.5 7.0 %collective-permute-start.13 = (f32[3,4,8,256]{3,2,1,0:T(8,128)S(1)}, f32[3,4,8,256]{3,2,1,0:T(8,128)S(1)}, u32[]{:S(2)}, u32[]{:S(2)}) collective-permute-start(f32[3,4,8,256]{3,2,1,0:T(8,128)S(1)} %get-tuple-element.78), channel_id=1, source_target_pairs={{0,24},{8,0},{16,8},{24,16},{1,25},{9,1},{17,9},{25,17},{2,26},{10... | collective-permute-start | bytes 294920 | tf_op jit(solution)/shard_map/ppermute | solution.py:455
  62.5 20.2 %collective-permute-start.33 = (f32[3,2,16,8,256]{4,3,2,1,0:T(8,128)S(1)}, f32[3,2,16,8,256]{4,3,2,1,0:T(8,128)S(1)}, u32[]{:S(2)}, u32[]{:S(2)}) collective-permute-start(f32[3,2,16,8,256]{4,3,2,1,0:T(8,128)S(1)} %get-tuple-element.84.late_send.ls.refs_1_), channel_id=1, source_target_pairs={{0,1},{1,0},{2,3},{3,2},{4,5},{5,4},{6,7},{7,6},{8,9},{9,8},{10,11... | collective-permute-start | bytes 2359304 | tf_op jit(solution)/shard_map/ppermute | solution.py:480
  62.9 1.1 copy-start.4
  65.6 23.3 %collective-permute-start.19 = (f32[3,2,2,32,128]{4,3,2,1,0:T(8,128)S(1)}, f32[3,2,2,32,128]{4,3,2,1,0:T(8,128)S(1)}, u32[]{:S(2)}, u32[]{:S(2)}) collective-permute-start(f32[3,2,2,32,128]{4,3,2,1,0:T(8,128)S(1)} %get-tuple-element.89), channel_id=1, source_target_pairs={{0,2},{2,4},{4,6},{6,0},{1,3},{3,5},{5,7},{7,1},{8,10},{10,12},{12... | collective-permute-start | bytes 589832 | tf_op jit(solution)/shard_map/ppermute | solution.py:455
  66.5 22.4 %collective-permute-start.20 = (f32[3,2,2,32,128]{4,3,2,1,0:T(8,128)S(1)}, f32[3,2,2,32,128]{4,3,2,1,0:T(8,128)S(1)}, u32[]{:S(2)}, u32[]{:S(2)}) collective-permute-start(f32[3,2,2,32,128]{4,3,2,1,0:T(8,128)S(1)} %get-tuple-element.90), channel_id=1, source_target_pairs={{0,6},{2,0},{4,2},{6,4},{1,7},{3,1},{5,3},{7,5},{8,14},{10,8},{12,... | collective-permute-start | bytes 589832 | tf_op jit(solution)/shard_map/ppermute | solution.py:455
  82.6 59.1 %collective-permute-start.39 = (f32[3,2,16,8,256]{4,3,2,1,0:T(8,128)S(1)}, f32[3,2,16,8,256]{4,3,2,1,0:T(8,128)S(1)}, u32[]{:S(2)}, u32[]{:S(2)}) collective-permute-start(f32[3,2,16,8,256]{4,3,2,1,0:T(8,128)S(1)} %get-tuple-element.112.late_keep.lk.refs_1_), channel_id=1, source_target_pairs={{0,1},{1,0},{2,3},{3,2},{4,5},{5,4},{6,7},{7,6},{8,9},{9,8},{10,11... | collective-permute-start | bytes 2359304 | tf_op jit(solution)/shard_map/ppermute | solution.py:480
  82.6 6.0 %collective-permute-start.17 = (f32[3,2,8,256]{3,2,1,0:T(8,128)S(1)}, f32[3,2,8,256]{3,2,1,0:T(8,128)S(1)}, u32[]{:S(2)}, u32[]{:S(2)}) collective-permute-start(f32[3,2,8,256]{3,2,1,0:T(8,128)S(1)} %get-tuple-element.87), channel_id=1, source_target_pairs={{0,8},{8,16},{16,24},{24,0},{1,9},{9,17},{17,25},{25,1},{2,10},{10... | collective-permute-start | bytes 147464 | tf_op jit(solution)/shard_map/ppermute | solution.py:455
  84.3 4.6 %collective-permute-start.18 = (f32[3,2,8,256]{3,2,1,0:T(8,128)S(1)}, f32[3,2,8,256]{3,2,1,0:T(8,128)S(1)}, u32[]{:S(2)}, u32[]{:S(2)}) collective-permute-start(f32[3,2,8,256]{3,2,1,0:T(8,128)S(1)} %get-tuple-element.88), channel_id=1, source_target_pairs={{0,24},{8,0},{16,8},{24,16},{1,25},{9,1},{17,9},{25,17},{2,26},{10... | collective-permute-start | bytes 147464 | tf_op jit(solution)/shard_map/ppermute | solution.py:455
  90.3 7.8 %collective-permute-start.23 = (f32[3,2,2,32,128]{4,3,2,1,0:T(8,128)S(1)}, f32[3,2,2,32,128]{4,3,2,1,0:T(8,128)S(1)}, u32[]{:S(2)}, u32[]{:S(2)}) collective-permute-start(f32[3,2,2,32,128]{4,3,2,1,0:T(8,128)S(1)} %get-tuple-element.94), channel_id=1, source_target_pairs={{0,2},{2,4},{4,6},{6,0},{1,3},{3,5},{5,7},{7,1},{8,10},{10,12},{12... | collective-permute-start | bytes 589832 | tf_op jit(solution)/shard_map/ppermute | solution.py:455
  90.3 7.7 %collective-permute-start.24 = (f32[3,2,2,32,128]{4,3,2,1,0:T(8,128)S(1)}, f32[3,2,2,32,128]{4,3,2,1,0:T(8,128)S(1)}, u32[]{:S(2)}, u32[]{:S(2)}) collective-permute-start(f32[3,2,2,32,128]{4,3,2,1,0:T(8,128)S(1)} %get-tuple-element.95), channel_id=1, source_target_pairs={{0,6},{2,0},{4,2},{6,4},{1,7},{3,1},{5,3},{7,5},{8,14},{10,8},{12,... | collective-permute-start | bytes 589832 | tf_op jit(solution)/shard_map/ppermute | solution.py:455
  92.1 6.0 %collective-permute-start.21 = (f32[3,2,8,256]{3,2,1,0:T(8,128)S(1)}, f32[3,2,8,256]{3,2,1,0:T(8,128)S(1)}, u32[]{:S(2)}, u32[]{:S(2)}) collective-permute-start(f32[3,2,8,256]{3,2,1,0:T(8,128)S(1)} %get-tuple-element.92), channel_id=1, source_target_pairs={{0,8},{8,16},{16,24},{24,0},{1,9},{9,17},{17,25},{25,1},{2,10},{10... | collective-permute-start | bytes 147464 | tf_op jit(solution)/shard_map/ppermute | solution.py:455
  93.1 4.9 %collective-permute-start.22 = (f32[3,2,8,256]{3,2,1,0:T(8,128)S(1)}, f32[3,2,8,256]{3,2,1,0:T(8,128)S(1)}, u32[]{:S(2)}, u32[]{:S(2)}) collective-permute-start(f32[3,2,8,256]{3,2,1,0:T(8,128)S(1)} %get-tuple-element.93), channel_id=1, source_target_pairs={{0,24},{8,0},{16,8},{24,16},{1,25},{9,1},{17,9},{25,17},{2,26},{10... | collective-permute-start | bytes 147464 | tf_op jit(solution)/shard_map/ppermute | solution.py:455
  101.0 7.8 %collective-permute-start.27 = (f32[3,2,2,32,128]{4,3,2,1,0:T(8,128)S(1)}, f32[3,2,2,32,128]{4,3,2,1,0:T(8,128)S(1)}, u32[]{:S(2)}, u32[]{:S(2)}) collective-permute-start(f32[3,2,2,32,128]{4,3,2,1,0:T(8,128)S(1)} %get-tuple-element.100), channel_id=1, source_target_pairs={{0,2},{2,4},{4,6},{6,0},{1,3},{3,5},{5,7},{7,1},{8,10},{10,12},{12... | collective-permute-start | bytes 589832 | tf_op jit(solution)/shard_map/ppermute | solution.py:455
  101.0 7.8 %collective-permute-start.28 = (f32[3,2,2,32,128]{4,3,2,1,0:T(8,128)S(1)}, f32[3,2,2,32,128]{4,3,2,1,0:T(8,128)S(1)}, u32[]{:S(2)}, u32[]{:S(2)}) collective-permute-start(f32[3,2,2,32,128]{4,3,2,1,0:T(8,128)S(1)} %get-tuple-element.101), channel_id=1, source_target_pairs={{0,6},{2,0},{4,2},{6,4},{1,7},{3,1},{5,3},{7,5},{8,14},{10,8},{12,... | collective-permute-start | bytes 589832 | tf_op jit(solution)/shard_map/ppermute | solution.py:455
  102.8 5.9 %collective-permute-start.25 = (f32[3,2,8,256]{3,2,1,0:T(8,128)S(1)}, f32[3,2,8,256]{3,2,1,0:T(8,128)S(1)}, u32[]{:S(2)}, u32[]{:S(2)}) collective-permute-start(f32[3,2,8,256]{3,2,1,0:T(8,128)S(1)} %get-tuple-element.98), channel_id=1, source_target_pairs={{0,8},{8,16},{16,24},{24,0},{1,9},{9,17},{17,25},{25,1},{2,10},{10... | collective-permute-start | bytes 147464 | tf_op jit(solution)/shard_map/ppermute | solution.py:455
  103.8 5.0 %collective-permute-start.26 = (f32[3,2,8,256]{3,2,1,0:T(8,128)S(1)}, f32[3,2,8,256]{3,2,1,0:T(8,128)S(1)}, u32[]{:S(2)}, u32[]{:S(2)}) collective-permute-start(f32[3,2,8,256]{3,2,1,0:T(8,128)S(1)} %get-tuple-element.99), channel_id=1, source_target_pairs={{0,24},{8,0},{16,8},{24,16},{1,25},{9,1},{17,9},{25,17},{2,26},{10... | collective-permute-start | bytes 147464 | tf_op jit(solution)/shard_map/ppermute | solution.py:455
  110.3 8.1 %collective-permute-start.31 = (f32[3,2,2,32,128]{4,3,2,1,0:T(8,128)S(1)}, f32[3,2,2,32,128]{4,3,2,1,0:T(8,128)S(1)}, u32[]{:S(2)}, u32[]{:S(2)}) collective-permute-start(f32[3,2,2,32,128]{4,3,2,1,0:T(8,128)S(1)} %get-tuple-element.105), channel_id=1, source_target_pairs={{0,2},{2,4},{4,6},{6,0},{1,3},{3,5},{5,7},{7,1},{8,10},{10,12},{12... | collective-permute-start | bytes 589832 | tf_op jit(solution)/shard_map/ppermute | solution.py:455
  110.3 8.1 %collective-permute-start.32 = (f32[3,2,2,32,128]{4,3,2,1,0:T(8,128)S(1)}, f32[3,2,2,32,128]{4,3,2,1,0:T(8,128)S(1)}, u32[]{:S(2)}, u32[]{:S(2)}) collective-permute-start(f32[3,2,2,32,128]{4,3,2,1,0:T(8,128)S(1)} %get-tuple-element.106), channel_id=1, source_target_pairs={{0,6},{2,0},{4,2},{6,4},{1,7},{3,1},{5,3},{7,5},{8,14},{10,8},{12,... | collective-permute-start | bytes 589832 | tf_op jit(solution)/shard_map/ppermute | solution.py:455
  112.1 6.3 %collective-permute-start.29 = (f32[3,2,8,256]{3,2,1,0:T(8,128)S(1)}, f32[3,2,8,256]{3,2,1,0:T(8,128)S(1)}, u32[]{:S(2)}, u32[]{:S(2)}) collective-permute-start(f32[3,2,8,256]{3,2,1,0:T(8,128)S(1)} %get-tuple-element.103), channel_id=1, source_target_pairs={{0,8},{8,16},{16,24},{24,0},{1,9},{9,17},{17,25},{25,1},{2,10},{10... | collective-permute-start | bytes 147464 | tf_op jit(solution)/shard_map/ppermute | solution.py:455
  113.2 5.2 %collective-permute-start.30 = (f32[3,2,8,256]{3,2,1,0:T(8,128)S(1)}, f32[3,2,8,256]{3,2,1,0:T(8,128)S(1)}, u32[]{:S(2)}, u32[]{:S(2)}) collective-permute-start(f32[3,2,8,256]{3,2,1,0:T(8,128)S(1)} %get-tuple-element.104), channel_id=1, source_target_pairs={{0,24},{8,0},{16,8},{24,16},{1,25},{9,1},{17,9},{25,17},{2,26},{10... | collective-permute-start | bytes 147464 | tf_op jit(solution)/shard_map/ppermute | solution.py:455
  121.7 3.7 %collective-permute-start.34 = (f32[8,128]{1,0:T(8,128)S(1)}, f32[8,128]{1,0:T(8,128)S(1)}, u32[]{:S(2)}, u32[]{:S(2)}) collective-permute-start(f32[8,128]{1,0:T(8,128)S(1)} %shard_map.60), channel_id=1, source_target_pairs={{0,8},{8,0},{16,24},{24,16},{1,9},{9,1},{17,25},{25,17},{2,10},{10... | collective-permute-start | bytes 12296 | tf_op jit(solution)/shard_map/ppermute | solution.py:474
  125.4 4.5 %collective-permute-start.35 = (f32[8,128]{1,0:T(8,128)S(1)}, f32[8,128]{1,0:T(8,128)S(1)}, u32[]{:S(2)}, u32[]{:S(2)}) collective-permute-start(f32[8,128]{1,0:T(8,128)S(1)} %add.15), channel_id=1, source_target_pairs={{0,16},{8,24},{16,0},{24,8},{1,17},{9,25},{17,1},{25,9},{2,18},{10... | collective-permute-start | bytes 12296 | tf_op jit(solution)/shard_map/ppermute | solution.py:474
  129.9 1.2 collective-permute-start.36
  131.1 3.6 %collective-permute-start.37 = (f32[8,128]{1,0:T(8,128)S(1)}, f32[8,128]{1,0:T(8,128)S(1)}, u32[]{:S(2)}, u32[]{:S(2)}) collective-permute-start(f32[8,128]{1,0:T(8,128)S(1)} %add.17), channel_id=1, source_target_pairs={{0,4},{2,6},{4,0},{6,2},{1,5},{3,7},{5,1},{7,3},{8,12},{10,14},{12... | collective-permute-start | bytes 12296 | tf_op jit(solution)/shard_map/ppermute | solution.py:474
  134.7 3.6 %collective-permute-start.38 = (f32[8,128]{1,0:T(8,128)S(1)}, f32[8,128]{1,0:T(8,128)S(1)}, u32[]{:S(2)}, u32[]{:S(2)}) collective-permute-start(f32[8,128]{1,0:T(8,128)S(1)} %add.18), channel_id=1, source_target_pairs={{0,1},{1,0},{2,3},{3,2},{4,5},{5,4},{6,7},{7,6},{8,9},{9,8},{10,11... | collective-permute-start | bytes 12296 | tf_op jit(solution)/shard_map/ppermute | solution.py:474

commit v3 on v2

--- a/solution.py
+++ b/solution.py
@@ -53,38 +53,50 @@
     return value
 
 
-def put_faces(result, comp, lanes_ref, first_x, last_x, first_z, last_z):
+def put_faces(result, comp, lanes_ref, faces, nz):
+    first_z, last_z, *x_faces = faces
     size = result.shape[0]
-    nx, nz = first_z.shape[3], first_x.shape[2]
-    first_x[comp, 0] = result[:nz]
-    last_x[comp, 0] = result[size - nz :]
+    nx = size // nz
+    if x_faces:
+        x_faces[0][comp, 0] = result[:nz]
+        x_faces[1][comp, 0] = result[size - nz :]
     for h in range(lanes_ref.shape[0]):
         lanes_ref[h] = result[:, h * 128 : (h + 1) * 128]
         first_z[comp, 0, h] = lanes_ref[h, pl.ds(0, nx, stride=nz), :]
         last_z[comp, 0, h] = lanes_ref[h, pl.ds(nz - 1, nx, stride=nz), :]
 
 
-def stage_body(kind, span, *refs):
-    half_ref, *refs = refs
+def stage_body(kind, span, guest, relayed, *refs):
+    if kind == "adjoint_last":
+        half_ref, *refs = refs
     src = None
     if kind == "forward_first":
         cur, *refs = refs
     else:
         cur, src, *refs = refs
-    xlo, xhi, zlo, zhi, coef, wall, *rest = refs
+    if guest:
+        both, *refs = refs
+        xlo, xhi = both.at[0], both.at[1]
+    else:
+        xlo, xhi, *refs = refs
+    zlo, zhi, coef, wall, *rest = refs
+    if relayed:
+        relay, *rest = rest
+        relay[0] = xlo[:, : relay.shape[2]]
+        relay[1] = xhi[:, : relay.shape[2]]
 
     def one(j, _):
         view = lambda ref: ref.at[:, pl.ds(j, 1)]
         fields = [view(cur), None if src is None else view(src), view(xlo), view(xhi), view(zlo), view(zhi), coef, wall]
         if kind == "adjoint_last":
             last_column(half_ref, *fields[:7], *[r.at[:, pl.ds(j - span[0], 1)] for r in rest])
-        elif kind == "forward_last":
-            out, solved, squares, *more = rest
-            faces, work = more[:4], more[4:]
-            outs = [view(out), view(solved), squares.at[pl.ds(j, 1)]] + [view(r) for r in faces]
-            stage_column(kind, *fields, outs, *work)
         else:
-            stage_column(kind, *fields, [view(r) for r in rest[:5]], *rest[5:])
+            *outs, high, low, lanes = rest
+            squares = None
+            if len(outs[-1].shape) == 3:
+                *outs, squares = outs
+                squares = squares.at[pl.ds(j, 1)]
+            stage_column(kind, *fields, [view(r) for r in outs], squares, high, low, lanes)
         return 0
 
     lax.fori_loop(span[0], span[1], one, 0)
@@ -111,7 +123,7 @@
                 target[comp, 0, spot : spot + X_CHUNK] = value + src[comp, 0, pl.ds(x0, X_CHUNK)]
 
 
-def stage_column(kind, cur, src, xlo, xhi, zlo, zhi, coef, wall, outs, high, low, lanes):
+def stage_column(kind, cur, src, xlo, xhi, zlo, zhi, coef, wall, outs, squares, high, low, lanes):
     nx, nz, ny = cur.shape[2:]
     adjoint = kind.startswith("adjoint")
     center = 1.0 / (step_length * viscosity) - 4.0
@@ -119,6 +131,7 @@
         center = center + 1.0 / viscosity
     size = nx * nz
     total = None
+    faces = outs[2:] if kind == "forward_last" else outs[1:]
     for comp in range(3):
         for x0 in range(0, nx, X_CHUNK):
             west = xlo[comp, 0] if x0 == 0 else cur[comp, 0, x0 - 1]
@@ -135,9 +148,10 @@
         part = slice(comp * size, (comp + 1) * size)
         result = wall_product(high[part], low[part], wall.at[pl.ds(2, 2)] if adjoint else wall.at[pl.ds(0, 2)])
         if kind == "forward_last":
-            tile = result.reshape(nx, nz, ny)
-            sums = jnp.sum(tile * tile, axis=0)
-            total = sums if total is None else total + sums
+            if squares is not None:
+                tile = result.reshape(nx, nz, ny)
+                sums = jnp.sum(tile * tile, axis=0)
+                total = sums if total is None else total + sums
             scaled = result * (1.0 / viscosity)
             outs[0][comp, 0] = scaled.reshape(nx, nz, ny)
             h, l = split_halves(scaled)
@@ -145,9 +159,9 @@
             outs[1][comp, 0] = result.reshape(nx, nz, ny)
         else:
             outs[0][comp, 0] = result.reshape(nx, nz, ny)
-        put_faces(result, comp, lanes, *outs[-4:])
-    if kind == "forward_last":
-        outs[2][0] = total
+        put_faces(result, comp, lanes, faces, nz)
+    if total is not None:
+        squares[0] = total
 
 
 def in_vmem(shape):
@@ -158,29 +172,34 @@
     return pltpu.with_memory_space_constraint(value, pltpu.VMEM)
 
 
-def run_stage(kind, half, cur, src, faces, coef, wall, span=None):
+def run_stage(kind, half, cur, src, faces, coef, wall, span=None, squares=False, relay=0):
     three, columns, nx, nz, ny = cur.shape
     span = span or (0, columns)
+    guest = len(faces) == 3
     field = in_vmem(cur.shape)
     half_field = in_vmem((three, span[1] - span[0], nx // 2, nz, ny))
     x_out = in_vmem((three, columns, nz, ny))
     z_out = in_vmem((three, columns, ny // 128, nx, 128))
-    face_outs = [x_out, x_out, z_out, z_out]
+    face_outs = [z_out, z_out] + ([] if guest else [x_out, x_out])
     scratch = [pltpu.VMEM((three * nx * nz, ny), jnp.bfloat16)] * 2
     scratch += [pltpu.VMEM((ny // 128, nx * nz, 128), jnp.float32)]
+    outs = [in_vmem((2, three, relay, nz, ny))] if relay else []
     if kind == "forward_last":
-        outs = [field, field, in_vmem((columns, nz, ny))] + face_outs
+        outs += [field, field] + face_outs + [in_vmem((columns, nz, ny))] * squares
     elif kind == "adjoint_last":
-        outs, scratch = [half_field, half_field], []
+        outs, scratch = outs + [half_field, half_field], []
     else:
-        outs = [field] + face_outs
+        outs += [field] + face_outs
     fields = (cur,) if src is None else (cur, src)
-    operands = [half] + [hold(v) for v in (*fields, *faces, coef, wall)]
+    operands = [hold(v) for v in (*fields, *faces[2:], *faces[:2], coef, wall)]
     vmem = pl.BlockSpec(memory_space=pltpu.VMEM)
-    return pl.pallas_call(
-        functools.partial(stage_body, kind, span),
+    in_specs = [vmem] * len(operands)
+    if kind == "adjoint_last":
+        operands, in_specs = [half] + operands, [pl.BlockSpec(memory_space=pltpu.SMEM)] + in_specs
+    return pl.pallas_call(
+        functools.partial(stage_body, kind, span, guest, bool(relay)),
         out_shape=outs,
-        in_specs=[pl.BlockSpec(memory_space=pltpu.SMEM)] + [vmem] * (len(operands) - 1),
+        in_specs=in_specs,
         out_specs=[vmem] * len(outs),
         scratch_shapes=scratch,
         compiler_params=pltpu.CompilerParams(vmem_limit_bytes=VMEM_LIMIT),
@@ -216,9 +235,7 @@
     )(wall_solve, velocity.reshape(1, ny))
 
 
-def edges_body(source, *refs):
-    *outs, lanes, sems = refs
-    field, first_x, last_x, first_z, last_z = outs[:5]
+def edges_body(source, half_ref, field, front, first_z, last_z, first_x, last_x, lanes, sems):
     three, columns, nx, nz, ny = field.shape
 
     def fetch(j):
@@ -226,33 +243,53 @@
 
     for j in range(columns):
         fetch(j).start()
+    ahead = pltpu.make_async_copy(source.at[:, pl.ds(0, front.shape[1])], front, sems.at[columns])
+    ahead.start()
     for j in range(columns):
         fetch(j).wait()
-        view = lambda ref: ref.at[:, pl.ds(j, 1)]
+        faces = [ref.at[:, pl.ds(j, 1)] for ref in (first_z, last_z, first_x, last_x)]
         for comp in range(three):
-            tile = field[comp, j].reshape(nx * nz, ny)
-            put_faces(tile, comp, lanes, view(first_x), view(last_x), view(first_z), view(last_z))
-            if len(outs) > 5 and j < outs[5].shape[1]:
-                outs[5][comp, j] = field[comp, j]
-
-
-def run_edges(source, front=None):
+            put_faces(field[comp, j].reshape(nx * nz, ny), comp, lanes, faces, nz)
+    ahead.wait()
+
+
+def run_edges(source, half, front):
     three, columns, nx, nz, ny = source.shape
     x_out = in_vmem((three, columns, nz, ny))
     z_out = in_vmem((three, columns, ny // 128, nx, 128))
-    outs = [in_vmem(source.shape), x_out, x_out, z_out, z_out]
-    if front is not None:
-        outs += [in_vmem((three, front, nx, nz, ny))]
-    vmem = pl.BlockSpec(memory_space=pltpu.VMEM)
+    outs = [in_vmem(source.shape), in_vmem((three, front, nx, nz, ny)), z_out, z_out, x_out, x_out]
     return pl.pallas_call(
         edges_body,
         out_shape=outs,
-        in_specs=[pl.BlockSpec(memory_space=pltpu.HBM)],
-        out_specs=[vmem] * len(outs),
-        scratch_shapes=[pltpu.VMEM((ny // 128, nx * nz, 128), jnp.float32), pltpu.SemaphoreType.DMA((columns,))],
+        in_specs=[pl.BlockSpec(memory_space=pltpu.HBM), pl.BlockSpec(memory_space=pltpu.SMEM)],
+        out_specs=[pl.BlockSpec(memory_space=pltpu.VMEM)] * len(outs),
+        scratch_shapes=[pltpu.VMEM((ny // 128, nx * nz, 128), jnp.float32), pltpu.SemaphoreType.DMA((columns + 1,))],
         compiler_params=pltpu.CompilerParams(vmem_limit_bytes=VMEM_LIMIT),
         name="edges",
-    )(pltpu.with_memory_space_constraint(source, pltpu.HBM))
+    )(pltpu.with_memory_space_constraint(source, pltpu.HBM), half)
+
+
+def guest_edges_body(field, first_z, last_z, lanes):
+    three, columns, nx, nz, ny = field.shape
+    for j in range(columns):
+        faces = [ref.at[:, pl.ds(j, 1)] for ref in (first_z, last_z)]
+        for comp in range(three):
+            put_faces(field[comp, j].reshape(nx * nz, ny), comp, lanes, faces, nz)
+
+
+def run_guest_edges(field):
+    three, columns, nx, nz, ny = field.shape
+    z_out = in_vmem((three, columns, ny // 128, nx, 128))
+    vmem = pl.BlockSpec(memory_space=pltpu.VMEM)
+    return pl.pallas_call(
+        guest_edges_body,
+        out_shape=[z_out, z_out],
+        in_specs=[vmem],
+        out_specs=[vmem] * 2,
+        scratch_shapes=[pltpu.VMEM((ny // 128, nx * nz, 128), jnp.float32)],
+        compiler_params=pltpu.CompilerParams(vmem_limit_bytes=VMEM_LIMIT),
+        name="guest_edges",
+    )(hold(field))
 
 
 def rows_to_matrix(sums, table, count, columns):
@@ -278,17 +315,18 @@
 
 def pair_sums(fields, pairs, acc, nx, three, ny):
     used = sorted({i for pair in pairs for i in pair})
-    for lane in range(0, ny, 128):
-
-        def body(k, carry):
-            comp = k // nx
-            x = k - comp * nx
-            cols = {i: fields[i][0][comp, fields[i][1], x, :, lane : lane + 128] for i in used}
-            return tuple(c + cols[i] * cols[j] for c, (i, j) in zip(carry, pairs))
-
-        done = lax.fori_loop(0, three * nx, body, tuple(acc[p] for p in range(len(pairs))), unroll=4)
-        for p in range(len(pairs)):
-            acc[p] = done[p]
+    total = tuple(acc[p] for p in range(len(pairs)))
+    for comp in range(three):
+
+        def body(x, carry):
+            for lane in range(0, ny, 128):
+                cols = {i: fields[i][0][comp, fields[i][1], x, :, lane : lane + 128] for i in used}
+                carry = tuple(c + cols[i] * cols[j] for c, (i, j) in zip(carry, pairs))
+            return carry
+
+        total = lax.fori_loop(0, nx, body, total, unroll=4)
+    for p in range(len(pairs)):
+        acc[p] = total[p]
 
 
 def gram_tables(sums, acc, pairs):
@@ -409,20 +447,20 @@
     base = pl.program_id(0) * nx
     spots = [(ref, i) for ref in fields for i in range(ref.shape[1])]
 
-    def body(k, _):
-        comp = k // nx
-        x = k - comp * nx
-        for lane in range(0, ny, 128):
-            part = slice(lane, lane + 128)
-            cols = [ref[comp, i, base + x, :, part] for ref, i in spots]
-            for j in range(columns):
-                terms = [coef[j * count + i] * cols[i] for i in range(count)]
-                while len(terms) > 1:
-                    terms = [a + b for a, b in zip(terms[::2], terms[1::2])]
-                out[comp, j, x, :, part] = terms[0]
-        return 0
-
-    lax.fori_loop(0, three * nx, body, 0, unroll=2)
+    for comp in range(three):
+
+        def body(x, _):
+            for lane in range(0, ny, 128):
+                part = slice(lane, lane + 128)
+                cols = [ref[comp, i, base + x, :, part] for ref, i in spots]
+                for j in range(columns):
+                    terms = [coef[j * count + i] * cols[i] for i in range(count)]
+                    while len(terms) > 1:
+                        terms = [a + b for a, b in zip(terms[::2], terms[1::2])]
+                    out[comp, j, x, :, part] = terms[0]
+            return 0
+
+        lax.fori_loop(0, nx, body, 0, unroll=4)
 
 
 def run_basis(half, coef, fields, columns, keep, target=None):
@@ -455,15 +493,21 @@
     return lax.ppermute(value, axis, [(i, (i + amount) % count) for i in range(count)])
 
 
-def exchange(first_x, last_x, first_z, last_z):
+def exchange(first_z, last_z, first_x=None, last_x=None):
     zlo = shift(last_z, "gz", 1)
     zhi = shift(first_z, "gz", -1)
+    if first_x is None:
+        return zlo, zhi
     xlo = shift(last_x, "gx", 1)
     xhi = shift(first_x, "gx", -1)
-    return xlo, xhi, zlo, zhi
-
-
-def all_sum(value, axes):
+    return zlo, zhi, xlo, xhi
+
+
+def partner(value, axis, count, mask):
+    return lax.ppermute(value, axis, [(i, i ^ mask) for i in range(count)])
+
+
+def all_sum(value, axes, wide):
     for axis in axes:
         count = lax.axis_size(axis)
         if count & (count - 1):
@@ -471,8 +515,13 @@
             continue
         mask = 1
         while mask < count:
-            value = value + lax.ppermute(value, axis, [(i, i ^ mask) for i in range(count)])
-            mask *= 2
+            if wide == axis and 4 * mask <= count:
+                near, far, both = (partner(value, axis, count, k * mask) for k in (1, 2, 3))
+                value = (value + near) + (far + both)
+                mask *= 4
+            else:
+                value = value + partner(value, axis, count, mask)
+                mask *= 2
     return value
 
 
@@ -486,33 +535,37 @@
     half = lax.axis_index("sa").astype(jnp.int32).reshape(1)
     early = columns // 2
     count = 2 * columns
-    forcing, *edge, front = run_edges(forcing, early)
+    forcing, front, *edge = run_edges(forcing, half, early)
     guest = swap(front)
     faces = exchange(*edge)
     coef, wall = run_setup(wall_solve, velocity, nz)
 
-    def stage(kind, *args):
-        return run_stage(kind, half, *args)
-
-    q1, *edge = stage("forward_first", forcing, None, faces, coef, wall)
-    faces = exchange(*edge)
-    q2, s1, squares, *edge = stage("forward_last", q1, forcing, faces, coef, wall)
-    faces = exchange(*edge)
-    s2, *edge = stage("adjoint_first", s1, q2, faces, coef, wall)
-    faces = exchange(*edge)
-    late_keep, late_send = stage("adjoint_last", s2, q2, faces, coef, wall, (early, columns))
+    def stage(kind, *args, **kwargs):
+        return run_stage(kind, half, *args, **kwargs)
+
+    relay, q1, *edge = stage("forward_first", forcing, None, faces, coef, wall, relay=early)
+    faces = exchange(*edge)
+    side1 = swap(relay)
+    relay, q2, s1, *edge, squares = stage("forward_last", q1, forcing, faces, coef, wall, squares=True, relay=early)
+    faces = exchange(*edge)
+    side2 = swap(relay)
+    relay, s2, *edge = stage("adjoint_first", s1, q2, faces, coef, wall, relay=early)
+    faces = exchange(*edge)
+    side3 = swap(relay)
+    relay, late_keep, late_send = stage("adjoint_last", s2, q2, faces, coef, wall, span=(early, columns), relay=early)
+    side4 = swap(relay)
     other_keep = swap(late_send)
-    front_keep, front_send = stage("adjoint_last", s2, q2, faces, coef, wall, (0, early))
-
-    guest, *edge = run_edges(guest)
-    faces = exchange(*edge)
-    g1, *edge = stage("forward_first", guest, None, faces, coef, wall)
-    faces = exchange(*edge)
-    g2, h1, _, *edge = stage("forward_last", g1, guest, faces, coef, wall)
-    faces = exchange(*edge)
-    h2, *edge = stage("adjoint_first", h1, g2, faces, coef, wall)
-    faces = exchange(*edge)
-    early_keep, early_send = stage("adjoint_last", h2, g2, faces, coef, wall)
+    front_keep, front_send = stage("adjoint_last", s2, q2, faces, coef, wall, span=(0, early))
+
+    edge = run_guest_edges(guest)
+    faces = exchange(*edge)
+    g1, *edge = stage("forward_first", guest, None, (*faces, side1), coef, wall)
+    faces = exchange(*edge)
+    g2, h1, *edge = stage("forward_last", g1, guest, (*faces, side2), coef, wall)
+    faces = exchange(*edge)
+    h2, *edge = stage("adjoint_first", h1, g2, (*faces, side3), coef, wall)
+    faces = exchange(*edge)
+    early_keep, early_send = stage("adjoint_last", h2, g2, (*faces, side4), coef, wall)
 
     own = (front_keep, front_send, late_keep, late_send)
     base = run_gram(own_gram_body, half, (*own, squares), columns * (columns + 1) // 2, count)
@@ -521,7 +574,9 @@
     cross = (*own, early_keep, early_send, other_keep, base)
     npairs = columns * early + (columns - early) ** 2
     raw = run_gram(cross_gram_body, half, cross, npairs, count)
-    raw = all_sum(raw, ("gx", "gz", "sa"))
+    raw = all_sum(raw, ("sa",), "gz")
+    raw = all_sum(raw, ("gx",), "gz")
+    raw = all_sum(raw, ("gz",), "gz")
     factor, coef = run_factor(entries, columns, half, raw)
     basis = run_basis(half, coef, (front_keep, late_keep, early_keep, other_keep), columns, True)
     basis = run_basis(half, coef, (front_send, late_send, early_send, other_send), columns, False, basis)

time: 144 us -> 146 us (1.014)
  waiting for transfers between devices: 50.7 us -> 76.2 us
  starting transfers between devices: 55.1 us -> 41.1 us
  Pallas kernels: 33.9 us -> 27.2 us
  local copies, waits for them, and re-layouts: 3.24 us -> 0.01 us
    ppermute x3 -> x7, waiting for transfers between devices: 15.7 us -> 45 us  [swap(): return lax.ppermute(value, 'sa', [(0, 1), (1, 0)])]
    ppermute x32 -> x24, starting transfers between devices: 47.5 us -> 32.5 us  [shift(): lax.ppermute(value, axis, [(i, (i + amount) % count) for i in range(count)])]
    ppermute x32 -> x24, waiting for transfers between devices: 24.6 us -> 18.5 us  [shift(): lax.ppermute(value, axis, [(i, (i + amount) % count) for i in range(count)])]
    ppermute x3 -> x7, starting transfers between devices: 1.4 us -> 5.91 us  [swap(): return lax.ppermute(value, 'sa', [(0, 1), (1, 0)])]
    ppermute x5 -> x6, starting transfers between devices: 6.14 us -> 2.78 us  [partner(): return lax.ppermute(value, axis, [(i, i ^ mask) for i in range(count)])]
    unnamed x10 -> x4, local copies, waits for them, and re-layouts: 3.24 us -> 0.01 us
    pallas_call x2, Pallas kernels: 4.35 us -> 1.48 us  [run_gram(): pl.pallas_call(body, out_shape=jax.ShapeDtypeStruct((count, 128), jnp.flo...]
    ppermute x5 -> x6, waiting for transfers between devices: 10.4 us -> 12.7 us  [partner(): return lax.ppermute(value, axis, [(i, i ^ mask) for i in range(count)])]
  transfers between devices with their start and end apart: 40 -> 37, of which waited for: 24 -> 22; matrix products, arithmetic and copies ran while one was open for 0% -> 0% of each run, Pallas kernels for 17% -> 14%
where the time goes in v3:
time: 146 us; the launch traced here: 145 us
  waiting for transfers between devices  76.2 us (52%)
  starting transfers between devices  41.1 us (28%)
  Pallas kernels  27.2 us (19%)
    ppermute x7, waiting for transfers between devices, swap(): return lax.ppermute(value, 'sa', [(0, 1), (1, 0)])  45 us
    ppermute x24, starting transfers between devices, shift(): lax.ppermute(value, axis, [(i, (i + amount) % count) for i in range(count)])  32.5 us
    ppermute x24, waiting for transfers between devices, shift(): lax.ppermute(value, axis, [(i, (i + amount) % count) for i in range(count)])  18.5 us
    pallas_call x9, Pallas kernels, run_stage(): pl.pallas_call(functools.partial(stage_body, kind, span, guest, bool(rela...  18 us
    ppermute x6, waiting for transfers between devices, partner(): return lax.ppermute(value, axis, [(i, i ^ mask) for i in range(count)])  12.7 us
    ppermute x7, starting transfers between devices, swap(): return lax.ppermute(value, 'sa', [(0, 1), (1, 0)])  5.91 us
    pallas_call x2, Pallas kernels, run_basis(): pl.pallas_call(functools.partial(basis_body, 2 * columns, target is not N...  3.52 us
  transfers between devices with their start and end apart: 37, of which 22 were waited for; matrix products, arithmetic and copies ran while one was open for 0% of the time, Pallas kernels for 14%

profile of v3, /device:TPU:0, one launch (start us, length us, event | category | flops | bytes accessed | tf_op | source)
XLA Modules:
  0.0 145.4 jit_solution(17988122443739755911)
XLA Ops:
  0.7 2.4 %edges.1 = (f32[3,4,32,8,256]{4,3,2,1,0:T(8,128)S(1)}, f32[3,2,32,8,256]{4,3,2,1,0:T(8,128)S(1)}, f32[3,4,2,32,128]{4,3,2,1,0:T(8,128)S(1)}, f32[3,4,2,32,128]{4...) custom-call(f32[3,4,32,8,256]{4,3,2,1,0:T(8,128)} %source.1, s32[1]{0:T(128)} %bitcast.half_ref.refs_0_), custom_call_target="tpu_custom_call" | custom-call | tf_op jit(solution)/shard_map/edges/pallas_call | solution.py:261
  3.1 0.5 collective-permute-start.2
  3.6 2.0 %collective-permute-start.3 = (f32[3,4,2,32,128]{4,3,2,1,0:T(8,128)S(1)}, f32[3,4,2,32,128]{4,3,2,1,0:T(8,128)S(1)}, u32[]{:S(2)}, u32[]{:S(2)}) collective-permute-start(f32[3,4,2,32,128]{4,3,2,1,0:T(8,128)S(1)} %get-tuple-element.57), channel_id=1, source_target_pairs={{0,6},{2,0},{4,2},{6,4},{1,7},{3,1},{5,3},{7,5},{8,14},{10,8},{12,... | collective-permute-start | bytes 1179656 | tf_op jit(solution)/shard_map/ppermute | solution.py:493
  5.7 2.3 %collective-permute-start = (f32[3,4,8,256]{3,2,1,0:T(8,128)S(1)}, f32[3,4,8,256]{3,2,1,0:T(8,128)S(1)}, u32[]{:S(2)}, u32[]{:S(2)}) collective-permute-start(f32[3,4,8,256]{3,2,1,0:T(8,128)S(1)} %get-tuple-element.54), channel_id=1, source_target_pairs={{0,8},{8,16},{16,24},{24,0},{1,9},{9,17},{17,25},{25,1},{2,10},{10... | collective-permute-start | bytes 294920 | tf_op jit(solution)/shard_map/ppermute | solution.py:493
  8.0 2.0 %collective-permute-start.1 = (f32[3,4,8,256]{3,2,1,0:T(8,128)S(1)}, f32[3,4,8,256]{3,2,1,0:T(8,128)S(1)}, u32[]{:S(2)}, u32[]{:S(2)}) collective-permute-start(f32[3,4,8,256]{3,2,1,0:T(8,128)S(1)} %get-tuple-element.55), channel_id=1, source_target_pairs={{0,24},{8,0},{16,8},{24,16},{1,25},{9,1},{17,9},{25,17},{2,26},{10... | collective-permute-start | bytes 294920 | tf_op jit(solution)/shard_map/ppermute | solution.py:493
  10.2 3.3 %collective-permute-done.refs_1_ = f32[3,4,8,256]{3,2,1,0:T(8,128)S(1)} collective-permute-done((f32[3,4,8,256]{3,2,1,0:T(8,128)S(1)}, f32[3,4,8,256]{3,2,1,0:T(8,128)S(1)}, u32[]{:S(2)}, u32[]{:S(2)}) %collective-permute-start) | collective-permute-done | bytes 98336 | tf_op jit(solution)/shard_map/ppermute | solution.py:493
  13.5 0.9 collective-permute-done.1.refs_2_
  14.4 0.7 collective-permute-done.3.refs_4_
  15.1 2.8 %shard_map.50 = (f32[2,3,2,8,256]{4,3,2,1,0:T(8,128)S(1)}, f32[3,4,32,8,256]{4,3,2,1,0:T(8,128)S(1)}, f32[3,4,2,32,128]{4,3,2,1,0:T(8,128)S(1)}, f32[3,4,2,32,12...) custom-call(f32[3,4,32,8,256]{4,3,2,1,0:T(8,128)S(1)} %get-tuple-element.53.refs_0_.refs_1_, ...), custom_call_target="tpu_custom_call" | custom-call | tf_op jit(solution)/shard_map/pallas_call | solution.py:199
  18.0 2.1 %collective-permute-start.7 = (f32[3,4,2,32,128]{4,3,2,1,0:T(8,128)S(1)}, f32[3,4,2,32,128]{4,3,2,1,0:T(8,128)S(1)}, u32[]{:S(2)}, u32[]{:S(2)}) collective-permute-start(f32[3,4,2,32,128]{4,3,2,1,0:T(8,128)S(1)} %get-tuple-element.64), channel_id=1, source_target_pairs={{0,6},{2,0},{4,2},{6,4},{1,7},{3,1},{5,3},{7,5},{8,14},{10,8},{12,... | collective-permute-start | bytes 1179656 | tf_op jit(solution)/shard_map/ppermute | solution.py:493
  20.1 1.3 collective-permute-start.16
  21.4 1.6 %collective-permute-start.4 = (f32[3,4,8,256]{3,2,1,0:T(8,128)S(1)}, f32[3,4,8,256]{3,2,1,0:T(8,128)S(1)}, u32[]{:S(2)}, u32[]{:S(2)}) collective-permute-start(f32[3,4,8,256]{3,2,1,0:T(8,128)S(1)} %get-tuple-element.61), channel_id=1, source_target_pairs={{0,8},{8,16},{16,24},{24,0},{1,9},{9,17},{17,25},{25,1},{2,10},{10... | collective-permute-start | bytes 294920 | tf_op jit(solution)/shard_map/ppermute | solution.py:493
  23.0 2.2 %collective-permute-start.5 = (f32[3,4,8,256]{3,2,1,0:T(8,128)S(1)}, f32[3,4,8,256]{3,2,1,0:T(8,128)S(1)}, u32[]{:S(2)}, u32[]{:S(2)}) collective-permute-start(f32[3,4,8,256]{3,2,1,0:T(8,128)S(1)} %get-tuple-element.62), channel_id=1, source_target_pairs={{0,24},{8,0},{16,8},{24,16},{1,25},{9,1},{17,9},{25,17},{2,26},{10... | collective-permute-start | bytes 294920 | tf_op jit(solution)/shard_map/ppermute | solution.py:493
  25.2 3.5 %collective-permute-done.4.refs_2_ = f32[3,4,8,256]{3,2,1,0:T(8,128)S(1)} collective-permute-done((f32[3,4,8,256]{3,2,1,0:T(8,128)S(1)}, f32[3,4,8,256]{3,2,1,0:T(8,128)S(1)}, u32[]{:S(2)}, u32[]{:S(2)}) %collective-permute-start.4) | collective-permute-done | bytes 98336 | tf_op jit(solution)/shard_map/ppermute | solution.py:493
  28.8 0.3 collective-permute-done.5.refs_3_
  29.3 4.9 %shard_map.51 = (f32[2,3,2,8,256]{4,3,2,1,0:T(8,128)S(1)}, f32[3,4,32,8,256]{4,3,2,1,0:T(8,128)S(1)}, f32[3,4,32,8,256]{4,3,2,1,0:T(8,128)S(1)}, f32[3,4,2,32,12...) custom-call(f32[3,4,32,8,256]{4,3,2,1,0:T(8,128)S(1)} %get-tuple-ele, ...), custom_call_target="tpu_custom_call" | custom-call | tf_op jit(solution)/shard_map/pallas_call | solution.py:199
  34.2 0.6 collective-permute-start.10
  34.8 1.7 %collective-permute-start.11 = (f32[3,4,2,32,128]{4,3,2,1,0:T(8,128)S(1)}, f32[3,4,2,32,128]{4,3,2,1,0:T(8,128)S(1)}, u32[]{:S(2)}, u32[]{:S(2)}) collective-permute-start(f32[3,4,2,32,128]{4,3,2,1,0:T(8,128)S(1)} %get-tuple-element.70), channel_id=1, source_target_pairs={{0,6},{2,0},{4,2},{6,4},{1,7},{3,1},{5,3},{7,5},{8,14},{10,8},{12,... | collective-permute-start | bytes 1179656 | tf_op jit(solution)/shard_map/ppermute | solution.py:493
  36.5 0.9 collective-permute-start.8
  37.4 3.0 %collective-permute-start.9 = (f32[3,4,8,256]{3,2,1,0:T(8,128)S(1)}, f32[3,4,8,256]{3,2,1,0:T(8,128)S(1)}, u32[]{:S(2)}, u32[]{:S(2)}) collective-permute-start(f32[3,4,8,256]{3,2,1,0:T(8,128)S(1)} %get-tuple-element.68), channel_id=1, source_target_pairs={{0,24},{8,0},{16,8},{24,16},{1,25},{9,1},{17,9},{25,17},{2,26},{10... | collective-permute-start | bytes 294920 | tf_op jit(solution)/shard_map/ppermute | solution.py:493
  40.3 3.7 %collective-permute-done.8.refs_2_ = f32[3,4,8,256]{3,2,1,0:T(8,128)S(1)} collective-permute-done((f32[3,4,8,256]{3,2,1,0:T(8,128)S(1)}, f32[3,4,8,256]{3,2,1,0:T(8,128)S(1)}, u32[]{:S(2)}, u32[]{:S(2)}) %collective-permute-start.8) | collective-permute-done | bytes 98336 | tf_op jit(solution)/shard_map/ppermute | solution.py:493
  44.2 1.1 collective-permute-done.11.refs_5_
  45.3 2.9 %shard_map.52 = (f32[2,3,2,8,256]{4,3,2,1,0:T(8,128)S(1)}, f32[3,4,32,8,256]{4,3,2,1,0:T(8,128)S(1)}, f32[3,4,2,32,128]{4,3,2,1,0:T(8,128)S(1)}, f32[3,4,2,32,12...) custom-call(f32[3,4,32,8,256]{4,3,2,1,0:T(8,128)S(1)} %get-tuple-element.65.refs_0_, ...), custom_call_target="tpu_custom_call" | custom-call | tf_op jit(solution)/shard_map/pallas_call | solution.py:199
  48.2 1.0 collective-permute-start.14
  49.2 1.3 collective-permute-start.15
  50.5 0.3 collective-permute-start.12
  50.9 3.5 %collective-permute-start.13 = (f32[3,4,8,256]{3,2,1,0:T(8,128)S(1)}, f32[3,4,8,256]{3,2,1,0:T(8,128)S(1)}, u32[]{:S(2)}, u32[]{:S(2)}) collective-permute-start(f32[3,4,8,256]{3,2,1,0:T(8,128)S(1)} %get-tuple-element.73), channel_id=1, source_target_pairs={{0,24},{8,0},{16,8},{24,16},{1,25},{9,1},{17,9},{25,17},{2,26},{10... | collective-permute-start | bytes 294920 | tf_op jit(solution)/shard_map/ppermute | solution.py:493
  54.3 3.4 %collective-permute-done.12.refs_3_ = f32[3,4,8,256]{3,2,1,0:T(8,128)S(1)} collective-permute-done((f32[3,4,8,256]{3,2,1,0:T(8,128)S(1)}, f32[3,4,8,256]{3,2,1,0:T(8,128)S(1)}, u32[]{:S(2)}, u32[]{:S(2)}) %collective-permute-start.12) | collective-permute-done | bytes 98336 | tf_op jit(solution)/shard_map/ppermute | solution.py:493
  57.7 0.8 collective-permute-done.14.refs_5_
  58.5 0.4 collective-permute-done.15.refs_6_
  59.0 0.7 shard_map.54
  59.7 0.3 collective-permute-start.29
  60.1 0.9 collective-permute-start.18
  61.0 1.0 collective-permute-start.19
  62.0 1.8 %collective-permute-start.17 = (f32[2,3,2,8,256]{4,3,2,1,0:T(8,128)S(1)}, f32[2,3,2,8,256]{4,3,2,1,0:T(8,128)S(1)}, u32[]{:S(2)}, u32[]{:S(2)}) collective-permute-start(f32[2,3,2,8,256]{4,3,2,1,0:T(8,128)S(1)} %get-tuple-element.81), channel_id=1, source_target_pairs={{0,1},{1,0},{2,3},{3,2},{4,5},{5,4},{6,7},{7,6},{8,9},{9,8},{10,11... | collective-permute-start | bytes 294920 | tf_op jit(solution)/shard_map/ppermute | solution.py:529
  63.8 18.5 %collective-permute-done.17.refs_1_ = f32[2,3,2,8,256]{4,3,2,1,0:T(8,128)S(1)} collective-permute-done((f32[2,3,2,8,256]{4,3,2,1,0:T(8,128)S(1)}, f32[2,3,2,8,256]{4,3,2,1,0:T(8,128)S(1)}, u32[]{:S(2)}, u32[]{:S(2)}) %collective-permute-start.17) | collective-permute-done | bytes 98336 | tf_op jit(solution)/shard_map/ppermute | solution.py:529
  82.3 1.4 shard_map.55
  83.8 1.6 %collective-permute-start.22 = (f32[3,2,2,32,128]{4,3,2,1,0:T(8,128)S(1)}, f32[3,2,2,32,128]{4,3,2,1,0:T(8,128)S(1)}, u32[]{:S(2)}, u32[]{:S(2)}) collective-permute-start(f32[3,2,2,32,128]{4,3,2,1,0:T(8,128)S(1)} %get-tuple-element.87), channel_id=1, source_target_pairs={{0,6},{2,0},{4,2},{6,4},{1,7},{3,1},{5,3},{7,5},{8,14},{10,8},{12,... | collective-permute-start | bytes 589832 | tf_op jit(solution)/shard_map/ppermute | solution.py:493
  85.6 1.9 %collective-permute-start.20 = (f32[2,3,2,8,256]{4,3,2,1,0:T(8,128)S(1)}, f32[2,3,2,8,256]{4,3,2,1,0:T(8,128)S(1)}, u32[]{:S(2)}, u32[]{:S(2)}) collective-permute-start(f32[2,3,2,8,256]{4,3,2,1,0:T(8,128)S(1)} %get-tuple-element.85), channel_id=1, source_target_pairs={{0,1},{1,0},{2,3},{3,2},{4,5},{5,4},{6,7},{7,6},{8,9},{9,8},{10,11... | collective-permute-start | bytes 294920 | tf_op jit(solution)/shard_map/ppermute | solution.py:529
  87.5 19.3 %collective-permute-done.20.refs_2_ = f32[2,3,2,8,256]{4,3,2,1,0:T(8,128)S(1)} collective-permute-done((f32[2,3,2,8,256]{4,3,2,1,0:T(8,128)S(1)}, f32[2,3,2,8,256]{4,3,2,1,0:T(8,128)S(1)}, u32[]{:S(2)}, u32[]{:S(2)}) %collective-permute-start.20) | collective-permute-done | bytes 98336 | tf_op jit(solution)/shard_map/ppermute | solution.py:529
  106.8 2.4 %shard_map.56 = (f32[3,2,32,8,256]{4,3,2,1,0:T(8,128)S(1)}, f32[3,2,32,8,256]{4,3,2,1,0:T(8,128)S(1)}, f32[3,2,2,32,128]{4,3,2,1,0:T(8,128)S(1)}, f32[3,2,2,32,128]{4,3,2,1,0:T(8,128)S(1)}) custom-call(f32[3,2,32,8,256]{4,3,2,1,0:T(8,128)S(1)} %get-tuple-element.84.refs_0_, f32[3,2,32,8,256]{4,3,2,1,0:T(8,128)S(1)} %collective-permute-done.16.field.refs_0_.refs_1_, ...), custom_call_target="tpu_custom_call" | custom-call | tf_op jit(solution)/shard_map/pallas_call | solution.py:199
  109.2 1.7 %collective-permute-start.25 = (f32[3,2,2,32,128]{4,3,2,1,0:T(8,128)S(1)}, f32[3,2,2,32,128]{4,3,2,1,0:T(8,128)S(1)}, u32[]{:S(2)}, u32[]{:S(2)}) collective-permute-start(f32[3,2,2,32,128]{4,3,2,1,0:T(8,128)S(1)} %get-tuple-element.92), channel_id=1, source_target_pairs={{0,6},{2,0},{4,2},{6,4},{1,7},{3,1},{5,3},{7,5},{8,14},{10,8},{12,... | collective-permute-start | bytes 589832 | tf_op jit(solution)/shard_map/ppermute | solution.py:493
  110.9 0.3 collective-permute-start.23
  111.2 4.3 %collective-permute-done.23.refs_2_ = f32[2,3,2,8,256]{4,3,2,1,0:T(8,128)S(1)} collective-permute-done((f32[2,3,2,8,256]{4,3,2,1,0:T(8,128)S(1)}, f32[2,3,2,8,256]{4,3,2,1,0:T(8,128)S(1)}, u32[]{:S(2)}, u32[]{:S(2)}) %collective-permute-start.23) | collective-permute-done | bytes 98336 | tf_op jit(solution)/shard_map/ppermute | solution.py:529
  115.5 1.5 %shard_map.57 = (f32[3,2,32,8,256]{4,3,2,1,0:T(8,128)S(1)}, f32[3,2,2,32,128]{4,3,2,1,0:T(8,128)S(1)}, f32[3,2,2,32,128]{4,3,2,1,0:T(8,128)S(1)}) custom-call(f32[3,2,32,8,256]{4,3,2,1,0:T(8,128)S(1)} %get-tuple-element.88.refs_0_, f32[3,2,32,8,256]{4,3,2,1,0:T(8,128)S(1)} %get-tuple-element.89.refs_1_.refs_2_, ...), custom_call_target="tpu_custom_call" | custom-call | tf_op jit(solution)/shard_map/pallas_call | solution.py:199
  117.0 0.7 collective-permute-start.27
  117.7 1.1 collective-permute-start.28
  118.8 0.3 collective-permute-start.26
  119.1 0.7 shard_map.53
  119.8 0.7 shard_map.59.base
  120.5 2.9 %collective-permute-done.26.refs_3_ = f32[2,3,2,8,256]{4,3,2,1,0:T(8,128)S(1)} collective-permute-done((f32[2,3,2,8,256]{4,3,2,1,0:T(8,128)S(1)}, f32[2,3,2,8,256]{4,3,2,1,0:T(8,128)S(1)}, u32[]{:S(2)}, u32[]{:S(2)}) %collective-permute-start.26) | collective-permute-done | bytes 98336 | tf_op jit(solution)/shard_map/ppermute | solution.py:529
  123.4 0.8 shard_map.58
  124.2 0.8 shard_map.60
  125.0 0.3 collective-permute-start.30
  125.3 3.3 %collective-permute-done.30 = f32[8,128]{1,0:T(8,128)S(1)} collective-permute-done((f32[8,128]{1,0:T(8,128)S(1)}, f32[8,128]{1,0:T(8,128)S(1)}, u32[]{:S(2)}, u32[]{:S(2)}) %collective-permute-start.30) | collective-permute-done | bytes 4128 | tf_op jit(solution)/shard_map/ppermute | solution.py:507
  128.7 3.6 %collective-permute-done.31 = f32[8,128]{1,0:T(8,128)S(1)} collective-permute-done((f32[8,128]{1,0:T(8,128)S(1)}, f32[8,128]{1,0:T(8,128)S(1)}, u32[]{:S(2)}, u32[]{:S(2)}) %collective-permute-start.31) | collective-permute-done | bytes 4128 | tf_op jit(solution)/shard_map/ppermute | solution.py:507
  132.3 0.6 collective-permute-start.32
  132.8 3.9 %collective-permute-done.32 = f32[8,128]{1,0:T(8,128)S(1)} collective-permute-done((f32[8,128]{1,0:T(8,128)S(1)}, f32[8,128]{1,0:T(8,128)S(1)}, u32[]{:S(2)}, u32[]{:S(2)}) %collective-permute-start.32) | collective-permute-done | bytes 4128 | tf_op jit(solution)/shard_map/ppermute | solution.py:507
  136.8 0.7 collective-permute-start.34
  137.5 1.2 collective-permute-start.35
  138.7 1.7 %collective-permute-done.34 = f32[8,128]{1,0:T(8,128)S(1)} collective-permute-done((f32[8,128]{1,0:T(8,128)S(1)}, f32[8,128]{1,0:T(8,128)S(1)}, u32[]{:S(2)}, u32[]{:S(2)}) %collective-permute-start.34) | collective-permute-done | bytes 4128 | tf_op jit(solution)/shard_map/ppermute | solution.py:507
  140.5 1.4 factor.1
  141.9 1.8 %basis.2.refs_4_ = f32[3,4,32,8,256]{4,3,2,1,0:T(8,128)} custom-call(s32[1]{0:T(128)} %bitcast.half_ref.refs_0_, f32[32,8,128]{2,1,0:T(8,128)S(1)} %get-tuple-element.101.coef, f32[3,2,16,8,256]{4,3,2,1,0:T(8,128)S(1)} %get-tuple-element.76.front_keep.fk.refs_0_, f32[3,2,16,8,256]{4,3,2,1,0:T(8,128)S(1)} %get-tuple-element.102.late_keep.lk.refs_1_, ...), custom_call_target="tpu_custom_call" | custom-call | tf_op jit(solution)/shard_map/basis/pallas_call | solution.py:479
  143.6 1.8 %basis.3 = f32[3,4,32,8,256]{4,3,2,1,0:T(8,128)} custom-call(s32[1]{0:T(128)} %bitcast.half_ref.refs_0_, f32[32,8,128]{2,1,0:T(8,128)S(1)} %get-tuple-element.101.coef, f32[3,2,16,8,256]{4,3,2,1,0:T(8,128)S(1)} %get-tuple-element.77.front_send.fs.refs_0_, ...), custom_call_target="tpu_custom_call", output_to_operand_aliasing={{}: (6, {})} | custom-call | tf_op jit(solution)/shard_map/basis/pallas_call | solution.py:479
  (35 shorter events, 1.3 us)
Async XLA Ops:
  0.6 9.4 %copy-start.1 = (f32[256]{0:T(256)S(1)}, f32[256]{0:T(256)}, u32[]{:S(2)}) copy-start(f32[256]{0:T(256)} %param.4) | copy-start | bytes 3076
  0.6 9.3 %copy-start = (f32[256,256]{1,0:T(8,128)S(1)}, f32[256,256]{1,0:T(8,128)}, u32[]{:S(2)}) copy-start(f32[256,256]{1,0:T(8,128)} %wall_solve.1) | copy-start | bytes 786436
  3.1 11.3 %collective-permute-start.2 = (f32[3,4,2,32,128]{4,3,2,1,0:T(8,128)S(1)}, f32[3,4,2,32,128]{4,3,2,1,0:T(8,128)S(1)}, u32[]{:S(2)}, u32[]{:S(2)}) collective-permute-start(f32[3,4,2,32,128]{4,3,2,1,0:T(8,128)S(1)} %get-tuple-element.56), channel_id=1, source_target_pairs={{0,2},{2,4},{4,6},{6,0},{1,3},{3,5},{5,7},{7,1},{8,10},{10,12},{12... | collective-permute-start | bytes 1179656 | tf_op jit(solution)/shard_map/ppermute | solution.py:493
  3.6 11.4 %collective-permute-start.3 = (f32[3,4,2,32,128]{4,3,2,1,0:T(8,128)S(1)}, f32[3,4,2,32,128]{4,3,2,1,0:T(8,128)S(1)}, u32[]{:S(2)}, u32[]{:S(2)}) collective-permute-start(f32[3,4,2,32,128]{4,3,2,1,0:T(8,128)S(1)} %get-tuple-element.57), channel_id=1, source_target_pairs={{0,6},{2,0},{4,2},{6,4},{1,7},{3,1},{5,3},{7,5},{8,14},{10,8},{12,... | collective-permute-start | bytes 1179656 | tf_op jit(solution)/shard_map/ppermute | solution.py:493
  5.7 7.8 %collective-permute-start = (f32[3,4,8,256]{3,2,1,0:T(8,128)S(1)}, f32[3,4,8,256]{3,2,1,0:T(8,128)S(1)}, u32[]{:S(2)}, u32[]{:S(2)}) collective-permute-start(f32[3,4,8,256]{3,2,1,0:T(8,128)S(1)} %get-tuple-element.54), channel_id=1, source_target_pairs={{0,8},{8,16},{16,24},{24,0},{1,9},{9,17},{17,25},{25,1},{2,10},{10... | collective-permute-start | bytes 294920 | tf_op jit(solution)/shard_map/ppermute | solution.py:493
  8.0 6.4 %collective-permute-start.1 = (f32[3,4,8,256]{3,2,1,0:T(8,128)S(1)}, f32[3,4,8,256]{3,2,1,0:T(8,128)S(1)}, u32[]{:S(2)}, u32[]{:S(2)}) collective-permute-start(f32[3,4,8,256]{3,2,1,0:T(8,128)S(1)} %get-tuple-element.55), channel_id=1, source_target_pairs={{0,24},{8,0},{16,8},{24,16},{1,25},{9,1},{17,9},{25,17},{2,26},{10... | collective-permute-start | bytes 294920 | tf_op jit(solution)/shard_map/ppermute | solution.py:493
  17.9 11.2 %collective-permute-start.6 = (f32[3,4,2,32,128]{4,3,2,1,0:T(8,128)S(1)}, f32[3,4,2,32,128]{4,3,2,1,0:T(8,128)S(1)}, u32[]{:S(2)}, u32[]{:S(2)}) collective-permute-start(f32[3,4,2,32,128]{4,3,2,1,0:T(8,128)S(1)} %get-tuple-element.63), channel_id=1, source_target_pairs={{0,2},{2,4},{4,6},{6,0},{1,3},{3,5},{5,7},{7,1},{8,10},{10,12},{12... | collective-permute-start | bytes 1179656 | tf_op jit(solution)/shard_map/ppermute | solution.py:493
  18.0 11.3 %collective-permute-start.7 = (f32[3,4,2,32,128]{4,3,2,1,0:T(8,128)S(1)}, f32[3,4,2,32,128]{4,3,2,1,0:T(8,128)S(1)}, u32[]{:S(2)}, u32[]{:S(2)}) collective-permute-start(f32[3,4,2,32,128]{4,3,2,1,0:T(8,128)S(1)} %get-tuple-element.64), channel_id=1, source_target_pairs={{0,6},{2,0},{4,2},{6,4},{1,7},{3,1},{5,3},{7,5},{8,14},{10,8},{12,... | collective-permute-start | bytes 1179656 | tf_op jit(solution)/shard_map/ppermute | solution.py:493
  20.1 39.8 %collective-permute-start.16 = (f32[3,2,32,8,256]{4,3,2,1,0:T(8,128)S(1)}, f32[3,2,32,8,256]{4,3,2,1,0:T(8,128)S(1)}, u32[]{:S(2)}, u32[]{:S(2)}) collective-permute-start(f32[3,2,32,8,256]{4,3,2,1,0:T(8,128)S(1)} %get-tuple-element.80), channel_id=1, source_target_pairs={{0,1},{1,0},{2,3},{3,2},{4,5},{5,4},{6,7},{7,6},{8,9},{9,8},{10,11... | collective-permute-start | bytes 4718600 | tf_op jit(solution)/shard_map/ppermute | solution.py:529
  21.4 7.4 %collective-permute-start.4 = (f32[3,4,8,256]{3,2,1,0:T(8,128)S(1)}, f32[3,4,8,256]{3,2,1,0:T(8,128)S(1)}, u32[]{:S(2)}, u32[]{:S(2)}) collective-permute-start(f32[3,4,8,256]{3,2,1,0:T(8,128)S(1)} %get-tuple-element.61), channel_id=1, source_target_pairs={{0,8},{8,16},{16,24},{24,0},{1,9},{9,17},{17,25},{25,1},{2,10},{10... | collective-permute-start | bytes 294920 | tf_op jit(solution)/shard_map/ppermute | solution.py:493
  23.0 6.1 %collective-permute-start.5 = (f32[3,4,8,256]{3,2,1,0:T(8,128)S(1)}, f32[3,4,8,256]{3,2,1,0:T(8,128)S(1)}, u32[]{:S(2)}, u32[]{:S(2)}) collective-permute-start(f32[3,4,8,256]{3,2,1,0:T(8,128)S(1)} %get-tuple-element.62), channel_id=1, source_target_pairs={{0,24},{8,0},{16,8},{24,16},{1,25},{9,1},{17,9},{25,17},{2,26},{10... | collective-permute-start | bytes 294920 | tf_op jit(solution)/shard_map/ppermute | solution.py:493
  34.2 10.0 %collective-permute-start.10 = (f32[3,4,2,32,128]{4,3,2,1,0:T(8,128)S(1)}, f32[3,4,2,32,128]{4,3,2,1,0:T(8,128)S(1)}, u32[]{:S(2)}, u32[]{:S(2)}) collective-permute-start(f32[3,4,2,32,128]{4,3,2,1,0:T(8,128)S(1)} %get-tuple-element.69), channel_id=1, source_target_pairs={{0,2},{2,4},{4,6},{6,0},{1,3},{3,5},{5,7},{7,1},{8,10},{10,12},{12... | collective-permute-start | bytes 1179656 | tf_op jit(solution)/shard_map/ppermute | solution.py:493
  34.8 10.5 %collective-permute-start.11 = (f32[3,4,2,32,128]{4,3,2,1,0:T(8,128)S(1)}, f32[3,4,2,32,128]{4,3,2,1,0:T(8,128)S(1)}, u32[]{:S(2)}, u32[]{:S(2)}) collective-permute-start(f32[3,4,2,32,128]{4,3,2,1,0:T(8,128)S(1)} %get-tuple-element.70), channel_id=1, source_target_pairs={{0,6},{2,0},{4,2},{6,4},{1,7},{3,1},{5,3},{7,5},{8,14},{10,8},{12,... | collective-permute-start | bytes 1179656 | tf_op jit(solution)/shard_map/ppermute | solution.py:493
  36.5 7.5 %collective-permute-start.8 = (f32[3,4,8,256]{3,2,1,0:T(8,128)S(1)}, f32[3,4,8,256]{3,2,1,0:T(8,128)S(1)}, u32[]{:S(2)}, u32[]{:S(2)}) collective-permute-start(f32[3,4,8,256]{3,2,1,0:T(8,128)S(1)} %get-tuple-element.67), channel_id=1, source_target_pairs={{0,8},{8,16},{16,24},{24,0},{1,9},{9,17},{17,25},{25,1},{2,10},{10... | collective-permute-start | bytes 294920 | tf_op jit(solution)/shard_map/ppermute | solution.py:493
  37.4 6.7 %collective-permute-start.9 = (f32[3,4,8,256]{3,2,1,0:T(8,128)S(1)}, f32[3,4,8,256]{3,2,1,0:T(8,128)S(1)}, u32[]{:S(2)}, u32[]{:S(2)}) collective-permute-start(f32[3,4,8,256]{3,2,1,0:T(8,128)S(1)} %get-tuple-element.68), channel_id=1, source_target_pairs={{0,24},{8,0},{16,8},{24,16},{1,25},{9,1},{17,9},{25,17},{2,26},{10... | collective-permute-start | bytes 294920 | tf_op jit(solution)/shard_map/ppermute | solution.py:493
  48.2 10.3 %collective-permute-start.14 = (f32[3,4,2,32,128]{4,3,2,1,0:T(8,128)S(1)}, f32[3,4,2,32,128]{4,3,2,1,0:T(8,128)S(1)}, u32[]{:S(2)}, u32[]{:S(2)}) collective-permute-start(f32[3,4,2,32,128]{4,3,2,1,0:T(8,128)S(1)} %get-tuple-element.74), channel_id=1, source_target_pairs={{0,2},{2,4},{4,6},{6,0},{1,3},{3,5},{5,7},{7,1},{8,10},{10,12},{12... | collective-permute-start | bytes 1179656 | tf_op jit(solution)/shard_map/ppermute | solution.py:493
  49.2 9.8 %collective-permute-start.15 = (f32[3,4,2,32,128]{4,3,2,1,0:T(8,128)S(1)}, f32[3,4,2,32,128]{4,3,2,1,0:T(8,128)S(1)}, u32[]{:S(2)}, u32[]{:S(2)}) collective-permute-start(f32[3,4,2,32,128]{4,3,2,1,0:T(8,128)S(1)} %get-tuple-element.75), channel_id=1, source_target_pairs={{0,6},{2,0},{4,2},{6,4},{1,7},{3,1},{5,3},{7,5},{8,14},{10,8},{12,... | collective-permute-start | bytes 1179656 | tf_op jit(solution)/shard_map/ppermute | solution.py:493
  50.5 7.2 %collective-permute-start.12 = (f32[3,4,8,256]{3,2,1,0:T(8,128)S(1)}, f32[3,4,8,256]{3,2,1,0:T(8,128)S(1)}, u32[]{:S(2)}, u32[]{:S(2)}) collective-permute-start(f32[3,4,8,256]{3,2,1,0:T(8,128)S(1)} %get-tuple-element.72), channel_id=1, source_target_pairs={{0,8},{8,16},{16,24},{24,0},{1,9},{9,17},{17,25},{25,1},{2,10},{10... | collective-permute-start | bytes 294920 | tf_op jit(solution)/shard_map/ppermute | solution.py:493
  50.9 6.9 %collective-permute-start.13 = (f32[3,4,8,256]{3,2,1,0:T(8,128)S(1)}, f32[3,4,8,256]{3,2,1,0:T(8,128)S(1)}, u32[]{:S(2)}, u32[]{:S(2)}) collective-permute-start(f32[3,4,8,256]{3,2,1,0:T(8,128)S(1)} %get-tuple-element.73), channel_id=1, source_target_pairs={{0,24},{8,0},{16,8},{24,16},{1,25},{9,1},{17,9},{25,17},{2,26},{10... | collective-permute-start | bytes 294920 | tf_op jit(solution)/shard_map/ppermute | solution.py:493
  59.7 25.8 %collective-permute-start.29 = (f32[3,2,16,8,256]{4,3,2,1,0:T(8,128)S(1)}, f32[3,2,16,8,256]{4,3,2,1,0:T(8,128)S(1)}, u32[]{:S(2)}, u32[]{:S(2)}) collective-permute-start(f32[3,2,16,8,256]{4,3,2,1,0:T(8,128)S(1)} %get-tuple-element.79.late_send.ls.refs_1_), channel_id=1, source_target_pairs={{0,1},{1,0},{2,3},{3,2},{4,5},{5,4},{6,7},{7,6},{8,9},{9,8},{10,11... | collective-permute-start | bytes 2359304 | tf_op jit(solution)/shard_map/ppermute | solution.py:529
  60.1 22.1 %collective-permute-start.18 = (f32[3,2,2,32,128]{4,3,2,1,0:T(8,128)S(1)}, f32[3,2,2,32,128]{4,3,2,1,0:T(8,128)S(1)}, u32[]{:S(2)}, u32[]{:S(2)}) collective-permute-start(f32[3,2,2,32,128]{4,3,2,1,0:T(8,128)S(1)} %get-tuple-element.82), channel_id=1, source_target_pairs={{0,2},{2,4},{4,6},{6,0},{1,3},{3,5},{5,7},{7,1},{8,10},{10,12},{12... | collective-permute-start | bytes 589832 | tf_op jit(solution)/shard_map/ppermute | solution.py:493
  61.0 21.2 %collective-permute-start.19 = (f32[3,2,2,32,128]{4,3,2,1,0:T(8,128)S(1)}, f32[3,2,2,32,128]{4,3,2,1,0:T(8,128)S(1)}, u32[]{:S(2)}, u32[]{:S(2)}) collective-permute-start(f32[3,2,2,32,128]{4,3,2,1,0:T(8,128)S(1)} %get-tuple-element.83), channel_id=1, source_target_pairs={{0,6},{2,0},{4,2},{6,4},{1,7},{3,1},{5,3},{7,5},{8,14},{10,8},{12,... | collective-permute-start | bytes 589832 | tf_op jit(solution)/shard_map/ppermute | solution.py:493
  62.0 20.3 %collective-permute-start.17 = (f32[2,3,2,8,256]{4,3,2,1,0:T(8,128)S(1)}, f32[2,3,2,8,256]{4,3,2,1,0:T(8,128)S(1)}, u32[]{:S(2)}, u32[]{:S(2)}) collective-permute-start(f32[2,3,2,8,256]{4,3,2,1,0:T(8,128)S(1)} %get-tuple-element.81), channel_id=1, source_target_pairs={{0,1},{1,0},{2,3},{3,2},{4,5},{5,4},{6,7},{7,6},{8,9},{9,8},{10,11... | collective-permute-start | bytes 294920 | tf_op jit(solution)/shard_map/ppermute | solution.py:529
  83.7 23.1 %collective-permute-start.21 = (f32[3,2,2,32,128]{4,3,2,1,0:T(8,128)S(1)}, f32[3,2,2,32,128]{4,3,2,1,0:T(8,128)S(1)}, u32[]{:S(2)}, u32[]{:S(2)}) collective-permute-start(f32[3,2,2,32,128]{4,3,2,1,0:T(8,128)S(1)} %get-tuple-element.86), channel_id=1, source_target_pairs={{0,2},{2,4},{4,6},{6,0},{1,3},{3,5},{5,7},{7,1},{8,10},{10,12},{12... | collective-permute-start | bytes 589832 | tf_op jit(solution)/shard_map/ppermute | solution.py:493
  83.8 22.9 %collective-permute-start.22 = (f32[3,2,2,32,128]{4,3,2,1,0:T(8,128)S(1)}, f32[3,2,2,32,128]{4,3,2,1,0:T(8,128)S(1)}, u32[]{:S(2)}, u32[]{:S(2)}) collective-permute-start(f32[3,2,2,32,128]{4,3,2,1,0:T(8,128)S(1)} %get-tuple-element.87), channel_id=1, source_target_pairs={{0,6},{2,0},{4,2},{6,4},{1,7},{3,1},{5,3},{7,5},{8,14},{10,8},{12,... | collective-permute-start | bytes 589832 | tf_op jit(solution)/shard_map/ppermute | solution.py:493
  85.5 58.2 %collective-permute-start.36 = (f32[3,2,16,8,256]{4,3,2,1,0:T(8,128)S(1)}, f32[3,2,16,8,256]{4,3,2,1,0:T(8,128)S(1)}, u32[]{:S(2)}, u32[]{:S(2)}) collective-permute-start(f32[3,2,16,8,256]{4,3,2,1,0:T(8,128)S(1)} %get-tuple-element.102.late_keep.lk.refs_1_), channel_id=1, source_target_pairs={{0,1},{1,0},{2,3},{3,2},{4,5},{5,4},{6,7},{7,6},{8,9},{9,8},{10,11... | collective-permute-start | bytes 2359304 | tf_op jit(solution)/shard_map/ppermute | solution.py:529
  85.6 21.2 %collective-permute-start.20 = (f32[2,3,2,8,256]{4,3,2,1,0:T(8,128)S(1)}, f32[2,3,2,8,256]{4,3,2,1,0:T(8,128)S(1)}, u32[]{:S(2)}, u32[]{:S(2)}) collective-permute-start(f32[2,3,2,8,256]{4,3,2,1,0:T(8,128)S(1)} %get-tuple-element.85), channel_id=1, source_target_pairs={{0,1},{1,0},{2,3},{3,2},{4,5},{5,4},{6,7},{7,6},{8,9},{9,8},{10,11... | collective-permute-start | bytes 294920 | tf_op jit(solution)/shard_map/ppermute | solution.py:529
  109.1 6.4 %collective-permute-start.24 = (f32[3,2,2,32,128]{4,3,2,1,0:T(8,128)S(1)}, f32[3,2,2,32,128]{4,3,2,1,0:T(8,128)S(1)}, u32[]{:S(2)}, u32[]{:S(2)}) collective-permute-start(f32[3,2,2,32,128]{4,3,2,1,0:T(8,128)S(1)} %get-tuple-element.91), channel_id=1, source_target_pairs={{0,2},{2,4},{4,6},{6,0},{1,3},{3,5},{5,7},{7,1},{8,10},{10,12},{12... | collective-permute-start | bytes 589832 | tf_op jit(solution)/shard_map/ppermute | solution.py:493
  109.2 6.4 %collective-permute-start.25 = (f32[3,2,2,32,128]{4,3,2,1,0:T(8,128)S(1)}, f32[3,2,2,32,128]{4,3,2,1,0:T(8,128)S(1)}, u32[]{:S(2)}, u32[]{:S(2)}) collective-permute-start(f32[3,2,2,32,128]{4,3,2,1,0:T(8,128)S(1)} %get-tuple-element.92), channel_id=1, source_target_pairs={{0,6},{2,0},{4,2},{6,4},{1,7},{3,1},{5,3},{7,5},{8,14},{10,8},{12,... | collective-permute-start | bytes 589832 | tf_op jit(solution)/shard_map/ppermute | solution.py:493
  110.9 4.6 %collective-permute-start.23 = (f32[2,3,2,8,256]{4,3,2,1,0:T(8,128)S(1)}, f32[2,3,2,8,256]{4,3,2,1,0:T(8,128)S(1)}, u32[]{:S(2)}, u32[]{:S(2)}) collective-permute-start(f32[2,3,2,8,256]{4,3,2,1,0:T(8,128)S(1)} %get-tuple-element.90), channel_id=1, source_target_pairs={{0,1},{1,0},{2,3},{3,2},{4,5},{5,4},{6,7},{7,6},{8,9},{9,8},{10,11... | collective-permute-start | bytes 294920 | tf_op jit(solution)/shard_map/ppermute | solution.py:529
  117.0 6.4 %collective-permute-start.27 = (f32[3,2,2,32,128]{4,3,2,1,0:T(8,128)S(1)}, f32[3,2,2,32,128]{4,3,2,1,0:T(8,128)S(1)}, u32[]{:S(2)}, u32[]{:S(2)}) collective-permute-start(f32[3,2,2,32,128]{4,3,2,1,0:T(8,128)S(1)} %get-tuple-element.95), channel_id=1, source_target_pairs={{0,2},{2,4},{4,6},{6,0},{1,3},{3,5},{5,7},{7,1},{8,10},{10,12},{12... | collective-permute-start | bytes 589832 | tf_op jit(solution)/shard_map/ppermute | solution.py:493
  117.7 5.7 %collective-permute-start.28 = (f32[3,2,2,32,128]{4,3,2,1,0:T(8,128)S(1)}, f32[3,2,2,32,128]{4,3,2,1,0:T(8,128)S(1)}, u32[]{:S(2)}, u32[]{:S(2)}) collective-permute-start(f32[3,2,2,32,128]{4,3,2,1,0:T(8,128)S(1)} %get-tuple-element.96), channel_id=1, source_target_pairs={{0,6},{2,0},{4,2},{6,4},{1,7},{3,1},{5,3},{7,5},{8,14},{10,8},{12,... | collective-permute-start | bytes 589832 | tf_op jit(solution)/shard_map/ppermute | solution.py:493
  118.8 4.6 %collective-permute-start.26 = (f32[2,3,2,8,256]{4,3,2,1,0:T(8,128)S(1)}, f32[2,3,2,8,256]{4,3,2,1,0:T(8,128)S(1)}, u32[]{:S(2)}, u32[]{:S(2)}) collective-permute-start(f32[2,3,2,8,256]{4,3,2,1,0:T(8,128)S(1)} %get-tuple-element.94), channel_id=1, source_target_pairs={{0,1},{1,0},{2,3},{3,2},{4,5},{5,4},{6,7},{7,6},{8,9},{9,8},{10,11... | collective-permute-start | bytes 294920 | tf_op jit(solution)/shard_map/ppermute | solution.py:529
  125.0 3.7 %collective-permute-start.30 = (f32[8,128]{1,0:T(8,128)S(1)}, f32[8,128]{1,0:T(8,128)S(1)}, u32[]{:S(2)}, u32[]{:S(2)}) collective-permute-start(f32[8,128]{1,0:T(8,128)S(1)} %shard_map.60), channel_id=1, source_target_pairs={{0,1},{1,0},{2,3},{3,2},{4,5},{5,4},{6,7},{7,6},{8,9},{9,8},{10,11... | collective-permute-start | bytes 12296 | tf_op jit(solution)/shard_map/ppermute | solution.py:507
  128.7 3.6 %collective-permute-start.31 = (f32[8,128]{1,0:T(8,128)S(1)}, f32[8,128]{1,0:T(8,128)S(1)}, u32[]{:S(2)}, u32[]{:S(2)}) collective-permute-start(f32[8,128]{1,0:T(8,128)S(1)} %add.18), channel_id=1, source_target_pairs={{0,8},{8,0},{16,24},{24,16},{1,9},{9,1},{17,25},{25,17},{2,10},{10... | collective-permute-start | bytes 12296 | tf_op jit(solution)/shard_map/ppermute | solution.py:507
  132.3 4.5 %collective-permute-start.32 = (f32[8,128]{1,0:T(8,128)S(1)}, f32[8,128]{1,0:T(8,128)S(1)}, u32[]{:S(2)}, u32[]{:S(2)}) collective-permute-start(f32[8,128]{1,0:T(8,128)S(1)} %add.19), channel_id=1, source_target_pairs={{0,16},{8,24},{16,0},{24,8},{1,17},{9,25},{17,1},{25,9},{2,18},{10... | collective-permute-start | bytes 12296 | tf_op jit(solution)/shard_map/ppermute | solution.py:507
  136.8 1.9 %collective-permute-start.33 = (f32[8,128]{1,0:T(8,128)S(1)}, f32[8,128]{1,0:T(8,128)S(1)}, u32[]{:S(2)}, u32[]{:S(2)}) collective-permute-start(f32[8,128]{1,0:T(8,128)S(1)} %add.20), channel_id=1, source_target_pairs={{0,2},{2,0},{4,6},{6,4},{1,3},{3,1},{5,7},{7,5},{8,10},{10,8},{12,... | collective-permute-start | bytes 12296 | tf_op jit(solution)/shard_map/ppermute | solution.py:507
  136.8 3.6 %collective-permute-start.34 = (f32[8,128]{1,0:T(8,128)S(1)}, f32[8,128]{1,0:T(8,128)S(1)}, u32[]{:S(2)}, u32[]{:S(2)}) collective-permute-start(f32[8,128]{1,0:T(8,128)S(1)} %add.20), channel_id=1, source_target_pairs={{0,4},{2,6},{4,0},{6,2},{1,5},{3,7},{5,1},{7,3},{8,12},{10,14},{12... | collective-permute-start | bytes 12296 | tf_op jit(solution)/shard_map/ppermute | solution.py:507
  137.5 3.0 %collective-permute-start.35 = (f32[8,128]{1,0:T(8,128)S(1)}, f32[8,128]{1,0:T(8,128)S(1)}, u32[]{:S(2)}, u32[]{:S(2)}) collective-permute-start(f32[8,128]{1,0:T(8,128)S(1)} %add.20), channel_id=1, source_target_pairs={{0,6},{2,4},{4,2},{6,0},{1,7},{3,5},{5,3},{7,1},{8,14},{10,12},{12... | collective-permute-start | bytes 12296 | tf_op jit(solution)/shard_map/ppermute | solution.py:507

commit v4 on v3

--- a/solution.py
+++ b/solution.py
@@ -12,6 +12,7 @@
 viscosity = 0.2
 VMEM_LIMIT = 8 * 1024 * 1024
 X_CHUNK = 4
+ROW_PARTS = 2
 
 
 def split_halves(value):
@@ -53,20 +54,21 @@
     return value
 
 
-def put_faces(result, comp, lanes_ref, faces, nz):
+def put_faces(result, comp, lanes_ref, faces, nz, x0=0, nx=None):
     first_z, last_z, *x_faces = faces
     size = result.shape[0]
-    nx = size // nz
-    if x_faces:
+    step = size // nz
+    if x_faces and x0 == 0:
         x_faces[0][comp, 0] = result[:nz]
+    if x_faces and x0 + step == (nx or step):
         x_faces[1][comp, 0] = result[size - nz :]
     for h in range(lanes_ref.shape[0]):
-        lanes_ref[h] = result[:, h * 128 : (h + 1) * 128]
-        first_z[comp, 0, h] = lanes_ref[h, pl.ds(0, nx, stride=nz), :]
-        last_z[comp, 0, h] = lanes_ref[h, pl.ds(nz - 1, nx, stride=nz), :]
-
-
-def stage_body(kind, span, guest, relayed, *refs):
+        lanes_ref[h, x0 * nz : x0 * nz + size] = result[:, h * 128 : (h + 1) * 128]
+        first_z[comp, 0, h, x0 : x0 + step] = lanes_ref[h, pl.ds(x0 * nz, step, stride=nz), :]
+        last_z[comp, 0, h, x0 : x0 + step] = lanes_ref[h, pl.ds(x0 * nz + nz - 1, step, stride=nz), :]
+
+
+def stage_body(kind, span, guest, place, relayed, *refs):
     if kind == "adjoint_last":
         half_ref, *refs = refs
     src = None
@@ -76,7 +78,7 @@
         cur, src, *refs = refs
     if guest:
         both, *refs = refs
-        xlo, xhi = both.at[0], both.at[1]
+        xlo, xhi = both.at[2 * place], both.at[2 * place + 1]
     else:
         xlo, xhi, *refs = refs
     zlo, zhi, coef, wall, *rest = refs
@@ -129,7 +131,6 @@
     center = 1.0 / (step_length * viscosity) - 4.0
     if kind == "forward_first":
         center = center + 1.0 / viscosity
-    size = nx * nz
     total = None
     faces = outs[2:] if kind == "forward_last" else outs[1:]
     for comp in range(3):
@@ -145,21 +146,23 @@
             spot = (comp * nx + x0) * nz
             high[spot : spot + X_CHUNK * nz] = h
             low[spot : spot + X_CHUNK * nz] = l
-        part = slice(comp * size, (comp + 1) * size)
-        result = wall_product(high[part], low[part], wall.at[pl.ds(2, 2)] if adjoint else wall.at[pl.ds(0, 2)])
-        if kind == "forward_last":
-            if squares is not None:
-                tile = result.reshape(nx, nz, ny)
-                sums = jnp.sum(tile * tile, axis=0)
-                total = sums if total is None else total + sums
-            scaled = result * (1.0 / viscosity)
-            outs[0][comp, 0] = scaled.reshape(nx, nz, ny)
-            h, l = split_halves(scaled)
-            result = wall_product(h, l, wall.at[pl.ds(4, 2)])
-            outs[1][comp, 0] = result.reshape(nx, nz, ny)
-        else:
-            outs[0][comp, 0] = result.reshape(nx, nz, ny)
-        put_faces(result, comp, lanes, faces, nz)
+        step = nx if kind == "forward_last" else nx // ROW_PARTS
+        for x0 in range(0, nx, step):
+            part = slice((comp * nx + x0) * nz, (comp * nx + x0 + step) * nz)
+            result = wall_product(high[part], low[part], wall.at[pl.ds(2, 2)] if adjoint else wall.at[pl.ds(0, 2)])
+            if kind == "forward_last":
+                if squares is not None:
+                    tile = result.reshape(step, nz, ny)
+                    sums = jnp.sum(tile * tile, axis=0)
+                    total = sums if total is None else total + sums
+                scaled = result * (1.0 / viscosity)
+                outs[0][comp, 0, x0 : x0 + step] = scaled.reshape(step, nz, ny)
+                h, l = split_halves(scaled)
+                result = wall_product(h, l, wall.at[pl.ds(4, 2)])
+                outs[1][comp, 0, x0 : x0 + step] = result.reshape(step, nz, ny)
+            else:
+                outs[0][comp, 0, x0 : x0 + step] = result.reshape(step, nz, ny)
+            put_faces(result, comp, lanes, faces, nz, x0, nx)
     if total is not None:
         squares[0] = total
 
@@ -172,7 +175,7 @@
     return pltpu.with_memory_space_constraint(value, pltpu.VMEM)
 
 
-def run_stage(kind, half, cur, src, faces, coef, wall, span=None, squares=False, relay=0):
+def run_stage(kind, half, cur, src, faces, coef, wall, span=None, squares=False, relay=0, place=0):
     three, columns, nx, nz, ny = cur.shape
     span = span or (0, columns)
     guest = len(faces) == 3
@@ -197,7 +200,7 @@
     if kind == "adjoint_last":
         operands, in_specs = [half] + operands, [pl.BlockSpec(memory_space=pltpu.SMEM)] + in_specs
     return pl.pallas_call(
-        functools.partial(stage_body, kind, span, guest, bool(relay)),
+        functools.partial(stage_body, kind, span, guest, place, bool(relay)),
         out_shape=outs,
         in_specs=in_specs,
         out_specs=[vmem] * len(outs),
@@ -275,6 +278,24 @@
         faces = [ref.at[:, pl.ds(j, 1)] for ref in (first_z, last_z)]
         for comp in range(three):
             put_faces(field[comp, j].reshape(nx * nz, ny), comp, lanes, faces, nz)
+
+
+def relay_body(earlier, xlo, xhi, out):
+    out[0], out[1] = earlier[0], earlier[1]
+    out[2] = xlo[:, : out.shape[2]]
+    out[3] = xhi[:, : out.shape[2]]
+
+
+def run_relay(earlier, xlo, xhi):
+    vmem = pl.BlockSpec(memory_space=pltpu.VMEM)
+    return pl.pallas_call(
+        relay_body,
+        out_shape=in_vmem((4, *earlier.shape[1:])),
+        in_specs=[vmem] * 3,
+        out_specs=vmem,
+        compiler_params=pltpu.CompilerParams(vmem_limit_bytes=VMEM_LIMIT),
+        name="relay",
+    )(hold(earlier), hold(xlo), hold(xhi))
 
 
 def run_guest_edges(field):
@@ -441,10 +462,11 @@
     )(half, raw)
 
 
-def basis_body(count, aliased, half_ref, coef, *refs):
+def basis_body(count, first, partial, aliased, half_ref, coef, *refs):
     fields, out = (refs[:-2], refs[-1]) if aliased else (refs[:-1], refs[-1])
+    *fields, begun = fields if partial else (*fields, None)
     three, columns, nx, _, ny = out.shape
-    base = pl.program_id(0) * nx
+    base = 0 if out.shape[2] == fields[0].shape[2] else pl.program_id(0) * nx
     spots = [(ref, i) for ref in fields for i in range(ref.shape[1])]
 
     for comp in range(three):
@@ -454,16 +476,31 @@
                 part = slice(lane, lane + 128)
                 cols = [ref[comp, i, base + x, :, part] for ref, i in spots]
                 for j in range(columns):
-                    terms = [coef[j * count + i] * cols[i] for i in range(count)]
+                    terms = [coef[j * count + first + i] * c for i, c in enumerate(cols)]
+                    if begun is not None:
+                        terms.append(begun[comp, j, base + x, :, part])
                     while len(terms) > 1:
-                        terms = [a + b for a, b in zip(terms[::2], terms[1::2])]
+                        terms = [sum(terms[k : k + 2][1:], terms[k]) for k in range(0, len(terms), 2)]
                     out[comp, j, x, :, part] = terms[0]
             return 0
 
         lax.fori_loop(0, nx, body, 0, unroll=4)
 
 
-def run_basis(half, coef, fields, columns, keep, target=None):
+def run_partial(half, coef, fields, columns, first):
+    three, _, half_x, nz, ny = fields[0].shape
+    vmem = pl.BlockSpec(memory_space=pltpu.VMEM)
+    return pl.pallas_call(
+        functools.partial(basis_body, 2 * columns, first, False, False),
+        out_shape=in_vmem((three, columns, half_x, nz, ny)),
+        in_specs=[pl.BlockSpec(memory_space=pltpu.SMEM)] + [vmem] * (len(fields) + 1),
+        out_specs=vmem,
+        compiler_params=pltpu.CompilerParams(vmem_limit_bytes=VMEM_LIMIT),
+        name="partial",
+    )(half, *[hold(v) for v in (coef, *fields)])
+
+
+def run_basis(half, coef, fields, columns, keep, target=None, begun=None, first=0):
     three, _, half_x, nz, ny = fields[0].shape
     per = 2
     block = (three, columns, half_x // per, nz, ny)
@@ -472,12 +509,14 @@
     def place(k, h):
         return (0, 0, k + per * (h[0] if keep else 1 - h[0]), 0, 0)
 
+    if begun is not None:
+        fields = (*fields, begun)
     operands = [hold(v) for v in (coef, *fields)]
     specs = [vmem] * len(operands)
     if target is not None:
         operands, specs = operands + [target], specs + [pl.BlockSpec(memory_space=pl.ANY)]
     return pl.pallas_call(
-        functools.partial(basis_body, 2 * columns, target is not None),
+        functools.partial(basis_body, 2 * columns, first, begun is not None, target is not None),
         out_shape=jax.ShapeDtypeStruct((three, columns, 2 * half_x, nz, ny), jnp.float32),
         grid_spec=pltpu.PrefetchScalarGridSpec(
             num_scalar_prefetch=1, grid=(per,), in_specs=specs, out_specs=pl.BlockSpec(block, place)
@@ -551,9 +590,8 @@
     side2 = swap(relay)
     relay, s2, *edge = stage("adjoint_first", s1, q2, faces, coef, wall, relay=early)
     faces = exchange(*edge)
-    side3 = swap(relay)
-    relay, late_keep, late_send = stage("adjoint_last", s2, q2, faces, coef, wall, span=(early, columns), relay=early)
-    side4 = swap(relay)
+    side3 = swap(run_relay(relay, *faces[2:]))
+    late_keep, late_send = stage("adjoint_last", s2, q2, faces, coef, wall, span=(early, columns))
     other_keep = swap(late_send)
     front_keep, front_send = stage("adjoint_last", s2, q2, faces, coef, wall, span=(0, early))
 
@@ -565,7 +603,7 @@
     faces = exchange(*edge)
     h2, *edge = stage("adjoint_first", h1, g2, (*faces, side3), coef, wall)
     faces = exchange(*edge)
-    early_keep, early_send = stage("adjoint_last", h2, g2, (*faces, side4), coef, wall)
+    early_keep, early_send = stage("adjoint_last", h2, g2, (*faces, side3), coef, wall, place=1)
 
     own = (front_keep, front_send, late_keep, late_send)
     base = run_gram(own_gram_body, half, (*own, squares), columns * (columns + 1) // 2, count)
@@ -579,7 +617,8 @@
     raw = all_sum(raw, ("gz",), "gz")
     factor, coef = run_factor(entries, columns, half, raw)
     basis = run_basis(half, coef, (front_keep, late_keep, early_keep, other_keep), columns, True)
-    basis = run_basis(half, coef, (front_send, late_send, early_send, other_send), columns, False, basis)
+    begun = run_partial(half, coef, (front_send, late_send, early_send), columns, 0)
+    basis = run_basis(half, coef, (other_send,), columns, False, basis, begun, columns + early)
     return basis, factor
 
 

time: 146 us -> 147 us (level)
    ppermute x24, waiting for transfers between devices: 18.5 us -> 25.7 us  [shift(): lax.ppermute(value, axis, [(i, (i + amount) % count) for i in range(count)])]
    ppermute x7 -> x6, waiting for transfers between devices: 45 us -> 38.8 us  [swap(): return lax.ppermute(value, 'sa', [(0, 1), (1, 0)])]
    pallas_call x11 -> x13, Pallas kernels: 21.6 us -> 21 us  [the longest x9 17.3 us: run_stage(): pl.pallas_call(functools.partial(stage_body, kind, span, guest, place, bo...]
    ppermute x7 -> x6, starting transfers between devices: 5.91 us -> 5.55 us  [swap(): return lax.ppermute(value, 'sa', [(0, 1), (1, 0)])]
  transfers between devices with their start and end apart: 37 -> 36, of which waited for: 22 -> 24; matrix products, arithmetic and copies ran while one was open for 0% -> 0% of each run, Pallas kernels for 14% -> 14%
where the time goes in v4:
time: 147 us; the launch traced here: 146 us
  waiting for transfers between devices  77.2 us (53%)
  starting transfers between devices  41.8 us (28%)
  Pallas kernels  26.7 us (18%)
    ppermute x6, waiting for transfers between devices, swap(): return lax.ppermute(value, 'sa', [(0, 1), (1, 0)])  38.8 us
    ppermute x24, starting transfers between devices, shift(): lax.ppermute(value, axis, [(i, (i + amount) % count) for i in range(count)])  32.7 us
    ppermute x24, waiting for transfers between devices, shift(): lax.ppermute(value, axis, [(i, (i + amount) % count) for i in range(count)])  25.7 us
    pallas_call x9, Pallas kernels, run_stage(): pl.pallas_call(functools.partial(stage_body, kind, span, guest, place, bo...  17.3 us
    ppermute x6, waiting for transfers between devices, partner(): return lax.ppermute(value, axis, [(i, i ^ mask) for i in range(count)])  12.7 us
    ppermute x6, starting transfers between devices, swap(): return lax.ppermute(value, 'sa', [(0, 1), (1, 0)])  5.55 us
    ppermute x6, starting transfers between devices, partner(): return lax.ppermute(value, axis, [(i, i ^ mask) for i in range(count)])  3.54 us
    pallas_call x2, Pallas kernels, run_basis(): pl.pallas_call(functools.partial(basis_body, 2 * columns, first, begun is...  3.09 us
  transfers between devices with their start and end apart: 36, of which 24 were waited for; matrix products, arithmetic and copies ran while one was open for 0% of the time, Pallas kernels for 14%

profile of v4, /device:TPU:0, one launch (start us, length us, event | category | flops | bytes accessed | tf_op | source)
XLA Modules:
  0.0 146.5 jit_solution(8027245812985483887)
XLA Ops:
  0.7 2.4 %edges.1 = (f32[3,4,32,8,256]{4,3,2,1,0:T(8,128)S(1)}, f32[3,2,32,8,256]{4,3,2,1,0:T(8,128)S(1)}, f32[3,4,2,32,128]{4,3,2,1,0:T(8,128)S(1)}, f32[3,4,2,32,128]{4...) custom-call(f32[3,4,32,8,256]{4,3,2,1,0:T(8,128)} %source.1, s32[1]{0:T(128)} %bitcast.half_ref.refs_0_), custom_call_target="tpu_custom_call" | custom-call | tf_op jit(solution)/shard_map/edges/pallas_call | solution.py:264
  3.1 0.5 collective-permute-start.2
  3.6 2.0 %collective-permute-start.3 = (f32[3,4,2,32,128]{4,3,2,1,0:T(8,128)S(1)}, f32[3,4,2,32,128]{4,3,2,1,0:T(8,128)S(1)}, u32[]{:S(2)}, u32[]{:S(2)}) collective-permute-start(f32[3,4,2,32,128]{4,3,2,1,0:T(8,128)S(1)} %get-tuple-element.56), channel_id=1, source_target_pairs={{0,6},{2,0},{4,2},{6,4},{1,7},{3,1},{5,3},{7,5},{8,14},{10,8},{12,... | collective-permute-start | bytes 1179656 | tf_op jit(solution)/shard_map/ppermute | solution.py:532
  5.7 2.3 %collective-permute-start = (f32[3,4,8,256]{3,2,1,0:T(8,128)S(1)}, f32[3,4,8,256]{3,2,1,0:T(8,128)S(1)}, u32[]{:S(2)}, u32[]{:S(2)}) collective-permute-start(f32[3,4,8,256]{3,2,1,0:T(8,128)S(1)} %get-tuple-element.53), channel_id=1, source_target_pairs={{0,8},{8,16},{16,24},{24,0},{1,9},{9,17},{17,25},{25,1},{2,10},{10... | collective-permute-start | bytes 294920 | tf_op jit(solution)/shard_map/ppermute | solution.py:532
  8.0 2.0 %collective-permute-start.1 = (f32[3,4,8,256]{3,2,1,0:T(8,128)S(1)}, f32[3,4,8,256]{3,2,1,0:T(8,128)S(1)}, u32[]{:S(2)}, u32[]{:S(2)}) collective-permute-start(f32[3,4,8,256]{3,2,1,0:T(8,128)S(1)} %get-tuple-element.54), channel_id=1, source_target_pairs={{0,24},{8,0},{16,8},{24,16},{1,25},{9,1},{17,9},{25,17},{2,26},{10... | collective-permute-start | bytes 294920 | tf_op jit(solution)/shard_map/ppermute | solution.py:532
  10.2 3.3 %collective-permute-done.refs_1_ = f32[3,4,8,256]{3,2,1,0:T(8,128)S(1)} collective-permute-done((f32[3,4,8,256]{3,2,1,0:T(8,128)S(1)}, f32[3,4,8,256]{3,2,1,0:T(8,128)S(1)}, u32[]{:S(2)}, u32[]{:S(2)}) %collective-permute-start) | collective-permute-done | bytes 98336 | tf_op jit(solution)/shard_map/ppermute | solution.py:532
  13.5 0.9 collective-permute-done.1.refs_2_
  14.4 0.7 collective-permute-done.3.refs_4_
  15.1 2.6 %shard_map.50 = (f32[2,3,2,8,256]{4,3,2,1,0:T(8,128)S(1)}, f32[3,4,32,8,256]{4,3,2,1,0:T(8,128)S(1)}, f32[3,4,2,32,128]{4,3,2,1,0:T(8,128)S(1)}, f32[3,4,2,32,12...) custom-call(f32[3,4,32,8,256]{4,3,2,1,0:T(8,128)S(1)} %get-tuple-element.52.refs_0_.refs_1_, ...), custom_call_target="tpu_custom_call" | custom-call | tf_op jit(solution)/shard_map/pallas_call | solution.py:202
  17.8 2.1 %collective-permute-start.7 = (f32[3,4,2,32,128]{4,3,2,1,0:T(8,128)S(1)}, f32[3,4,2,32,128]{4,3,2,1,0:T(8,128)S(1)}, u32[]{:S(2)}, u32[]{:S(2)}) collective-permute-start(f32[3,4,2,32,128]{4,3,2,1,0:T(8,128)S(1)} %get-tuple-element.63), channel_id=1, source_target_pairs={{0,6},{2,0},{4,2},{6,4},{1,7},{3,1},{5,3},{7,5},{8,14},{10,8},{12,... | collective-permute-start | bytes 1179656 | tf_op jit(solution)/shard_map/ppermute | solution.py:532
  19.9 1.3 collective-permute-start.16
  21.2 1.6 %collective-permute-start.4 = (f32[3,4,8,256]{3,2,1,0:T(8,128)S(1)}, f32[3,4,8,256]{3,2,1,0:T(8,128)S(1)}, u32[]{:S(2)}, u32[]{:S(2)}) collective-permute-start(f32[3,4,8,256]{3,2,1,0:T(8,128)S(1)} %get-tuple-element.60), channel_id=1, source_target_pairs={{0,8},{8,16},{16,24},{24,0},{1,9},{9,17},{17,25},{25,1},{2,10},{10... | collective-permute-start | bytes 294920 | tf_op jit(solution)/shard_map/ppermute | solution.py:532
  22.8 2.2 %collective-permute-start.5 = (f32[3,4,8,256]{3,2,1,0:T(8,128)S(1)}, f32[3,4,8,256]{3,2,1,0:T(8,128)S(1)}, u32[]{:S(2)}, u32[]{:S(2)}) collective-permute-start(f32[3,4,8,256]{3,2,1,0:T(8,128)S(1)} %get-tuple-element.61), channel_id=1, source_target_pairs={{0,24},{8,0},{16,8},{24,16},{1,25},{9,1},{17,9},{25,17},{2,26},{10... | collective-permute-start | bytes 294920 | tf_op jit(solution)/shard_map/ppermute | solution.py:532
  25.0 3.5 %collective-permute-done.4.refs_2_ = f32[3,4,8,256]{3,2,1,0:T(8,128)S(1)} collective-permute-done((f32[3,4,8,256]{3,2,1,0:T(8,128)S(1)}, f32[3,4,8,256]{3,2,1,0:T(8,128)S(1)}, u32[]{:S(2)}, u32[]{:S(2)}) %collective-permute-start.4) | collective-permute-done | bytes 98336 | tf_op jit(solution)/shard_map/ppermute | solution.py:532
  29.1 4.9 %shard_map.51 = (f32[2,3,2,8,256]{4,3,2,1,0:T(8,128)S(1)}, f32[3,4,32,8,256]{4,3,2,1,0:T(8,128)S(1)}, f32[3,4,32,8,256]{4,3,2,1,0:T(8,128)S(1)}, f32[3,4,2,32,12...) custom-call(f32[3,4,32,8,256]{4,3,2,1,0:T(8,128)S(1)} %get-tuple-ele, ...), custom_call_target="tpu_custom_call" | custom-call | tf_op jit(solution)/shard_map/pallas_call | solution.py:202
  34.0 0.6 collective-permute-start.10
  34.6 1.7 %collective-permute-start.11 = (f32[3,4,2,32,128]{4,3,2,1,0:T(8,128)S(1)}, f32[3,4,2,32,128]{4,3,2,1,0:T(8,128)S(1)}, u32[]{:S(2)}, u32[]{:S(2)}) collective-permute-start(f32[3,4,2,32,128]{4,3,2,1,0:T(8,128)S(1)} %get-tuple-element.69), channel_id=1, source_target_pairs={{0,6},{2,0},{4,2},{6,4},{1,7},{3,1},{5,3},{7,5},{8,14},{10,8},{12,... | collective-permute-start | bytes 1179656 | tf_op jit(solution)/shard_map/ppermute | solution.py:532
  36.3 0.9 collective-permute-start.8
  37.1 3.0 %collective-permute-start.9 = (f32[3,4,8,256]{3,2,1,0:T(8,128)S(1)}, f32[3,4,8,256]{3,2,1,0:T(8,128)S(1)}, u32[]{:S(2)}, u32[]{:S(2)}) collective-permute-start(f32[3,4,8,256]{3,2,1,0:T(8,128)S(1)} %get-tuple-element.67), channel_id=1, source_target_pairs={{0,24},{8,0},{16,8},{24,16},{1,25},{9,1},{17,9},{25,17},{2,26},{10... | collective-permute-start | bytes 294920 | tf_op jit(solution)/shard_map/ppermute | solution.py:532
  40.1 3.7 %collective-permute-done.8.refs_2_ = f32[3,4,8,256]{3,2,1,0:T(8,128)S(1)} collective-permute-done((f32[3,4,8,256]{3,2,1,0:T(8,128)S(1)}, f32[3,4,8,256]{3,2,1,0:T(8,128)S(1)}, u32[]{:S(2)}, u32[]{:S(2)}) %collective-permute-start.8) | collective-permute-done | bytes 98336 | tf_op jit(solution)/shard_map/ppermute | solution.py:532
  43.9 1.1 collective-permute-done.11.refs_5_
  45.1 2.7 %shard_map.52 = (f32[2,3,2,8,256]{4,3,2,1,0:T(8,128)S(1)}, f32[3,4,32,8,256]{4,3,2,1,0:T(8,128)S(1)}, f32[3,4,2,32,128]{4,3,2,1,0:T(8,128)S(1)}, f32[3,4,2,32,12...) custom-call(f32[3,4,32,8,256]{4,3,2,1,0:T(8,128)S(1)} %get-tuple-element.64.refs_0_, ...), custom_call_target="tpu_custom_call" | custom-call | tf_op jit(solution)/shard_map/pallas_call | solution.py:202
  47.8 1.0 collective-permute-start.14
  48.8 1.3 collective-permute-start.15
  50.1 0.3 collective-permute-start.12
  50.4 3.5 %collective-permute-start.13 = (f32[3,4,8,256]{3,2,1,0:T(8,128)S(1)}, f32[3,4,8,256]{3,2,1,0:T(8,128)S(1)}, u32[]{:S(2)}, u32[]{:S(2)}) collective-permute-start(f32[3,4,8,256]{3,2,1,0:T(8,128)S(1)} %get-tuple-element.72), channel_id=1, source_target_pairs={{0,24},{8,0},{16,8},{24,16},{1,25},{9,1},{17,9},{25,17},{2,26},{10... | collective-permute-start | bytes 294920 | tf_op jit(solution)/shard_map/ppermute | solution.py:532
  53.9 3.4 %collective-permute-done.12.refs_3_.xlo = f32[3,4,8,256]{3,2,1,0:T(8,128)S(1)} collective-permute-done((f32[3,4,8,256]{3,2,1,0:T(8,128)S(1)}, f32[3,4,8,256]{3,2,1,0:T(8,128)S(1)}, u32[]{:S(2)}, u32[]{:S(2)}) %collective-permute-start.12) | collective-permute-done | bytes 98336 | tf_op jit(solution)/shard_map/ppermute | solution.py:532
  57.3 0.8 collective-permute-done.14.refs_5_
  58.1 0.4 collective-permute-done.15.refs_6_
  58.5 0.7 shard_map.54
  59.7 0.9 collective-permute-start.18
  60.6 1.0 collective-permute-start.19
  61.5 1.8 %collective-permute-start.17 = (f32[2,3,2,8,256]{4,3,2,1,0:T(8,128)S(1)}, f32[2,3,2,8,256]{4,3,2,1,0:T(8,128)S(1)}, u32[]{:S(2)}, u32[]{:S(2)}) collective-permute-start(f32[2,3,2,8,256]{4,3,2,1,0:T(8,128)S(1)} %get-tuple-element.80), channel_id=1, source_target_pairs={{0,1},{1,0},{2,3},{3,2},{4,5},{5,4},{6,7},{7,6},{8,9},{9,8},{10,11... | collective-permute-start | bytes 294920 | tf_op jit(solution)/shard_map/ppermute | solution.py:568
  63.3 18.5 %collective-permute-done.17.refs_1_ = f32[2,3,2,8,256]{4,3,2,1,0:T(8,128)S(1)} collective-permute-done((f32[2,3,2,8,256]{4,3,2,1,0:T(8,128)S(1)}, f32[2,3,2,8,256]{4,3,2,1,0:T(8,128)S(1)}, u32[]{:S(2)}, u32[]{:S(2)}) %collective-permute-start.17) | collective-permute-done | bytes 98336 | tf_op jit(solution)/shard_map/ppermute | solution.py:568
  81.8 1.3 shard_map.55
  83.3 1.6 %collective-permute-start.22 = (f32[3,2,2,32,128]{4,3,2,1,0:T(8,128)S(1)}, f32[3,2,2,32,128]{4,3,2,1,0:T(8,128)S(1)}, u32[]{:S(2)}, u32[]{:S(2)}) collective-permute-start(f32[3,2,2,32,128]{4,3,2,1,0:T(8,128)S(1)} %get-tuple-element.86), channel_id=1, source_target_pairs={{0,6},{2,0},{4,2},{6,4},{1,7},{3,1},{5,3},{7,5},{8,14},{10,8},{12,... | collective-permute-start | bytes 589832 | tf_op jit(solution)/shard_map/ppermute | solution.py:532
  85.0 1.9 %collective-permute-start.20 = (f32[2,3,2,8,256]{4,3,2,1,0:T(8,128)S(1)}, f32[2,3,2,8,256]{4,3,2,1,0:T(8,128)S(1)}, u32[]{:S(2)}, u32[]{:S(2)}) collective-permute-start(f32[2,3,2,8,256]{4,3,2,1,0:T(8,128)S(1)} %get-tuple-element.84), channel_id=1, source_target_pairs={{0,1},{1,0},{2,3},{3,2},{4,5},{5,4},{6,7},{7,6},{8,9},{9,8},{10,11... | collective-permute-start | bytes 294920 | tf_op jit(solution)/shard_map/ppermute | solution.py:568
  87.1 20.3 %collective-permute-done.20.refs_2_ = f32[2,3,2,8,256]{4,3,2,1,0:T(8,128)S(1)} collective-permute-done((f32[2,3,2,8,256]{4,3,2,1,0:T(8,128)S(1)}, f32[2,3,2,8,256]{4,3,2,1,0:T(8,128)S(1)}, u32[]{:S(2)}, u32[]{:S(2)}) %collective-permute-start.20) | collective-permute-done | bytes 98336 | tf_op jit(solution)/shard_map/ppermute | solution.py:568
  107.4 2.3 %shard_map.56 = (f32[3,2,32,8,256]{4,3,2,1,0:T(8,128)S(1)}, f32[3,2,32,8,256]{4,3,2,1,0:T(8,128)S(1)}, f32[3,2,2,32,128]{4,3,2,1,0:T(8,128)S(1)}, f32[3,2,2,32,128]{4,3,2,1,0:T(8,128)S(1)}) custom-call(f32[3,2,32,8,256]{4,3,2,1,0:T(8,128)S(1)} %get-tuple-element.83.refs_0_, f32[3,2,32,8,256]{4,3,2,1,0:T(8,128)S(1)} %collective-permute-done.16.field.refs_0_.refs_1_, ...), custom_call_target="tpu_custom_call" | custom-call | tf_op jit(solution)/shard_map/pallas_call | solution.py:202
  109.8 1.7 %collective-permute-start.25 = (f32[3,2,2,32,128]{4,3,2,1,0:T(8,128)S(1)}, f32[3,2,2,32,128]{4,3,2,1,0:T(8,128)S(1)}, u32[]{:S(2)}, u32[]{:S(2)}) collective-permute-start(f32[3,2,2,32,128]{4,3,2,1,0:T(8,128)S(1)} %get-tuple-element.91), channel_id=1, source_target_pairs={{0,6},{2,0},{4,2},{6,4},{1,7},{3,1},{5,3},{7,5},{8,14},{10,8},{12,... | collective-permute-start | bytes 589832 | tf_op jit(solution)/shard_map/ppermute | solution.py:532
  111.5 3.8 %collective-permute-done.24.refs_3_ = f32[3,2,2,32,128]{4,3,2,1,0:T(8,128)S(1)} collective-permute-done((f32[3,2,2,32,128]{4,3,2,1,0:T(8,128)S(1)}, f32[3,2,2,32,128]{4,3,2,1,0:T(8,128)S(1)}, u32[]{:S(2)}, u32[]{:S(2)}) %collective-permute-start.24) | collective-permute-done | bytes 196640 | tf_op jit(solution)/shard_map/ppermute | solution.py:532
  115.3 0.5 collective-permute-done.25.refs_4_
  115.9 1.4 shard_map.57
  117.2 1.0 collective-permute-start.26
  118.2 1.0 collective-permute-start.27
  119.3 0.7 shard_map.53
  120.0 0.7 shard_map.59.base
  120.7 2.3 %collective-permute-done.26.refs_4_ = f32[3,2,2,32,128]{4,3,2,1,0:T(8,128)S(1)} collective-permute-done((f32[3,2,2,32,128]{4,3,2,1,0:T(8,128)S(1)}, f32[3,2,2,32,128]{4,3,2,1,0:T(8,128)S(1)}, u32[]{:S(2)}, u32[]{:S(2)}) %collective-permute-start.26) | collective-permute-done | bytes 196640 | tf_op jit(solution)/shard_map/ppermute | solution.py:532
  123.0 0.5 collective-permute-done.27.refs_5_
  123.5 0.7 shard_map.58
  124.3 0.8 shard_map.60
  125.1 3.6 %collective-permute-done.29 = f32[8,128]{1,0:T(8,128)S(1)} collective-permute-done((f32[8,128]{1,0:T(8,128)S(1)}, f32[8,128]{1,0:T(8,128)S(1)}, u32[]{:S(2)}, u32[]{:S(2)}) %collective-permute-start.29) | collective-permute-done | bytes 4128 | tf_op jit(solution)/shard_map/ppermute | solution.py:546
  128.8 0.3 collective-permute-start.30
  129.1 3.3 %collective-permute-done.30 = f32[8,128]{1,0:T(8,128)S(1)} collective-permute-done((f32[8,128]{1,0:T(8,128)S(1)}, f32[8,128]{1,0:T(8,128)S(1)}, u32[]{:S(2)}, u32[]{:S(2)}) %collective-permute-start.30) | collective-permute-done | bytes 4128 | tf_op jit(solution)/shard_map/ppermute | solution.py:546
  132.4 1.3 collective-permute-start.31
  133.7 3.2 %collective-permute-done.31 = f32[8,128]{1,0:T(8,128)S(1)} collective-permute-done((f32[8,128]{1,0:T(8,128)S(1)}, f32[8,128]{1,0:T(8,128)S(1)}, u32[]{:S(2)}, u32[]{:S(2)}) %collective-permute-start.31) | collective-permute-done | bytes 4128 | tf_op jit(solution)/shard_map/ppermute | solution.py:546
  136.9 1.4 collective-permute-start.33
  138.3 0.4 collective-permute-start.34
  138.8 1.7 %collective-permute-done.33 = f32[8,128]{1,0:T(8,128)S(1)} collective-permute-done((f32[8,128]{1,0:T(8,128)S(1)}, f32[8,128]{1,0:T(8,128)S(1)}, u32[]{:S(2)}, u32[]{:S(2)}) %collective-permute-start.33) | collective-permute-done | bytes 4128 | tf_op jit(solution)/shard_map/ppermute | solution.py:546
  140.5 0.9 collective-permute-done.34
  141.4 1.4 factor.1
  142.7 1.8 %basis.2.refs_2_ = f32[3,4,32,8,256]{4,3,2,1,0:T(8,128)} custom-call(s32[1]{0:T(128)} %bitcast.half_ref.refs_0_, f32[32,8,128]{2,1,0:T(8,128)S(1)} %get-tuple-element.99.coef, f32[3,2,16,8,256]{4,3,2,1,0:T(8,128)S(1)} %get-tuple-element.75.front_keep.fk.refs_0_, f32[3,2,16,8,256]{4,3,2,1,0:T(8,128)S(1)} %get-tuple-element.100.late_keep.lk.refs_1_, ...), custom_call_target="tpu_custom_call" | custom-call | tf_op jit(solution)/shard_map/basis/pallas_call | solution.py:518
  144.5 0.7 partial.1.refs_1_
  145.2 1.3 basis.3
  (35 shorter events, 2.1 us)
Async XLA Ops:
  0.6 9.4 %copy-start.1 = (f32[256]{0:T(256)S(1)}, f32[256]{0:T(256)}, u32[]{:S(2)}) copy-start(f32[256]{0:T(256)} %param.4) | copy-start | bytes 3076
  0.6 9.3 %copy-start = (f32[256,256]{1,0:T(8,128)S(1)}, f32[256,256]{1,0:T(8,128)}, u32[]{:S(2)}) copy-start(f32[256,256]{1,0:T(8,128)} %wall_solve.1) | copy-start | bytes 786436
  3.1 11.3 %collective-permute-start.2 = (f32[3,4,2,32,128]{4,3,2,1,0:T(8,128)S(1)}, f32[3,4,2,32,128]{4,3,2,1,0:T(8,128)S(1)}, u32[]{:S(2)}, u32[]{:S(2)}) collective-permute-start(f32[3,4,2,32,128]{4,3,2,1,0:T(8,128)S(1)} %get-tuple-element.55), channel_id=1, source_target_pairs={{0,2},{2,4},{4,6},{6,0},{1,3},{3,5},{5,7},{7,1},{8,10},{10,12},{12... | collective-permute-start | bytes 1179656 | tf_op jit(solution)/shard_map/ppermute | solution.py:532
  3.6 11.4 %collective-permute-start.3 = (f32[3,4,2,32,128]{4,3,2,1,0:T(8,128)S(1)}, f32[3,4,2,32,128]{4,3,2,1,0:T(8,128)S(1)}, u32[]{:S(2)}, u32[]{:S(2)}) collective-permute-start(f32[3,4,2,32,128]{4,3,2,1,0:T(8,128)S(1)} %get-tuple-element.56), channel_id=1, source_target_pairs={{0,6},{2,0},{4,2},{6,4},{1,7},{3,1},{5,3},{7,5},{8,14},{10,8},{12,... | collective-permute-start | bytes 1179656 | tf_op jit(solution)/shard_map/ppermute | solution.py:532
  5.7 7.8 %collective-permute-start = (f32[3,4,8,256]{3,2,1,0:T(8,128)S(1)}, f32[3,4,8,256]{3,2,1,0:T(8,128)S(1)}, u32[]{:S(2)}, u32[]{:S(2)}) collective-permute-start(f32[3,4,8,256]{3,2,1,0:T(8,128)S(1)} %get-tuple-element.53), channel_id=1, source_target_pairs={{0,8},{8,16},{16,24},{24,0},{1,9},{9,17},{17,25},{25,1},{2,10},{10... | collective-permute-start | bytes 294920 | tf_op jit(solution)/shard_map/ppermute | solution.py:532
  8.0 6.4 %collective-permute-start.1 = (f32[3,4,8,256]{3,2,1,0:T(8,128)S(1)}, f32[3,4,8,256]{3,2,1,0:T(8,128)S(1)}, u32[]{:S(2)}, u32[]{:S(2)}) collective-permute-start(f32[3,4,8,256]{3,2,1,0:T(8,128)S(1)} %get-tuple-element.54), channel_id=1, source_target_pairs={{0,24},{8,0},{16,8},{24,16},{1,25},{9,1},{17,9},{25,17},{2,26},{10... | collective-permute-start | bytes 294920 | tf_op jit(solution)/shard_map/ppermute | solution.py:532
  17.7 11.2 %collective-permute-start.6 = (f32[3,4,2,32,128]{4,3,2,1,0:T(8,128)S(1)}, f32[3,4,2,32,128]{4,3,2,1,0:T(8,128)S(1)}, u32[]{:S(2)}, u32[]{:S(2)}) collective-permute-start(f32[3,4,2,32,128]{4,3,2,1,0:T(8,128)S(1)} %get-tuple-element.62), channel_id=1, source_target_pairs={{0,2},{2,4},{4,6},{6,0},{1,3},{3,5},{5,7},{7,1},{8,10},{10,12},{12... | collective-permute-start | bytes 1179656 | tf_op jit(solution)/shard_map/ppermute | solution.py:532
  17.8 11.3 %collective-permute-start.7 = (f32[3,4,2,32,128]{4,3,2,1,0:T(8,128)S(1)}, f32[3,4,2,32,128]{4,3,2,1,0:T(8,128)S(1)}, u32[]{:S(2)}, u32[]{:S(2)}) collective-permute-start(f32[3,4,2,32,128]{4,3,2,1,0:T(8,128)S(1)} %get-tuple-element.63), channel_id=1, source_target_pairs={{0,6},{2,0},{4,2},{6,4},{1,7},{3,1},{5,3},{7,5},{8,14},{10,8},{12,... | collective-permute-start | bytes 1179656 | tf_op jit(solution)/shard_map/ppermute | solution.py:532
  19.9 39.6 %collective-permute-start.16 = (f32[3,2,32,8,256]{4,3,2,1,0:T(8,128)S(1)}, f32[3,2,32,8,256]{4,3,2,1,0:T(8,128)S(1)}, u32[]{:S(2)}, u32[]{:S(2)}) collective-permute-start(f32[3,2,32,8,256]{4,3,2,1,0:T(8,128)S(1)} %get-tuple-element.79), channel_id=1, source_target_pairs={{0,1},{1,0},{2,3},{3,2},{4,5},{5,4},{6,7},{7,6},{8,9},{9,8},{10,11... | collective-permute-start | bytes 4718600 | tf_op jit(solution)/shard_map/ppermute | solution.py:568
  21.2 7.4 %collective-permute-start.4 = (f32[3,4,8,256]{3,2,1,0:T(8,128)S(1)}, f32[3,4,8,256]{3,2,1,0:T(8,128)S(1)}, u32[]{:S(2)}, u32[]{:S(2)}) collective-permute-start(f32[3,4,8,256]{3,2,1,0:T(8,128)S(1)} %get-tuple-element.60), channel_id=1, source_target_pairs={{0,8},{8,16},{16,24},{24,0},{1,9},{9,17},{17,25},{25,1},{2,10},{10... | collective-permute-start | bytes 294920 | tf_op jit(solution)/shard_map/ppermute | solution.py:532
  22.8 6.1 %collective-permute-start.5 = (f32[3,4,8,256]{3,2,1,0:T(8,128)S(1)}, f32[3,4,8,256]{3,2,1,0:T(8,128)S(1)}, u32[]{:S(2)}, u32[]{:S(2)}) collective-permute-start(f32[3,4,8,256]{3,2,1,0:T(8,128)S(1)} %get-tuple-element.61), channel_id=1, source_target_pairs={{0,24},{8,0},{16,8},{24,16},{1,25},{9,1},{17,9},{25,17},{2,26},{10... | collective-permute-start | bytes 294920 | tf_op jit(solution)/shard_map/ppermute | solution.py:532
  34.0 10.0 %collective-permute-start.10 = (f32[3,4,2,32,128]{4,3,2,1,0:T(8,128)S(1)}, f32[3,4,2,32,128]{4,3,2,1,0:T(8,128)S(1)}, u32[]{:S(2)}, u32[]{:S(2)}) collective-permute-start(f32[3,4,2,32,128]{4,3,2,1,0:T(8,128)S(1)} %get-tuple-element.68), channel_id=1, source_target_pairs={{0,2},{2,4},{4,6},{6,0},{1,3},{3,5},{5,7},{7,1},{8,10},{10,12},{12... | collective-permute-start | bytes 1179656 | tf_op jit(solution)/shard_map/ppermute | solution.py:532
  34.6 10.5 %collective-permute-start.11 = (f32[3,4,2,32,128]{4,3,2,1,0:T(8,128)S(1)}, f32[3,4,2,32,128]{4,3,2,1,0:T(8,128)S(1)}, u32[]{:S(2)}, u32[]{:S(2)}) collective-permute-start(f32[3,4,2,32,128]{4,3,2,1,0:T(8,128)S(1)} %get-tuple-element.69), channel_id=1, source_target_pairs={{0,6},{2,0},{4,2},{6,4},{1,7},{3,1},{5,3},{7,5},{8,14},{10,8},{12,... | collective-permute-start | bytes 1179656 | tf_op jit(solution)/shard_map/ppermute | solution.py:532
  36.3 7.5 %collective-permute-start.8 = (f32[3,4,8,256]{3,2,1,0:T(8,128)S(1)}, f32[3,4,8,256]{3,2,1,0:T(8,128)S(1)}, u32[]{:S(2)}, u32[]{:S(2)}) collective-permute-start(f32[3,4,8,256]{3,2,1,0:T(8,128)S(1)} %get-tuple-element.66), channel_id=1, source_target_pairs={{0,8},{8,16},{16,24},{24,0},{1,9},{9,17},{17,25},{25,1},{2,10},{10... | collective-permute-start | bytes 294920 | tf_op jit(solution)/shard_map/ppermute | solution.py:532
  37.1 6.7 %collective-permute-start.9 = (f32[3,4,8,256]{3,2,1,0:T(8,128)S(1)}, f32[3,4,8,256]{3,2,1,0:T(8,128)S(1)}, u32[]{:S(2)}, u32[]{:S(2)}) collective-permute-start(f32[3,4,8,256]{3,2,1,0:T(8,128)S(1)} %get-tuple-element.67), channel_id=1, source_target_pairs={{0,24},{8,0},{16,8},{24,16},{1,25},{9,1},{17,9},{25,17},{2,26},{10... | collective-permute-start | bytes 294920 | tf_op jit(solution)/shard_map/ppermute | solution.py:532
  47.8 10.3 %collective-permute-start.14 = (f32[3,4,2,32,128]{4,3,2,1,0:T(8,128)S(1)}, f32[3,4,2,32,128]{4,3,2,1,0:T(8,128)S(1)}, u32[]{:S(2)}, u32[]{:S(2)}) collective-permute-start(f32[3,4,2,32,128]{4,3,2,1,0:T(8,128)S(1)} %get-tuple-element.73), channel_id=1, source_target_pairs={{0,2},{2,4},{4,6},{6,0},{1,3},{3,5},{5,7},{7,1},{8,10},{10,12},{12... | collective-permute-start | bytes 1179656 | tf_op jit(solution)/shard_map/ppermute | solution.py:532
  48.8 9.8 %collective-permute-start.15 = (f32[3,4,2,32,128]{4,3,2,1,0:T(8,128)S(1)}, f32[3,4,2,32,128]{4,3,2,1,0:T(8,128)S(1)}, u32[]{:S(2)}, u32[]{:S(2)}) collective-permute-start(f32[3,4,2,32,128]{4,3,2,1,0:T(8,128)S(1)} %get-tuple-element.74), channel_id=1, source_target_pairs={{0,6},{2,0},{4,2},{6,4},{1,7},{3,1},{5,3},{7,5},{8,14},{10,8},{12,... | collective-permute-start | bytes 1179656 | tf_op jit(solution)/shard_map/ppermute | solution.py:532
  50.1 7.2 %collective-permute-start.12 = (f32[3,4,8,256]{3,2,1,0:T(8,128)S(1)}, f32[3,4,8,256]{3,2,1,0:T(8,128)S(1)}, u32[]{:S(2)}, u32[]{:S(2)}) collective-permute-start(f32[3,4,8,256]{3,2,1,0:T(8,128)S(1)} %get-tuple-element.71), channel_id=1, source_target_pairs={{0,8},{8,16},{16,24},{24,0},{1,9},{9,17},{17,25},{25,1},{2,10},{10... | collective-permute-start | bytes 294920 | tf_op jit(solution)/shard_map/ppermute | solution.py:532
  50.4 6.9 %collective-permute-start.13 = (f32[3,4,8,256]{3,2,1,0:T(8,128)S(1)}, f32[3,4,8,256]{3,2,1,0:T(8,128)S(1)}, u32[]{:S(2)}, u32[]{:S(2)}) collective-permute-start(f32[3,4,8,256]{3,2,1,0:T(8,128)S(1)} %get-tuple-element.72), channel_id=1, source_target_pairs={{0,24},{8,0},{16,8},{24,16},{1,25},{9,1},{17,9},{25,17},{2,26},{10... | collective-permute-start | bytes 294920 | tf_op jit(solution)/shard_map/ppermute | solution.py:532
  59.2 25.7 %collective-permute-start.28 = (f32[3,2,16,8,256]{4,3,2,1,0:T(8,128)S(1)}, f32[3,2,16,8,256]{4,3,2,1,0:T(8,128)S(1)}, u32[]{:S(2)}, u32[]{:S(2)}) collective-permute-start(f32[3,2,16,8,256]{4,3,2,1,0:T(8,128)S(1)} %get-tuple-element.78.late_send.ls.refs_1_), channel_id=1, source_target_pairs={{0,1},{1,0},{2,3},{3,2},{4,5},{5,4},{6,7},{7,6},{8,9},{9,8},{10,11... | collective-permute-start | bytes 2359304 | tf_op jit(solution)/shard_map/ppermute | solution.py:568
  59.7 22.1 %collective-permute-start.18 = (f32[3,2,2,32,128]{4,3,2,1,0:T(8,128)S(1)}, f32[3,2,2,32,128]{4,3,2,1,0:T(8,128)S(1)}, u32[]{:S(2)}, u32[]{:S(2)}) collective-permute-start(f32[3,2,2,32,128]{4,3,2,1,0:T(8,128)S(1)} %get-tuple-element.81), channel_id=1, source_target_pairs={{0,2},{2,4},{4,6},{6,0},{1,3},{3,5},{5,7},{7,1},{8,10},{10,12},{12... | collective-permute-start | bytes 589832 | tf_op jit(solution)/shard_map/ppermute | solution.py:532
  60.6 21.2 %collective-permute-start.19 = (f32[3,2,2,32,128]{4,3,2,1,0:T(8,128)S(1)}, f32[3,2,2,32,128]{4,3,2,1,0:T(8,128)S(1)}, u32[]{:S(2)}, u32[]{:S(2)}) collective-permute-start(f32[3,2,2,32,128]{4,3,2,1,0:T(8,128)S(1)} %get-tuple-element.82), channel_id=1, source_target_pairs={{0,6},{2,0},{4,2},{6,4},{1,7},{3,1},{5,3},{7,5},{8,14},{10,8},{12,... | collective-permute-start | bytes 589832 | tf_op jit(solution)/shard_map/ppermute | solution.py:532
  61.5 20.3 %collective-permute-start.17 = (f32[2,3,2,8,256]{4,3,2,1,0:T(8,128)S(1)}, f32[2,3,2,8,256]{4,3,2,1,0:T(8,128)S(1)}, u32[]{:S(2)}, u32[]{:S(2)}) collective-permute-start(f32[2,3,2,8,256]{4,3,2,1,0:T(8,128)S(1)} %get-tuple-element.80), channel_id=1, source_target_pairs={{0,1},{1,0},{2,3},{3,2},{4,5},{5,4},{6,7},{7,6},{8,9},{9,8},{10,11... | collective-permute-start | bytes 294920 | tf_op jit(solution)/shard_map/ppermute | solution.py:568
  83.1 24.3 %collective-permute-start.21 = (f32[3,2,2,32,128]{4,3,2,1,0:T(8,128)S(1)}, f32[3,2,2,32,128]{4,3,2,1,0:T(8,128)S(1)}, u32[]{:S(2)}, u32[]{:S(2)}) collective-permute-start(f32[3,2,2,32,128]{4,3,2,1,0:T(8,128)S(1)} %get-tuple-element.85), channel_id=1, source_target_pairs={{0,2},{2,4},{4,6},{6,0},{1,3},{3,5},{5,7},{7,1},{8,10},{10,12},{12... | collective-permute-start | bytes 589832 | tf_op jit(solution)/shard_map/ppermute | solution.py:532
  83.3 24.2 %collective-permute-start.22 = (f32[3,2,2,32,128]{4,3,2,1,0:T(8,128)S(1)}, f32[3,2,2,32,128]{4,3,2,1,0:T(8,128)S(1)}, u32[]{:S(2)}, u32[]{:S(2)}) collective-permute-start(f32[3,2,2,32,128]{4,3,2,1,0:T(8,128)S(1)} %get-tuple-element.86), channel_id=1, source_target_pairs={{0,6},{2,0},{4,2},{6,4},{1,7},{3,1},{5,3},{7,5},{8,14},{10,8},{12,... | collective-permute-start | bytes 589832 | tf_op jit(solution)/shard_map/ppermute | solution.py:532
  84.9 60.3 %collective-permute-start.35 = (f32[3,2,16,8,256]{4,3,2,1,0:T(8,128)S(1)}, f32[3,2,16,8,256]{4,3,2,1,0:T(8,128)S(1)}, u32[]{:S(2)}, u32[]{:S(2)}) collective-permute-start(f32[3,2,16,8,256]{4,3,2,1,0:T(8,128)S(1)} %get-tuple-element.100.late_keep.lk.refs_1_), channel_id=1, source_target_pairs={{0,1},{1,0},{2,3},{3,2},{4,5},{5,4},{6,7},{7,6},{8,9},{9,8},{10,11... | collective-permute-start | bytes 2359304 | tf_op jit(solution)/shard_map/ppermute | solution.py:568
  85.0 22.4 %collective-permute-start.20 = (f32[2,3,2,8,256]{4,3,2,1,0:T(8,128)S(1)}, f32[2,3,2,8,256]{4,3,2,1,0:T(8,128)S(1)}, u32[]{:S(2)}, u32[]{:S(2)}) collective-permute-start(f32[2,3,2,8,256]{4,3,2,1,0:T(8,128)S(1)} %get-tuple-element.84), channel_id=1, source_target_pairs={{0,1},{1,0},{2,3},{3,2},{4,5},{5,4},{6,7},{7,6},{8,9},{9,8},{10,11... | collective-permute-start | bytes 294920 | tf_op jit(solution)/shard_map/ppermute | solution.py:568
  86.9 24.6 %collective-permute-start.23 = (f32[4,3,2,8,256]{4,3,2,1,0:T(8,128)S(1)}, f32[4,3,2,8,256]{4,3,2,1,0:T(8,128)S(1)}, u32[]{:S(2)}, u32[]{:S(2)}) collective-permute-start(f32[4,3,2,8,256]{4,3,2,1,0:T(8,128)S(1)} %relay.1), channel_id=1, source_target_pairs={{0,1},{1,0},{2,3},{3,2},{4,5},{5,4},{6,7},{7,6},{8,9},{9,8},{10,11... | collective-permute-start | bytes 589832 | tf_op jit(solution)/shard_map/ppermute | solution.py:568
  109.7 5.6 %collective-permute-start.24 = (f32[3,2,2,32,128]{4,3,2,1,0:T(8,128)S(1)}, f32[3,2,2,32,128]{4,3,2,1,0:T(8,128)S(1)}, u32[]{:S(2)}, u32[]{:S(2)}) collective-permute-start(f32[3,2,2,32,128]{4,3,2,1,0:T(8,128)S(1)} %get-tuple-element.90), channel_id=1, source_target_pairs={{0,2},{2,4},{4,6},{6,0},{1,3},{3,5},{5,7},{7,1},{8,10},{10,12},{12... | collective-permute-start | bytes 589832 | tf_op jit(solution)/shard_map/ppermute | solution.py:532
  109.8 6.1 %collective-permute-start.25 = (f32[3,2,2,32,128]{4,3,2,1,0:T(8,128)S(1)}, f32[3,2,2,32,128]{4,3,2,1,0:T(8,128)S(1)}, u32[]{:S(2)}, u32[]{:S(2)}) collective-permute-start(f32[3,2,2,32,128]{4,3,2,1,0:T(8,128)S(1)} %get-tuple-element.91), channel_id=1, source_target_pairs={{0,6},{2,0},{4,2},{6,4},{1,7},{3,1},{5,3},{7,5},{8,14},{10,8},{12,... | collective-permute-start | bytes 589832 | tf_op jit(solution)/shard_map/ppermute | solution.py:532
  117.2 5.8 %collective-permute-start.26 = (f32[3,2,2,32,128]{4,3,2,1,0:T(8,128)S(1)}, f32[3,2,2,32,128]{4,3,2,1,0:T(8,128)S(1)}, u32[]{:S(2)}, u32[]{:S(2)}) collective-permute-start(f32[3,2,2,32,128]{4,3,2,1,0:T(8,128)S(1)} %get-tuple-element.93), channel_id=1, source_target_pairs={{0,2},{2,4},{4,6},{6,0},{1,3},{3,5},{5,7},{7,1},{8,10},{10,12},{12... | collective-permute-start | bytes 589832 | tf_op jit(solution)/shard_map/ppermute | solution.py:532
  118.2 5.3 %collective-permute-start.27 = (f32[3,2,2,32,128]{4,3,2,1,0:T(8,128)S(1)}, f32[3,2,2,32,128]{4,3,2,1,0:T(8,128)S(1)}, u32[]{:S(2)}, u32[]{:S(2)}) collective-permute-start(f32[3,2,2,32,128]{4,3,2,1,0:T(8,128)S(1)} %get-tuple-element.94), channel_id=1, source_target_pairs={{0,6},{2,0},{4,2},{6,4},{1,7},{3,1},{5,3},{7,5},{8,14},{10,8},{12,... | collective-permute-start | bytes 589832 | tf_op jit(solution)/shard_map/ppermute | solution.py:532
  125.1 3.7 %collective-permute-start.29 = (f32[8,128]{1,0:T(8,128)S(1)}, f32[8,128]{1,0:T(8,128)S(1)}, u32[]{:S(2)}, u32[]{:S(2)}) collective-permute-start(f32[8,128]{1,0:T(8,128)S(1)} %shard_map.60), channel_id=1, source_target_pairs={{0,1},{1,0},{2,3},{3,2},{4,5},{5,4},{6,7},{7,6},{8,9},{9,8},{10,11... | collective-permute-start | bytes 12296 | tf_op jit(solution)/shard_map/ppermute | solution.py:546
  128.8 3.6 %collective-permute-start.30 = (f32[8,128]{1,0:T(8,128)S(1)}, f32[8,128]{1,0:T(8,128)S(1)}, u32[]{:S(2)}, u32[]{:S(2)}) collective-permute-start(f32[8,128]{1,0:T(8,128)S(1)} %add.18), channel_id=1, source_target_pairs={{0,8},{8,0},{16,24},{24,16},{1,9},{9,1},{17,25},{25,17},{2,10},{10... | collective-permute-start | bytes 12296 | tf_op jit(solution)/shard_map/ppermute | solution.py:546
  132.4 4.5 %collective-permute-start.31 = (f32[8,128]{1,0:T(8,128)S(1)}, f32[8,128]{1,0:T(8,128)S(1)}, u32[]{:S(2)}, u32[]{:S(2)}) collective-permute-start(f32[8,128]{1,0:T(8,128)S(1)} %add.19), channel_id=1, source_target_pairs={{0,16},{8,24},{16,0},{24,8},{1,17},{9,25},{17,1},{25,9},{2,18},{10... | collective-permute-start | bytes 12296 | tf_op jit(solution)/shard_map/ppermute | solution.py:546
  136.9 1.9 %collective-permute-start.32 = (f32[8,128]{1,0:T(8,128)S(1)}, f32[8,128]{1,0:T(8,128)S(1)}, u32[]{:S(2)}, u32[]{:S(2)}) collective-permute-start(f32[8,128]{1,0:T(8,128)S(1)} %add.20), channel_id=1, source_target_pairs={{0,2},{2,0},{4,6},{6,4},{1,3},{3,1},{5,7},{7,5},{8,10},{10,8},{12,... | collective-permute-start | bytes 12296 | tf_op jit(solution)/shard_map/ppermute | solution.py:546
  136.9 3.6 %collective-permute-start.33 = (f32[8,128]{1,0:T(8,128)S(1)}, f32[8,128]{1,0:T(8,128)S(1)}, u32[]{:S(2)}, u32[]{:S(2)}) collective-permute-start(f32[8,128]{1,0:T(8,128)S(1)} %add.20), channel_id=1, source_target_pairs={{0,4},{2,6},{4,0},{6,2},{1,5},{3,7},{5,1},{7,3},{8,12},{10,14},{12... | collective-permute-start | bytes 12296 | tf_op jit(solution)/shard_map/ppermute | solution.py:546
  138.3 3.0 %collective-permute-start.34 = (f32[8,128]{1,0:T(8,128)S(1)}, f32[8,128]{1,0:T(8,128)S(1)}, u32[]{:S(2)}, u32[]{:S(2)}) collective-permute-start(f32[8,128]{1,0:T(8,128)S(1)} %add.20), channel_id=1, source_target_pairs={{0,6},{2,4},{4,2},{6,0},{1,7},{3,5},{5,3},{7,1},{8,14},{10,12},{12... | collective-permute-start | bytes 12296 | tf_op jit(solution)/shard_map/ppermute | solution.py:546
